TPU v7x, 32 devices: a whole 2x2x4 slice. The times are simulated.
32 devices in a mesh: dp: 4 (over x, core), fsdp: 8 (over z, y).
Axes of the slice: x: 2, y: 2, z: 4, core: 2. Of those that a mesh axis runs over, the one named last changes fastest.
Arguments:
- tokens: bfloat16 [224, 128, 768], P(('dp', 'fsdp')), may hold values from -6 to 6
- lengths: int32 [224], P(('dp', 'fsdp')), may hold values from 5 to 128, as said below
- pooled_grad: float32 [224, 768], P(('dp', 'fsdp')), may hold values from -5 to 5
- w_qkv: bfloat16 [768, 2304], P('fsdp'), may hold values from -0.21875 to 0.21875
- bias_query: bfloat16 [768], P('fsdp'), may hold values from -3 to 3
- bias_value: bfloat16 [768], P('fsdp'), may hold values from -3 to 3
- w_out: bfloat16 [768, 768], P('fsdp'), may hold values from -0.875 to 0.875
- bias_out: bfloat16 [768], P('fsdp'), may hold values from -3 to 3
- gain_attn: bfloat16 [768], P('fsdp'), may hold values from 0.099609375 to 1.8984375
- shift_attn: bfloat16 [768], P('fsdp'), may hold values from -3 to 3
- w_in: bfloat16 [768, 3072], P('fsdp'), may hold values from -0.21875 to 0.21875
- bias_in: bfloat16 [3072], P('fsdp'), may hold values from -3 to 3
- w_down: bfloat16 [3072, 768], P('fsdp'), may hold values from -0.109375 to 0.109375
- bias_down: bfloat16 [768], P('fsdp'), may hold values from -2 to 2
- gain_ffn: bfloat16 [768], P('fsdp'), may hold values from 0.099609375 to 1.8984375
- shift_ffn: bfloat16 [768], P('fsdp'), may hold values from -3 to 3
Outputs:
- pooled: float32 [224, 768], P(('dp', 'fsdp'))
- grad_tokens: float32 [224, 128, 768], P(('dp', 'fsdp'))
- grad_w_qkv: float32 [768, 2304], P('fsdp')
- grad_bias_query: float32 [768], P('fsdp')
- grad_bias_value: float32 [768], P('fsdp')
- grad_w_out: float32 [768, 768], P('fsdp')
- grad_bias_out: float32 [768], P('fsdp')
- grad_gain_attn: float32 [768], P('fsdp')
- grad_shift_attn: float32 [768], P('fsdp')
- grad_w_in: float32 [768, 3072], P('fsdp')
- grad_bias_in: float32 [3072], P('fsdp')
- grad_w_down: float32 [3072, 768], P('fsdp')
- grad_bias_down: float32 [768], P('fsdp')
- grad_gain_ffn: float32 [768], P('fsdp')
- grad_shift_ffn: float32 [768], P('fsdp')
Inputs may be any that keep to these rules, and one draw needn't show every extreme that they name: `lengths`: some sentence has 128 real tokens and some has 5.
All inputs are finite; a program needn't handle non-finite values.
Results may differ from a plain program's by a relative error of at most 0.019.
Values may be sent and summed in bfloat16 or wider, within the bound.
No kernel may reach another device: no remote copies, remote signals or barrier semaphores. Data moves between devices by JAX's collectives and lax.ppermute only.
A program may use at most 192 MiB of HBM per device.

v0:
```python
from functools import partial

import jax
import jax.numpy as jnp
from jax import lax
from jax.sharding import PartitionSpec as P

HEAD = 64


norm_eps = 1e-06


def norm_parts(token_rows, gain_vec, shift_vec):
    row_mean = jnp.mean(token_rows, -1, keepdims=True)
    centred = token_rows - row_mean
    inverse = lax.rsqrt(jnp.mean(centred * centred, -1, keepdims=True) + norm_eps)
    normed = centred * inverse
    return (normed * gain_vec + shift_vec, normed, inverse)


def norm_back(grad_out, normed, inverse, gain_vec):
    grad_gain = jnp.sum(grad_out * normed, 0)
    grad_shift = jnp.sum(grad_out, 0)
    scaled = grad_out * gain_vec
    grad_in = inverse * (
        scaled
        - jnp.mean(scaled, -1, keepdims=True)
        - normed * jnp.mean(scaled * normed, -1, keepdims=True)
    )
    return (grad_in, grad_gain, grad_shift)


def attention_scores(query_rows, key_rows, key_valid):
    scores = jnp.einsum(
        "sqhd,skhd->shqk", query_rows, key_rows, preferred_element_type=jnp.float32
    ) * HEAD ** (-0.5)
    return jnp.where(key_valid[:, None, None, :], scores, -1000000000.0)


def forward(tokens, lengths, weights):
    (
        w_qkv,
        bias_query,
        bias_value,
        w_out,
        bias_out,
        gain_attn,
        shift_attn,
        w_in,
        bias_in,
        w_down,
        bias_down,
        gain_ffn,
        shift_ffn,
    ) = weights
    sentences, length, model_width = tokens.shape
    head_count = model_width // HEAD
    token_rows = tokens.reshape(sentences * length, model_width)
    bias_qkv = jnp.concatenate([bias_query, jnp.zeros_like(bias_query), bias_value]).astype(
        jnp.float32
    )
    packed = (jnp.dot(token_rows, w_qkv, preferred_element_type=jnp.float32) + bias_qkv).astype(
        jnp.bfloat16
    )
    packed = packed.reshape(sentences, length, 3, head_count, HEAD)
    query_rows = packed[:, :, 0]
    key_rows = packed[:, :, 1]
    value_rows = packed[:, :, 2]
    key_valid = jnp.arange(length)[None, :] < lengths[:, None]
    scores = attention_scores(query_rows, key_rows, key_valid)
    row_max = jnp.max(scores, -1, keepdims=True)
    log_total = row_max + jnp.log(jnp.sum(jnp.exp(scores - row_max), -1, keepdims=True))
    attn_probs = jnp.exp(scores - log_total)
    context = jnp.einsum(
        "shqk,skhd->sqhd",
        attn_probs.astype(jnp.bfloat16),
        value_rows,
        preferred_element_type=jnp.float32,
    )
    context = context.reshape(sentences * length, model_width).astype(jnp.bfloat16)
    attn_out = jnp.dot(context, w_out, preferred_element_type=jnp.float32) + bias_out.astype(
        jnp.float32
    )
    hidden, normed_attn, inverse_attn = norm_parts(
        token_rows.astype(jnp.float32) + attn_out,
        gain_attn.astype(jnp.float32),
        shift_attn.astype(jnp.float32),
    )
    hidden_low = hidden.astype(jnp.bfloat16)
    up_rows = jnp.dot(hidden_low, w_in, preferred_element_type=jnp.float32) + bias_in.astype(
        jnp.float32
    )
    active = jax.nn.gelu(up_rows, approximate=False).astype(jnp.bfloat16)
    ffn_out = jnp.dot(active, w_down, preferred_element_type=jnp.float32) + bias_down.astype(
        jnp.float32
    )
    output, normed_ffn, inverse_ffn = norm_parts(
        hidden + ffn_out, gain_ffn.astype(jnp.float32), shift_ffn.astype(jnp.float32)
    )
    valid_mask = key_valid.astype(jnp.float32)
    pooled = jnp.sum(
        output.reshape(sentences, length, model_width) * valid_mask[:, :, None], 1
    ) / lengths[:, None].astype(jnp.float32)
    kept = (
        key_valid,
        query_rows,
        key_rows,
        value_rows,
        log_total,
        context,
        normed_attn,
        inverse_attn,
        hidden_low,
        up_rows,
        active,
        normed_ffn,
        inverse_ffn,
    )
    return (pooled, kept)


def backward(tokens, lengths, pooled_grad, weights, kept):
    (
        w_qkv,
        bias_query,
        bias_value,
        w_out,
        bias_out,
        gain_attn,
        shift_attn,
        w_in,
        bias_in,
        w_down,
        bias_down,
        gain_ffn,
        shift_ffn,
    ) = weights
    (
        key_valid,
        query_rows,
        key_rows,
        value_rows,
        log_total,
        context,
        normed_attn,
        inverse_attn,
        hidden_low,
        up_rows,
        active,
        normed_ffn,
        inverse_ffn,
    ) = kept
    sentences, length, model_width = tokens.shape
    head_count = model_width // HEAD
    token_rows = tokens.reshape(sentences * length, model_width)
    valid_mask = key_valid.astype(jnp.float32)
    per_sentence = pooled_grad / lengths[:, None].astype(jnp.float32)
    grad_output = (valid_mask[:, :, None] * per_sentence[:, None, :]).reshape(
        sentences * length, model_width
    )
    grad_res_ffn, grad_gain_ffn, grad_shift_ffn = norm_back(
        grad_output, normed_ffn, inverse_ffn, gain_ffn.astype(jnp.float32)
    )
    grad_ffn_low = grad_res_ffn.astype(jnp.bfloat16)
    grad_bias_down = jnp.sum(grad_ffn_low.astype(jnp.float32), 0)
    grad_w_down = jnp.einsum("tf,td->fd", active, grad_ffn_low, preferred_element_type=jnp.float32)
    grad_active = jnp.einsum("td,fd->tf", grad_ffn_low, w_down, preferred_element_type=jnp.float32)
    gelu_value, gelu_pull = jax.vjp(partial(jax.nn.gelu, approximate=False), up_rows)
    grad_up = gelu_pull(grad_active)[0].astype(jnp.bfloat16)
    grad_bias_in = jnp.sum(grad_up.astype(jnp.float32), 0)
    grad_w_in = jnp.einsum("td,tf->df", hidden_low, grad_up, preferred_element_type=jnp.float32)
    grad_hidden = (
        jnp.einsum("tf,df->td", grad_up, w_in, preferred_element_type=jnp.float32) + grad_res_ffn
    )
    grad_res_attn, grad_gain_attn, grad_shift_attn = norm_back(
        grad_hidden, normed_attn, inverse_attn, gain_attn.astype(jnp.float32)
    )
    grad_attn_low = grad_res_attn.astype(jnp.bfloat16)
    grad_bias_out = jnp.sum(grad_attn_low.astype(jnp.float32), 0)
    grad_w_out = jnp.einsum("tc,td->cd", context, grad_attn_low, preferred_element_type=jnp.float32)
    grad_context = jnp.einsum("td,cd->tc", grad_attn_low, w_out, preferred_element_type=jnp.float32)
    grad_context = grad_context.astype(jnp.bfloat16).reshape(sentences, length, head_count, HEAD)
    scores = attention_scores(query_rows, key_rows, key_valid)
    attn_probs = jnp.exp(scores - log_total)
    grad_probs = jnp.einsum(
        "sqhd,skhd->shqk", grad_context, value_rows, preferred_element_type=jnp.float32
    )
    grad_values = jnp.einsum(
        "shqk,sqhd->skhd",
        attn_probs.astype(jnp.bfloat16),
        grad_context,
        preferred_element_type=jnp.float32,
    )
    grad_scores = (
        attn_probs * (grad_probs - jnp.sum(grad_probs * attn_probs, -1, keepdims=True))
    ).astype(jnp.bfloat16)
    grad_queries = jnp.einsum(
        "shqk,skhd->sqhd", grad_scores, key_rows, preferred_element_type=jnp.float32
    ) * HEAD ** (-0.5)
    grad_keys = jnp.einsum(
        "shqk,sqhd->skhd", grad_scores, query_rows, preferred_element_type=jnp.float32
    ) * HEAD ** (-0.5)
    grad_qkv = jnp.stack([grad_queries, grad_keys, grad_values], 2)
    grad_qkv = grad_qkv.reshape(sentences * length, 3 * model_width).astype(jnp.bfloat16)
    qkv_sums = jnp.sum(grad_qkv.astype(jnp.float32), 0)
    grad_bias_query = qkv_sums[:model_width]
    grad_bias_value = qkv_sums[2 * model_width :]
    grad_w_qkv = jnp.einsum("td,tc->dc", token_rows, grad_qkv, preferred_element_type=jnp.float32)
    grad_tokens = (
        jnp.einsum("tc,dc->td", grad_qkv, w_qkv, preferred_element_type=jnp.float32) + grad_res_attn
    )
    grad_tokens = grad_tokens.reshape(sentences, length, model_width)
    grad_terms = (
        grad_w_qkv,
        grad_bias_query,
        grad_bias_value,
        grad_w_out,
        grad_bias_out,
        grad_gain_attn,
        grad_shift_attn,
        grad_w_in,
        grad_bias_in,
        grad_w_down,
        grad_bias_down,
        grad_gain_ffn,
        grad_shift_ffn,
    )
    return (grad_terms, grad_tokens)


def on_device(
    tokens,
    lengths,
    pooled_grad,
    w_qkv,
    bias_query,
    bias_value,
    w_out,
    bias_out,
    gain_attn,
    shift_attn,
    w_in,
    bias_in,
    w_down,
    bias_down,
    gain_ffn,
    shift_ffn,
):
    weights = (
        lax.all_gather(w_qkv, "fsdp", axis=0, tiled=True),
        lax.all_gather(bias_query, "fsdp", axis=0, tiled=True),
        lax.all_gather(bias_value, "fsdp", axis=0, tiled=True),
        lax.all_gather(w_out, "fsdp", axis=0, tiled=True),
        lax.all_gather(bias_out, "fsdp", axis=0, tiled=True),
        lax.all_gather(gain_attn, "fsdp", axis=0, tiled=True),
        lax.all_gather(shift_attn, "fsdp", axis=0, tiled=True),
        lax.all_gather(w_in, "fsdp", axis=0, tiled=True),
        lax.all_gather(bias_in, "fsdp", axis=0, tiled=True),
        lax.all_gather(w_down, "fsdp", axis=0, tiled=True),
        lax.all_gather(bias_down, "fsdp", axis=0, tiled=True),
        lax.all_gather(gain_ffn, "fsdp", axis=0, tiled=True),
        lax.all_gather(shift_ffn, "fsdp", axis=0, tiled=True),
    )
    pooled, kept = forward(tokens, lengths, weights)
    weights = (
        lax.all_gather(w_qkv, "fsdp", axis=0, tiled=True),
        lax.all_gather(bias_query, "fsdp", axis=0, tiled=True),
        lax.all_gather(bias_value, "fsdp", axis=0, tiled=True),
        lax.all_gather(w_out, "fsdp", axis=0, tiled=True),
        lax.all_gather(bias_out, "fsdp", axis=0, tiled=True),
        lax.all_gather(gain_attn, "fsdp", axis=0, tiled=True),
        lax.all_gather(shift_attn, "fsdp", axis=0, tiled=True),
        lax.all_gather(w_in, "fsdp", axis=0, tiled=True),
        lax.all_gather(bias_in, "fsdp", axis=0, tiled=True),
        lax.all_gather(w_down, "fsdp", axis=0, tiled=True),
        lax.all_gather(bias_down, "fsdp", axis=0, tiled=True),
        lax.all_gather(gain_ffn, "fsdp", axis=0, tiled=True),
        lax.all_gather(shift_ffn, "fsdp", axis=0, tiled=True),
    )
    kept = forward(tokens, lengths, weights)[1]
    grad_terms, grad_tokens = backward(tokens, lengths, pooled_grad, weights, kept)
    (
        grad_w_qkv,
        grad_bias_query,
        grad_bias_value,
        grad_w_out,
        grad_bias_out,
        grad_gain_attn,
        grad_shift_attn,
        grad_w_in,
        grad_bias_in,
        grad_w_down,
        grad_bias_down,
        grad_gain_ffn,
        grad_shift_ffn,
    ) = grad_terms
    shares = (
        lax.psum_scatter(grad_w_qkv, "fsdp", scatter_dimension=0, tiled=True),
        lax.psum_scatter(grad_bias_query, "fsdp", scatter_dimension=0, tiled=True),
        lax.psum_scatter(grad_bias_value, "fsdp", scatter_dimension=0, tiled=True),
        lax.psum_scatter(grad_w_out, "fsdp", scatter_dimension=0, tiled=True),
        lax.psum_scatter(grad_bias_out, "fsdp", scatter_dimension=0, tiled=True),
        lax.psum_scatter(grad_gain_attn, "fsdp", scatter_dimension=0, tiled=True),
        lax.psum_scatter(grad_shift_attn, "fsdp", scatter_dimension=0, tiled=True),
        lax.psum_scatter(grad_w_in, "fsdp", scatter_dimension=0, tiled=True),
        lax.psum_scatter(grad_bias_in, "fsdp", scatter_dimension=0, tiled=True),
        lax.psum_scatter(grad_w_down, "fsdp", scatter_dimension=0, tiled=True),
        lax.psum_scatter(grad_bias_down, "fsdp", scatter_dimension=0, tiled=True),
        lax.psum_scatter(grad_gain_ffn, "fsdp", scatter_dimension=0, tiled=True),
        lax.psum_scatter(grad_shift_ffn, "fsdp", scatter_dimension=0, tiled=True),
    )
    (
        share_w_qkv,
        share_bias_query,
        share_bias_value,
        share_w_out,
        share_bias_out,
        share_gain_attn,
        share_shift_attn,
        share_w_in,
        share_bias_in,
        share_w_down,
        share_bias_down,
        share_gain_ffn,
        share_shift_ffn,
    ) = shares
    totals = (
        lax.psum(share_w_qkv.astype(jnp.bfloat16), "dp").astype(jnp.float32),
        lax.psum(share_bias_query.astype(jnp.bfloat16), "dp").astype(jnp.float32),
        lax.psum(share_bias_value.astype(jnp.bfloat16), "dp").astype(jnp.float32),
        lax.psum(share_w_out.astype(jnp.bfloat16), "dp").astype(jnp.float32),
        lax.psum(share_bias_out.astype(jnp.bfloat16), "dp").astype(jnp.float32),
        lax.psum(share_gain_attn.astype(jnp.bfloat16), "dp").astype(jnp.float32),
        lax.psum(share_shift_attn.astype(jnp.bfloat16), "dp").astype(jnp.float32),
        lax.psum(share_w_in.astype(jnp.bfloat16), "dp").astype(jnp.float32),
        lax.psum(share_bias_in.astype(jnp.bfloat16), "dp").astype(jnp.float32),
        lax.psum(share_w_down.astype(jnp.bfloat16), "dp").astype(jnp.float32),
        lax.psum(share_bias_down.astype(jnp.bfloat16), "dp").astype(jnp.float32),
        lax.psum(share_gain_ffn.astype(jnp.bfloat16), "dp").astype(jnp.float32),
        lax.psum(share_shift_ffn.astype(jnp.bfloat16), "dp").astype(jnp.float32),
    )
    return (
        pooled,
        grad_tokens,
        totals[0],
        totals[1],
        totals[2],
        totals[3],
        totals[4],
        totals[5],
        totals[6],
        totals[7],
        totals[8],
        totals[9],
        totals[10],
        totals[11],
        totals[12],
    )


def solution(mesh):
    placed = (
        P(("dp", "fsdp"), None, None),
        P(("dp", "fsdp")),
        P(("dp", "fsdp"), None),
        P("fsdp", None),
        P("fsdp"),
        P("fsdp"),
        P("fsdp", None),
        P("fsdp"),
        P("fsdp"),
        P("fsdp"),
        P("fsdp", None),
        P("fsdp"),
        P("fsdp", None),
        P("fsdp"),
        P("fsdp"),
        P("fsdp"),
    )
    return jax.shard_map(
        on_device,
        mesh=mesh,
        in_specs=placed,
        out_specs=(
            P(("dp", "fsdp"), None),
            P(("dp", "fsdp"), None, None),
            P("fsdp", None),
            P("fsdp"),
            P("fsdp"),
            P("fsdp", None),
            P("fsdp"),
            P("fsdp"),
            P("fsdp"),
            P("fsdp", None),
            P("fsdp"),
            P("fsdp", None),
            P("fsdp"),
            P("fsdp"),
            P("fsdp"),
        ),
        check_vma=False,
    )
```

profile of v0, /device:TPU:0, one launch (start us, length us, event | category | flops | bytes accessed | tf_op | source)
XLA Modules:
  0.0 920.5 jit_solution(971078755759636488)
XLA Ops:
  11.4 1.3 fusion.54
  13.4 0.8 dynamic-update-slice.2
  14.2 0.8 dynamic-update-slice.1
  15.1 0.8 dynamic-update-slice
  15.9 0.8 dynamic-update-slice.4
  16.7 0.8 dynamic-update-slice.3
  17.6 0.8 dynamic-update-slice.5
  18.4 0.8 dynamic-update-slice.6
  19.3 0.8 dynamic-update-slice.7
  20.1 40.4 %all-reduce.18 = (bf16[768]{0:T(1024)(128)(2,1)S(1)}, bf16[768]{0:T(1024)(128)(2,1)S(1)}, bf16[768]{0:T(1024)(128)(2,1)S(1)}, bf16[768]{0:T(1024)(128)(2,1)S(1)}...) all-reduce(bf16[768]{0:T(1024)(128)(2,1)S(1)} %dynamic-update-slice, ...), channel_id=1, replica_groups=mesh['dp'=4,'fsdp'=8] {'fsdp'}, use_global_device_ids=true, to_apply=%add.2 | all-reduce | flops 6144 | bytes 24576
  61.2 26.6 %all-gather = bf16[8,1,384]{2,1,0:T(2,128)(2,1)S(1)} all-gather(bf16[1,1,384]{2,1,0:T(2,128)(2,1)S(1)} %reshape.238), channel_id=1, replica_groups=mesh['dp'=4,'fsdp'=8] {'fsdp'}, dimensions={0}, use_global_device_ids=true | all-gather | bytes 6912 | tf_op jit(solution)/shard_map/all_gather | solution.py:259
  88.7 7.7 add_convert_fusion.1
  96.4 6.5 copy.55
  102.9 9.0 reshape.209
  111.9 2.9 fusion.52
  114.8 1.6 fusion.6
  116.5 1.5 exponential_reduce_fusion
  118.8 1.4 fusion.26
  120.2 2.2 copy.60
  122.5 3.6 fusion.55
  126.5 74.1 %all-gather.10.cloned.1.call-done = bf16[768,3072]{1,0:T(8,128)(2,1)} async-done(((bf16[96,3072]{1,0:T(8,128)(2,1)}), bf16[768,3072]{1,0:T(8,128)(2,1)}) %all-gather.10.cloned.1.call-update) | async-done | bytes 4718608 | tf_op jit(solution)/shard_map/all_gather | solution.py:258
  200.7 32.9 %multiply_convert_fusion = (bf16[896,3072]{1,0:T(8,128)(2,1)}, f32[896,3072]{1,0:T(8,128)}, f32[896,3072]{1,0:T(8,128)}) fusion(f32[3072]{0:T(1024)S(1)} %bitcast.117, bf16[768,3072]{1,0:T(8,128)(2,1)} %all-gather.10.cloned.1.call-done, f32[896,768]{1,0:T(8,128)S(1)} %get-tuple-element.124, f32[768]{0:T(1024)S(1)} %convert_element_type.215, ...), kind=kOutput, calls=%fused_computation.4 | convolution fusion | flops 4412964864 | bytes 35021824 | tf_op jit(solution)/shard_map/dot_general | solution.py:91
  233.6 46.9 %all-gather.12.cloned.1.call-done = bf16[3072,768]{1,0:T(8,128)(2,1)} async-done(((bf16[384,768]{1,0:T(8,128)(2,1)}), bf16[3072,768]{1,0:T(8,128)(2,1)}) %all-gather.12.cloned.1.call-update) | async-done | bytes 4718608 | tf_op jit(solution)/shard_map/all_gather | solution.py:260
  280.4 8.7 fusion.56
  289.6 1.3 fusion.21
  290.9 0.8 multiply_reduce_fusion.1
  291.7 2.5 convert_reduce_fusion.2
  294.3 13.9 %convert_reduce_fusion = (f32[3072]{0:T(1024)S(1)}, bf16[896,3072]{1,0:T(8,128)(2,1)S(1)}) fusion(f32[896,3072]{1,0:T(8,128)} %get-tuple-element.108, f32[896,3072]{1,0:T(8,128)} %get-tuple-element.125, f32[3072]{0:T(1024)S(1)} %bitcast.118, bf16[896,768]{1,0:T(8,128)(2,1)S(1)} %get-tuple-element.100, bf16[3072,768]{1,0:T(8,128)(2,1)} %all-gather.12.cloned.1.call-done), kind=kOutput, calls=%fused_computation.2 | convolution fusion | flops 4274648064 | bytes 33644544 | tf_op jit(solution)/shard_map/td,fd->tf/dot_general | solution.py:168
  308.2 10.2 %multiply_reduce_fusion.2 = (f32[768]{0:T(1024)S(1)}, f32[896]{0:T(1024)S(1)}, f32[896]{0:T(1024)S(1)}, f32[768]{0:T(1024)S(1)}, f32[896,768]{1,0:T(8,128)S(1)}) fusion(f32[896,768]{1,0:T(8,128)S(1)} %get-tuple-element.124, f32[896]{0:T(1024)S(1)} %add_rsqrt_fusion.1, f32[896]{0:T(1024)S(1)} %broadcast_multiply_fusion.4, ...), kind=kOutput, calls=%fused_computation.47 | convolution fusion | flops 4234736384 | bytes 18504704 | tf_op jit(solution)/shard_map/tf,df->td/dot_general | solution.py:174
  318.5 1.0 convert_reduce_fusion.3
  319.5 1.5 copy-done.12
  321.1 2.8 fusion.28
  323.9 4.2 convolution_convert_fusion
  328.1 2.8 copy.61
  330.9 4.1 reshape.211
  335.1 5.7 multiply_reduce_fusion
  340.7 2.2 multiply_convert_fusion.1
  343.0 2.0 multiply_bitcast_fusion
  345.0 0.9 multiply_bitcast_fusion.1
  346.4 2.1 convolution_bitcast_fusion.1
  348.5 1.6 convert_reduce_fusion.1
  350.1 8.1 copy.67
  358.2 2.1 copy-done.11
  360.3 5.9 convolution_bitcast_fusion
  366.2 8.0 copy.73
  374.3 1.7 copy-done.2
  376.0 10.7 %fusion.46 = f32[768,3072]{1,0:T(8,128)} fusion(bf16[896,3072]{1,0:T(8,128)(2,1)} %copy-done.3, f32[896,768]{1,0:T(8,128)S(1)} %copy-done.2, f32[768]{0:T(1024)S(1)} %convert_element_type.215, f32[768]{0:T(1024)S(1)} %convert_element_type.214, f32[896]{0:T(1024)S(1)} %add_rsqrt_fusion.1, f32[896]{0:T(1024)S(1)} %broadcast_multiply_fusion.4), kind=kOutput, calls=%fused_computation.113 | convolution fusion | flops 4231299072 | bytes 17708032 | tf_op jit(solution)/shard_map/td,tf->df/dot_general | solution.py:172
  386.8 1.3 copy-done.16
  388.0 9.9 %fusion.57 = f32[3072,768]{1,0:T(8,128)} fusion(bf16[896,3072]{1,0:T(8,128)(2,1)} %get-tuple-element.107, bf16[896,768]{1,0:T(8,128)(2,1)S(1)} %copy-done.16), kind=kOutput, calls=%fused_computation.120 | convolution fusion | flops 4227858432 | bytes 16318464 | tf_op jit(solution)/shard_map/tf,td->fd/dot_general | solution.py:167
  399.4 37.9 %all-reduce.17 = (bf16[768]{0:T(1024)(128)(2,1)S(1)}, bf16[768]{0:T(1024)(128)(2,1)S(1)}, bf16[768]{0:T(1024)(128)(2,1)S(1)}, bf16[768]{0:T(1024)(128)(2,1)S(1)}...) all-reduce(f32[768]{0:T(1024)S(1)} %slice.28, ...), channel_id=3, replica_groups=mesh['dp'=4,'fsdp'=8] {'fsdp'}, use_global_device_ids=true, to_apply=%region_15.16.clone | all-reduce | flops 9216 | bytes 55296
  438.0 6.1 all-reduce.19
  449.5 1.6 convert_element_type.240
  451.2 73.8 %reduce-scatter.13.cloned.1.call-done = f32[96,2304]{1,0:T(8,128)} async-done(((f32[768,2304]{1,0:T(8,128)}), f32[96,2304]{1,0:T(8,128)}) %reduce-scatter.13.cloned.1.call-update) | async-done | bytes 884752
  525.0 2.2 copy.74
  527.2 162.7 %reduce-scatter.9.cloned.1.call-done = f32[96,3072]{1,0:T(8,128)} async-done(((f32[768,3072]{1,0:T(8,128)}), f32[96,3072]{1,0:T(8,128)}) %reduce-scatter.9.cloned.1.call-update) | async-done | bytes 1179664 | tf_op jit(solution)/shard_map/reduce_scatter | solution.py:306
  689.9 2.2 convert_element_type.249
  692.0 162.7 %reduce-scatter.11.cloned.1.call-done = f32[384,768]{1,0:T(8,128)} async-done(((f32[3072,768]{1,0:T(8,128)}), f32[384,768]{1,0:T(8,128)}) %reduce-scatter.11.cloned.1.call-update) | async-done | bytes 1179664 | tf_op jit(solution)/shard_map/reduce_scatter | solution.py:308
  854.7 2.1 convert_element_type.254
  856.9 8.4 fusion.23
  865.3 41.0 %all-reduce.23.cloned.1.call-done = (bf16[96,2304]{0,1:T(8,128)(2,1)}, bf16[96,768]{1,0:T(8,128)(2,1)}, bf16[96,3072]{1,0:T(8,128)(2,1)}, bf16[384,768]{1,0:T(8,128)(2,1)}) async-done(((bf16[96,2304]{0,1:T(8,128)(2,1)}, bf16[96,768]{1,0:T(8,128)(2,1)}, bf16[96,3072]{1,0:T(8,128)(2,1)}, bf16[384,768]{1,0:T(8,128)(2,1)}), (bf16[96,2304]{0,1:T(8,128)(2,1)}, bf16[96,768]{1,0:T(8,128)(2,1)}, ...) | async-done | bytes 1769488 | tf_op jit(solution)/shard_map/psum | solution.py:329
  906.3 2.3 copy.68
  908.6 1.6 convert_element_type.241
  910.2 2.2 convert_element_type.250
  912.4 1.1 convert_element_type.255
  (119 shorter events, 14.6 us)
Async XLA Ops:
  7.2 81.5 %all-gather.6.cloned.1.call-start = ((), (), s32[]{:S(2)}) async-start(), calls=%async_computation.4 | async-start | bytes 3981312 | tf_op jit(solution)/shard_map/all_gather | solution.py:251
  7.9 114.5 %all-gather.8.cloned.1.call-start = ((), (), s32[]{:S(2)}) async-start(), calls=%async_computation.5 | async-start | bytes 1327104 | tf_op jit(solution)/shard_map/all_gather | solution.py:254
  8.7 192.0 %all-gather.10.cloned.1.call-start = ((), (), s32[]{:S(2)}) async-start(), calls=%async_computation.6 | async-start | bytes 5308416 | tf_op jit(solution)/shard_map/all_gather | solution.py:258
  9.4 271.0 %all-gather.12.cloned.1.call-start = ((), (), s32[]{:S(2)}) async-start(), calls=%async_computation.7 | async-start | bytes 5308416 | tf_op jit(solution)/shard_map/all_gather | solution.py:260
  10.0 439.5 %reduce-scatter.7.cloned.1.call-start = ((), (), s32[]{:S(2)}) async-start(), calls=%async_computation.8 | async-start | bytes 2654208 | tf_op jit(solution)/shard_map/reduce_scatter | solution.py:302
  10.7 78.0 %copy-start.18 = (f32[7]{0:T(128)}, f32[7]{0:T(128)S(1)}, u32[]{:S(2)}) copy-start(f32[7]{0:T(128)S(1)} %convert_element_type.223) | copy-start | bytes 88
  114.8 1.7 copy-start.4
  114.8 1.7 copy-start.6
  114.8 3.2 copy-start.8
  116.4 2.4 copy-start
  126.1 192.4 %copy-start.1 = (f32[896,768]{1,0:T(8,128)}, f32[896,768]{1,0:T(8,128)S(1)}, u32[]{:S(2)}) copy-start(f32[896,768]{1,0:T(8,128)S(1)} %get-tuple-element.124) | copy-start | bytes 8257540
  294.3 13.9 %copy-start.15 = (bf16[896,768]{1,0:T(8,128)(2,1)}, bf16[896,768]{1,0:T(8,128)(2,1)S(1)}, u32[]{:S(2)}) copy-start(bf16[896,768]{1,0:T(8,128)(2,1)S(1)} %get-tuple-element.100) | copy-start | bytes 4128772
  308.2 10.3 %copy-start.3 = (bf16[896,3072]{1,0:T(8,128)(2,1)}, bf16[896,3072]{1,0:T(8,128)(2,1)S(1)}, u32[]{:S(2)}) copy-start(bf16[896,3072]{1,0:T(8,128)(2,1)S(1)} %get-tuple-element.102) | copy-start | bytes 16515076
  318.5 2.5 copy-start.14
  319.5 1.5 copy-start.12
  321.0 2.9 copy-start.21
  323.9 201.1 %reduce-scatter.13.cloned.1.call-start = ((), (), s32[]{:S(2)}) async-start(), calls=%async_computation.11 | async-start | bytes 7962624
  328.1 7.0 copy-start.9
  330.9 9.8 %slice-start = ((s8[5505024]{0:T(1024)(128)(4,1)}), s8[1310720]{0:T(1024)(128)(4,1)S(1)}, s32[]{:S(2)}) async-start(s8[5505024]{0:T(1024)(128)(4,1)} %bitcast.110), calls=%async_computation.13 | async-start | bytes 2621440
  335.0 5.7 slice-start.1
  340.7 2.2 copy-start.7
  343.0 2.0 copy-start.5
  345.0 1.4 copy-start.10
  350.1 10.2 %copy-start.20 = (bf16[7,128,768]{2,1,0:T(8,128)(2,1)S(1)}, bf16[7,128,768]{2,1,0:T(8,128)(2,1)}, u32[]{:S(2)}) copy-start(bf16[7,128,768]{2,1,0:T(8,128)(2,1)} %param.16) | copy-start | bytes 4128772
  358.2 2.1 copy-start.11
  374.2 1.8 copy-start.2
  374.2 315.7 %reduce-scatter.9.cloned.1.call-start = ((), (), s32[]{:S(2)}) async-start(), calls=%async_computation.9 | async-start | bytes 10616832 | tf_op jit(solution)/shard_map/reduce_scatter | solution.py:306
  386.7 1.4 copy-start.16
  386.7 468.0 %reduce-scatter.11.cloned.1.call-start = ((), (), s32[]{:S(2)}) async-start(), calls=%async_computation.10 | async-start | bytes 10616832 | tf_op jit(solution)/shard_map/reduce_scatter | solution.py:308
  397.9 50.9 %copy-start.19 = (f32[7]{0:T(128)S(1)}, f32[7]{0:T(128)}, u32[]{:S(2)}) copy-start(f32[7]{0:T(128)} %copy-done.18) | copy-start | bytes 88
  397.9 508.3 %all-reduce.23.cloned.1.call-start = ((), (), s32[]{:S(2)}) async-start(), calls=%async_computation.12 | async-start | bytes 3833856 | tf_op jit(solution)/shard_map/psum | solution.py:329
  527.2 329.7 %copy-start.13 = (f32[896,768]{1,0:T(8,128)S(1)}, f32[896,768]{1,0:T(8,128)}, u32[]{:S(2)}) copy-start(f32[896,768]{1,0:T(8,128)} %copy-done.12) | copy-start | bytes 8257540
  906.3 6.1 copy-start.17
Sparse Core Ops, SparseCore 0:
  10.2 67.9 all-gather.5
  80.3 40.0 all-gather.7
  122.6 78.0 all-gather.9
  202.7 77.6 all-gather.11
  324.0 67.8 reduce-scatter.6
  395.4 129.4 reduce-scatter.12
  528.6 161.2 reduce-scatter.8
  693.5 161.1 reduce-scatter.10
  858.5 47.7 all-reduce.22
where the time goes:
time: 924 us; the launch traced here: 921 us
  waiting for transfers between devices  564 us (61%)
  matrix products  132 us (14%)
  blocking collectives  111 us (12%)
  local copies, waits for them, and re-layouts  65.7 us (7%)
  other arithmetic  30.4 us (3%)
  between operations  16.8 us (2%)
    reduce_scatter x1, waiting for transfers between devices, on_device(): lax.psum_scatter(grad_w_in, 'fsdp', scatter_dimension=0, tiled=True)  163 us
    reduce_scatter x1, waiting for transfers between devices, on_device(): lax.psum_scatter(grad_w_down, 'fsdp', scatter_dimension=0, tiled=True)  163 us
    unnamed x2, blocking collectives  78.3 us
    unnamed x10, waiting for transfers between devices  76.5 us
    all_gather x1, waiting for transfers between devices, on_device(): lax.all_gather(w_in, 'fsdp', axis=0, tiled=True)  74.1 us
    all_gather x1, waiting for transfers between devices, on_device(): lax.all_gather(w_down, 'fsdp', axis=0, tiled=True)  46.9 us
    psum x1, waiting for transfers between devices, on_device(): lax.psum(share_w_qkv.astype(jnp.bfloat16), 'dp').astype(jnp.float32)  41 us
    dot_general x1, matrix products, forward(): jnp.dot(hidden_low, w_in, preferred_element_type=jnp.float32)  32.9 us
  transfers between devices with their start and end apart: 9, of which 6 were waited for; matrix products, arithmetic and copies ran while one was open for 18% of the time, Pallas kernels for 0%

commit v1 on v0

--- a/solution.py
+++ b/solution.py
@@ -3,12 +3,551 @@
 import jax
 import jax.numpy as jnp
 from jax import lax
+from jax.experimental import pallas as pl
+from jax.experimental.pallas import tpu as pltpu
 from jax.sharding import PartitionSpec as P
 
+norm_eps = 1e-06
+
 HEAD = 64
-
-
-norm_eps = 1e-06
+NORM_EPS = 1e-06
+BF = jnp.bfloat16
+F32 = jnp.float32
+VMEM_LIMIT = 60 * 1024 * 1024
+
+
+def dot(a, b):
+    return lax.dot_general(a, b, (((1,), (0,)), ((), ())), preferred_element_type=F32)
+
+
+def dot_nt(a, b):
+    return lax.dot_general(a, b, (((1,), (1,)), ((), ())), preferred_element_type=F32)
+
+
+def dot_tn(a, b):
+    return lax.dot_general(a, b, (((0,), (0,)), ((), ())), preferred_element_type=F32)
+
+
+def aligned(value, step):
+    return pl.multiple_of(value, step)
+
+
+class Place:
+    def __init__(self, ids_ref):
+        self.z, self.y, self.x, self.c = ids_ref[0], ids_ref[1], ids_ref[2], ids_ref[3]
+
+    def shard(self, k, yy):
+        return lax.bitwise_xor(self.z, k) * 2 + lax.bitwise_xor(self.y, yy)
+
+
+def piece_copies(place, bufs, dst, sems, shard_rows, split_x):
+    half = shard_rows // 2
+    copies = []
+    at = 0
+    for cc in range(2):
+        core = lax.bitwise_xor(place.c, cc)
+        for xx in range(2 if split_x else 1):
+            for yy in range(2):
+                buf = bufs[at]
+                at += 1
+                width = buf.shape[-1]
+                for k in range(4):
+                    row = aligned(place.shard(k, yy) * shard_rows + core * half, 16)
+                    if split_x:
+                        col = aligned(lax.bitwise_xor(place.x, xx) * width, 128)
+                        target = dst.at[pl.ds(row, half), pl.ds(col, width)]
+                    else:
+                        target = dst.at[pl.ds(row, half), :]
+                    copies.append(
+                        pltpu.make_async_copy(buf.at[k], target, sems.at[len(copies)])
+                    )
+    return copies
+
+
+def emit_blocks(place, acc, send, keep, shard_rows, split_x):
+    half = shard_rows // 2
+    nx = 2 if split_x else 1
+    width = acc.shape[1] // nx
+    for cc, out in ((0, keep), (1, send)):
+        core = lax.bitwise_xor(place.c, cc)
+        for xx in range(nx):
+            for yy in range(2):
+
+                def step(k, carry, cc=cc, xx=xx, yy=yy, out=out, core=core):
+                    row = aligned(place.shard(k, yy) * shard_rows + core * half, 16)
+                    if split_x:
+                        col = aligned(lax.bitwise_xor(place.x, xx) * width, 128)
+                        block = acc[pl.ds(row, half), pl.ds(col, width)]
+                    else:
+                        block = acc[pl.ds(row, half), :]
+                    out[xx, yy, k] = block.astype(BF)
+                    return carry
+
+                lax.fori_loop(0, 4, step, 0)
+
+
+def call(body, name, ins, outs, scratch, flops, transcendentals=0):
+    spaces = {
+        "s": pl.BlockSpec(memory_space=pltpu.SMEM),
+        "v": pl.BlockSpec(memory_space=pltpu.VMEM),
+        "a": pl.BlockSpec(memory_space=pl.ANY),
+    }
+    moved = sum(a.size * a.dtype.itemsize for a, _ in ins) + sum(
+        o.size * o.dtype.itemsize for o in outs
+    )
+    return pl.pallas_call(
+        body,
+        name=name,
+        out_shape=tuple(outs),
+        in_specs=[spaces[s] for _, s in ins],
+        out_specs=tuple(spaces["v"] for _ in outs),
+        scratch_shapes=scratch,
+        compiler_params=pltpu.CompilerParams(vmem_limit_bytes=VMEM_LIMIT),
+        cost_estimate=pl.CostEstimate(
+            flops=flops, transcendentals=transcendentals, bytes_accessed=moved
+        ),
+    )(*[a for a, _ in ins])
+
+
+def struct(shape, dtype):
+    return jax.ShapeDtypeStruct(shape, dtype)
+
+
+def two_heads(block):
+    low = lax.broadcasted_iota(jnp.int32, block.shape, 1) < HEAD
+    zero = jnp.zeros_like(block)
+    return jnp.concatenate([jnp.where(low, block, zero), jnp.where(low, zero, block)], axis=0)
+
+
+def one_of_two(stacked):
+    rows = stacked.shape[0] // 2
+    low = lax.broadcasted_iota(jnp.int32, (rows, stacked.shape[1]), 1) < HEAD
+    return jnp.where(low, stacked[:rows], stacked[rows:])
+
+
+def masked_scores(query, keys2, count, length):
+    scores = dot_nt(query, keys2)
+    slot = lax.broadcasted_iota(jnp.int32, scores.shape, 1)
+    slot = jnp.where(slot >= length, slot - length, slot)
+    return jnp.where(slot < count, scores, -1000000000.0)
+
+
+def halves(stat_a, stat_b, length):
+    rows = stat_a.shape[0]
+    return jnp.concatenate(
+        [jnp.broadcast_to(stat_a, (rows, length)), jnp.broadcast_to(stat_b, (rows, length))], axis=1
+    )
+
+
+def attend_forward(tokens, counts, ids, bufs, sentences, length):
+    rows, width = tokens.shape
+    pairs = width // 128
+    group = 256
+
+    def body(ids_ref, counts_ref, x_ref, b0, b1, b2, b3, qkv_ref, ctx_ref, lse_ref, vec_ref, w_ref, sems):
+        place = Place(ids_ref)
+        copies = piece_copies(place, (b0, b1, b2, b3), w_ref, sems, width // 8, False)
+        for copy in copies:
+            copy.start()
+        for copy in copies:
+            copy.wait()
+        vec_ref[...] = w_ref[:, 3 * width :].astype(F32).T[: vec_ref.shape[0]]
+        x = x_ref[...]
+        for part in range(3):
+            for g in range(width // group):
+                col = part * width + g * group
+                y = dot(x, w_ref[:, col : col + group])
+                if part != 1:
+                    bias = vec_ref[part // 2 : part // 2 + 1, g * group : (g + 1) * group]
+                    y = y + bias
+                qkv_ref[:, col : col + group] = y.astype(BF)
+
+        def sentence(s, carry):
+            row = aligned(s * length, length)
+            count = counts_ref[s]
+            lane = lax.broadcasted_iota(jnp.int32, (length, 128), 1)
+            lse_all = jnp.zeros((length, 128), F32)
+            for p in range(pairs):
+                here = pl.ds(row, length)
+                query = qkv_ref[here, p * 128 : (p + 1) * 128] * jnp.asarray(HEAD**-0.5, BF)
+                keys2 = two_heads(qkv_ref[here, width + p * 128 : width + (p + 1) * 128])
+                values2 = two_heads(qkv_ref[here, 2 * width + p * 128 : 2 * width + (p + 1) * 128])
+                scores = masked_scores(query, keys2, count, length)
+                a, b = scores[:, :length], scores[:, length:]
+                max_a = jnp.max(a, -1, keepdims=True)
+                max_b = jnp.max(b, -1, keepdims=True)
+                e_a, e_b = jnp.exp(a - max_a), jnp.exp(b - max_b)
+                sum_a = jnp.sum(e_a, -1, keepdims=True)
+                sum_b = jnp.sum(e_b, -1, keepdims=True)
+                lse_all = jnp.where(lane == 2 * p, max_a + jnp.log(sum_a), lse_all)
+                lse_all = jnp.where(lane == 2 * p + 1, max_b + jnp.log(sum_b), lse_all)
+                probs = jnp.concatenate([e_a * (1.0 / sum_a), e_b * (1.0 / sum_b)], axis=1).astype(BF)
+                ctx_ref[here, p * 128 : (p + 1) * 128] = dot(probs, values2).astype(BF)
+            lse_ref[pl.ds(row, length), :] = lse_all
+            return carry
+
+        lax.fori_loop(0, sentences, sentence, 0)
+
+    return call(
+        body,
+        "qkv_attention",
+        [(ids, "s"), (counts, "s"), (tokens, "v")] + [(b, "a") for b in bufs],
+        [
+            struct((rows, 3 * width), BF),
+            struct((rows, width), BF),
+            struct((rows, 128), F32),
+            struct((16, width), F32),
+        ],
+        [pltpu.VMEM((width, 3 * width + 128), BF), pltpu.SemaphoreType.DMA((16,))],
+        2 * rows * width * 3 * width + 8 * rows * length * width,
+        rows * length * width // HEAD,
+    )
+
+
+def layer_norm(v):
+    centred = v - jnp.mean(v, -1, keepdims=True)
+    inverse = lax.rsqrt(jnp.mean(centred * centred, -1, keepdims=True) + NORM_EPS)
+    return centred * inverse, inverse
+
+
+def norm_back(grad, normed, inverse, gain):
+    scaled = grad * gain
+    return inverse * (
+        scaled
+        - jnp.mean(scaled, -1, keepdims=True)
+        - normed * jnp.mean(scaled * normed, -1, keepdims=True)
+    )
+
+
+def row(vec_ref, at):
+    return vec_ref[at : at + 1, :]
+
+
+def up_forward(context, tokens, vec, bias_in, ids, bufs, length):
+    rows, width = tokens.shape
+    wide = bias_in.shape[1]
+    group = 256
+
+    def body(ids_ref, ctx_ref, x_ref, vec_ref, bin_ref, *rest):
+        bufs_ref = rest[: len(bufs)]
+        n_ref, inv_ref, low_ref, act_ref, slope_ref, w_ref, sems = rest[len(bufs) :]
+        place = Place(ids_ref)
+        copies = piece_copies(place, bufs_ref, w_ref, sems, width // 8, True)
+        for copy in copies:
+            copy.start()
+        for copy in copies:
+            copy.wait()
+        n_ref[...] = dot(ctx_ref[...], w_ref[:, :width])
+
+        def norm_rows(s, carry):
+            here = pl.ds(aligned(s * length, length), length)
+            v = x_ref[here, :].astype(F32) + (n_ref[here, :] + row(vec_ref, 2))
+            normed, inverse = layer_norm(v)
+            n_ref[here, :] = normed
+            inv_ref[here, :] = jnp.broadcast_to(inverse, (length, 128))
+            low_ref[here, :] = (normed * row(vec_ref, 3) + row(vec_ref, 4)).astype(BF)
+            return carry
+
+        lax.fori_loop(0, rows // length, norm_rows, 0)
+
+        def columns(g, carry):
+            col = aligned(g * group, group)
+            u = dot(low_ref[...], w_ref[:, pl.ds(width + col, group)]) + bin_ref[:, pl.ds(col, group)]
+            cdf = 0.5 * (1.0 + lax.erf(u * (0.5**0.5)))
+            pdf = jnp.exp(-0.5 * u * u) * 0.3989422804014327
+            act_ref[:, pl.ds(col, group)] = (u * cdf).astype(BF)
+            slope_ref[:, pl.ds(col, group)] = (cdf + u * pdf).astype(BF)
+            return carry
+
+        lax.fori_loop(0, wide // group, columns, 0)
+
+    return call(
+        body,
+        "out_norm_up",
+        [(ids, "s"), (context, "v"), (tokens, "v"), (vec, "v"), (bias_in, "v")]
+        + [(b, "a") for b in bufs],
+        [
+            struct((rows, width), F32),
+            struct((rows, 128), F32),
+            struct((rows, width), BF),
+            struct((rows, wide), BF),
+            struct((rows, wide), BF),
+        ],
+        [pltpu.VMEM((width, width + wide), BF), pltpu.SemaphoreType.DMA((32,))],
+        2 * rows * width * (width + wide),
+        2 * rows * wide,
+    )
+
+
+def down_forward(active, normed, vec, counts, pooled_grad, ids, bufs, sentences, length):
+    rows, wide = active.shape
+    width = normed.shape[1]
+    shard = wide // 8
+    group = 256
+
+    def body(ids_ref, counts_ref, act_ref, n_ref, vec_ref, pg_ref, *rest):
+        bufs_ref = rest[: len(bufs)]
+        pooled_ref, gres_ref, glow_ref, vg_ref, send_ref, keep_ref, w_ref, dw_ref, sems = rest[len(bufs) :]
+        place = Place(ids_ref)
+        copies = piece_copies(place, bufs_ref, w_ref, sems, shard, False)
+        for copy in copies:
+            copy.start()
+        for copy in copies:
+            copy.wait()
+        for g in range(width // group):
+            gres_ref[:, g * group : (g + 1) * group] = dot(
+                act_ref[...], w_ref[:, g * group : (g + 1) * group]
+            )
+        vg_ref[...] = jnp.zeros_like(vg_ref)
+
+        def norm_rows(s, carry):
+            here = pl.ds(aligned(s * length, length), length)
+            hidden = n_ref[here, :] * row(vec_ref, 3) + row(vec_ref, 4)
+            n2, inverse = layer_norm(hidden + (gres_ref[here, :] + row(vec_ref, 5)))
+            valid = lax.broadcasted_iota(jnp.int32, (length, width), 0) < counts_ref[s]
+            count = counts_ref[s].astype(F32)
+            out = jnp.where(valid, n2 * row(vec_ref, 6) + row(vec_ref, 7), 0.0)
+            pooled_ref[pl.ds(s, 1), :] = jnp.sum(out, 0, keepdims=True) / count
+            grad = jnp.where(valid, pg_ref[pl.ds(s, 1), :] / count, 0.0)
+            vg_ref[0:1, :] += jnp.sum(grad * n2, 0, keepdims=True)
+            vg_ref[1:2, :] += jnp.sum(grad, 0, keepdims=True)
+            gres = norm_back(grad, n2, inverse, row(vec_ref, 6))
+            gres_ref[here, :] = gres
+            glow = gres.astype(BF)
+            glow_ref[here, :] = glow
+            vg_ref[2:3, :] += jnp.sum(glow.astype(F32), 0, keepdims=True)
+            return carry
+
+        lax.fori_loop(0, sentences, norm_rows, 0)
+        glow_t = glow_ref[...].T
+        for f in range(8):
+            dw_ref[...] = dot(glow_t, act_ref[:, f * shard : (f + 1) * shard])
+            rel = lax.bitwise_xor(place.z * 2 + place.y, f)
+            k, yy = lax.div(rel, 2), lax.rem(rel, 2)
+            half = width // 2
+            for cc, out in ((0, keep_ref), (1, send_ref)):
+                core = lax.bitwise_xor(place.c, cc)
+                out[0, yy, k] = dw_ref[pl.ds(aligned(core * half, half), half), :].astype(BF)
+
+    return call(
+        body,
+        "down_norm_back",
+        [(ids, "s"), (counts, "s"), (active, "v"), (normed, "v"), (vec, "v"), (pooled_grad, "v")]
+        + [(b, "a") for b in bufs],
+        [
+            struct((sentences, width), F32),
+            struct((rows, width), F32),
+            struct((rows, width), BF),
+            struct((8, width), F32),
+            struct((1, 2, 4, width // 2, shard), BF),
+            struct((1, 2, 4, width // 2, shard), BF),
+        ],
+        [pltpu.VMEM((wide, width), BF), pltpu.VMEM((width, shard), F32), pltpu.SemaphoreType.DMA((16,))],
+        4 * rows * width * wide,
+    )
+
+
+def up_backward(glow, slope, low, ids, bufs):
+    rows, width = glow.shape
+    wide = slope.shape[1]
+    shard = wide // 8
+    group = 256
+
+    def body(ids_ref, glow_ref, slope_ref, low_ref, *rest):
+        bufs_ref = rest[: len(bufs)]
+        gup_ref, gbias_ref, send_ref, keep_ref, w_ref, dw_ref, sems = rest[len(bufs) :]
+        place = Place(ids_ref)
+        copies = piece_copies(place, bufs_ref, w_ref, sems, shard, False)
+        for copy in copies:
+            copy.start()
+        for copy in copies:
+            copy.wait()
+        low_t = low_ref[...].T
+
+        def columns(g, carry):
+            col = aligned(g * group, group)
+            gact = dot_nt(glow_ref[...], w_ref[pl.ds(col, group), :])
+            gup = (gact * slope_ref[:, pl.ds(col, group)].astype(F32)).astype(BF)
+            gup_ref[:, pl.ds(col, group)] = gup
+            gbias_ref[:, pl.ds(col, group)] = jnp.sum(gup.astype(F32), 0, keepdims=True)
+            dw_ref[:, pl.ds(col, group)] = dot(low_t, gup)
+            return carry
+
+        lax.fori_loop(0, wide // group, columns, 0)
+        emit_blocks(place, dw_ref, send_ref, keep_ref, width // 8, True)
+
+    blocks = struct((2, 2, 4, width // 16, wide // 2), BF)
+    return call(
+        body,
+        "up_back",
+        [(ids, "s"), (glow, "v"), (slope, "v"), (low, "v")] + [(b, "a") for b in bufs],
+        [struct((rows, wide), BF), struct((1, wide), F32), blocks, blocks],
+        [pltpu.VMEM((wide, width), BF), pltpu.VMEM((width, wide), F32), pltpu.SemaphoreType.DMA((16,))],
+        4 * rows * width * wide,
+    )
+
+
+def hidden_backward(gup, gres, normed, inverse, vec, ids, bufs, length):
+    rows, wide = gup.shape
+    width = gres.shape[1]
+    group = 256
+
+    def body(ids_ref, gup_ref, gres_ref, n_ref, inv_ref, vec_ref, *rest):
+        bufs_ref = rest[: len(bufs)]
+        gattn_ref, glow_ref, gctx_ref, vg_ref, w_ref, sems = rest[len(bufs) :]
+        place = Place(ids_ref)
+        copies = piece_copies(place, bufs_ref, w_ref, sems, width // 8, True)
+        for copy in copies:
+            copy.start()
+        for copy in copies:
+            copy.wait()
+        for g in range(width // group):
+            gattn_ref[:, g * group : (g + 1) * group] = dot_nt(
+                gup_ref[...], w_ref[g * group : (g + 1) * group, width:]
+            )
+        vg_ref[...] = jnp.zeros_like(vg_ref)
+
+        def norm_rows(s, carry):
+            here = pl.ds(aligned(s * length, length), length)
+            grad = gattn_ref[here, :] + gres_ref[here, :]
+            normed = n_ref[here, :]
+            vg_ref[0:1, :] += jnp.sum(grad * normed, 0, keepdims=True)
+            vg_ref[1:2, :] += jnp.sum(grad, 0, keepdims=True)
+            gattn = norm_back(grad, normed, inv_ref[here, 0:1], row(vec_ref, 3))
+            gattn_ref[here, :] = gattn
+            glow = gattn.astype(BF)
+            glow_ref[here, :] = glow
+            vg_ref[2:3, :] += jnp.sum(glow.astype(F32), 0, keepdims=True)
+            return carry
+
+        lax.fori_loop(0, rows // length, norm_rows, 0)
+        for g in range(width // group):
+            gctx_ref[:, g * group : (g + 1) * group] = dot_nt(
+                glow_ref[...], w_ref[g * group : (g + 1) * group, :width]
+            ).astype(BF)
+
+    return call(
+        body,
+        "hidden_back",
+        [(ids, "s"), (gup, "v"), (gres, "v"), (normed, "v"), (inverse, "v"), (vec, "v")]
+        + [(b, "a") for b in bufs],
+        [
+            struct((rows, width), F32),
+            struct((rows, width), BF),
+            struct((rows, width), BF),
+            struct((8, width), F32),
+        ],
+        [pltpu.VMEM((width, width + wide), BF), pltpu.SemaphoreType.DMA((32,))],
+        2 * rows * width * (width + wide),
+    )
+
+
+def attend_backward(qkv, gctx, lse, tokens, context, glow, vgrads, counts, ids, sentences, length):
+    rows, width = tokens.shape
+    pairs = width // 128
+    group = 256
+    total = 4 * width + 256
+
+    def body(ids_ref, counts_ref, qkv_ref, gctx_ref, lse_ref, x_ref, ctx_ref, glow_ref, vg_ref, gqkv_ref, send_ref, keep_ref, dw_ref, vs_ref):
+        place = Place(ids_ref)
+        vs_ref[...] = jnp.zeros_like(vs_ref)
+        vs_ref[0:16, :] = vg_ref[...]
+
+        def sentence(s, carry):
+            here = pl.ds(aligned(s * length, length), length)
+            count = counts_ref[s]
+            lse_all = lse_ref[here, :]
+            for p in range(pairs):
+                cols = slice(p * 128, (p + 1) * 128)
+                query = qkv_ref[here, cols] * jnp.asarray(HEAD**-0.5, BF)
+                keys2 = two_heads(qkv_ref[here, width + p * 128 : width + (p + 1) * 128])
+                values2 = two_heads(qkv_ref[here, 2 * width + p * 128 : 2 * width + (p + 1) * 128])
+                gout = gctx_ref[here, cols]
+                scores = masked_scores(query, keys2, count, length)
+                lse2 = halves(lse_all[:, 2 * p : 2 * p + 1], lse_all[:, 2 * p + 1 : 2 * p + 2], length)
+                probs = jnp.exp(scores - lse2)
+                gprobs = dot_nt(gout, values2)
+                weighted = gprobs * probs
+                sums = halves(
+                    jnp.sum(weighted[:, :length], -1, keepdims=True),
+                    jnp.sum(weighted[:, length:], -1, keepdims=True),
+                    length,
+                )
+                gscores = (probs * (gprobs - sums)).astype(BF)
+                gq = dot(gscores, keys2) * HEAD**-0.5
+                gk = one_of_two(dot_tn(gscores, query))
+                gv = one_of_two(dot_tn(probs.astype(BF), gout))
+                gq, gk, gv = gq.astype(BF), gk.astype(BF), gv.astype(BF)
+                gqkv_ref[here, cols] = gq
+                gqkv_ref[here, width + p * 128 : width + (p + 1) * 128] = gk
+                gqkv_ref[here, 2 * width + p * 128 : 2 * width + (p + 1) * 128] = gv
+                vs_ref[0:1, cols] += jnp.sum(gq.astype(F32), 0, keepdims=True)
+                vs_ref[1:2, cols] += jnp.sum(gv.astype(F32), 0, keepdims=True)
+            return carry
+
+        lax.fori_loop(0, sentences, sentence, 0)
+        x_t = x_ref[...].T
+
+        def columns(g, carry):
+            col = aligned(g * group, group)
+            dw_ref[:, pl.ds(col, group)] = dot(x_t, gqkv_ref[:, pl.ds(col, group)])
+            return carry
+
+        lax.fori_loop(0, 3 * width // group, columns, 0)
+        dw_ref[:, 3 * width : 4 * width] = dot_tn(ctx_ref[...], glow_ref[...])
+        dw_ref[:, 4 * width : 4 * width + 128] = vs_ref[...].T
+        dw_ref[:, 4 * width + 128 :] = jnp.zeros((width, 128), F32)
+        emit_blocks(place, dw_ref, send_ref, keep_ref, width // 8, True)
+
+    blocks = struct((2, 2, 4, width // 16, total // 2), BF)
+    return call(
+        body,
+        "attention_back",
+        [
+            (ids, "s"),
+            (counts, "s"),
+            (qkv, "v"),
+            (gctx, "v"),
+            (lse, "v"),
+            (tokens, "v"),
+            (context, "v"),
+            (glow, "v"),
+            (vgrads, "v"),
+        ],
+        [struct((rows, 3 * width), BF), blocks, blocks],
+        [pltpu.VMEM((width, total), F32), pltpu.VMEM((128, width), F32)],
+        2 * rows * width * 4 * width + 20 * rows * length * width,
+        rows * length * width // HEAD,
+    )
+
+
+def tokens_backward(gqkv, gattn, ids, bufs):
+    rows, width = gattn.shape
+    group = 256
+
+    def body(ids_ref, gqkv_ref, gattn_ref, *rest):
+        bufs_ref = rest[: len(bufs)]
+        gx_ref, w_ref, sems = rest[len(bufs) :]
+        place = Place(ids_ref)
+        copies = piece_copies(place, bufs_ref, w_ref, sems, width // 8, False)
+        for copy in copies:
+            copy.start()
+        for copy in copies:
+            copy.wait()
+        for g in range(width // group):
+            gx_ref[:, g * group : (g + 1) * group] = (
+                dot_nt(gqkv_ref[...], w_ref[g * group : (g + 1) * group, : 3 * width])
+                + gattn_ref[:, g * group : (g + 1) * group]
+            )
+
+    return call(
+        body,
+        "tokens_back",
+        [(ids, "s"), (gqkv, "v"), (gattn, "v")] + [(b, "a") for b in bufs],
+        [struct((rows, width), F32)],
+        [pltpu.VMEM((width, 3 * width + 128), BF), pltpu.SemaphoreType.DMA((16,))],
+        2 * rows * width * 3 * width,
+    )[0]
 
 
 def norm_parts(token_rows, gain_vec, shift_vec):
@@ -19,7 +558,7 @@
     return (normed * gain_vec + shift_vec, normed, inverse)
 
 
-def norm_back(grad_out, normed, inverse, gain_vec):
+def plain_norm_back(grad_out, normed, inverse, gain_vec):
     grad_gain = jnp.sum(grad_out * normed, 0)
     grad_shift = jnp.sum(grad_out, 0)
     scaled = grad_out * gain_vec
@@ -159,7 +698,7 @@
     grad_output = (valid_mask[:, :, None] * per_sentence[:, None, :]).reshape(
         sentences * length, model_width
     )
-    grad_res_ffn, grad_gain_ffn, grad_shift_ffn = norm_back(
+    grad_res_ffn, grad_gain_ffn, grad_shift_ffn = plain_norm_back(
         grad_output, normed_ffn, inverse_ffn, gain_ffn.astype(jnp.float32)
     )
     grad_ffn_low = grad_res_ffn.astype(jnp.bfloat16)
@@ -173,7 +712,7 @@
     grad_hidden = (
         jnp.einsum("tf,df->td", grad_up, w_in, preferred_element_type=jnp.float32) + grad_res_ffn
     )
-    grad_res_attn, grad_gain_attn, grad_shift_attn = norm_back(
+    grad_res_attn, grad_gain_attn, grad_shift_attn = plain_norm_back(
         grad_hidden, normed_attn, inverse_attn, gain_attn.astype(jnp.float32)
     )
     grad_attn_low = grad_res_attn.astype(jnp.bfloat16)
@@ -263,22 +802,6 @@
         lax.all_gather(shift_ffn, "fsdp", axis=0, tiled=True),
     )
     pooled, kept = forward(tokens, lengths, weights)
-    weights = (
-        lax.all_gather(w_qkv, "fsdp", axis=0, tiled=True),
-        lax.all_gather(bias_query, "fsdp", axis=0, tiled=True),
-        lax.all_gather(bias_value, "fsdp", axis=0, tiled=True),
-        lax.all_gather(w_out, "fsdp", axis=0, tiled=True),
-        lax.all_gather(bias_out, "fsdp", axis=0, tiled=True),
-        lax.all_gather(gain_attn, "fsdp", axis=0, tiled=True),
-        lax.all_gather(shift_attn, "fsdp", axis=0, tiled=True),
-        lax.all_gather(w_in, "fsdp", axis=0, tiled=True),
-        lax.all_gather(bias_in, "fsdp", axis=0, tiled=True),
-        lax.all_gather(w_down, "fsdp", axis=0, tiled=True),
-        lax.all_gather(bias_down, "fsdp", axis=0, tiled=True),
-        lax.all_gather(gain_ffn, "fsdp", axis=0, tiled=True),
-        lax.all_gather(shift_ffn, "fsdp", axis=0, tiled=True),
-    )
-    kept = forward(tokens, lengths, weights)[1]
     grad_terms, grad_tokens = backward(tokens, lengths, pooled_grad, weights, kept)
     (
         grad_w_qkv,
@@ -359,6 +882,153 @@
     )
 
 
+def swap(array, axis, bits):
+    pairs = [(i, i ^ bits) for i in range(lax.axis_size(axis))]
+    return lax.ppermute(array, axis, pairs)
+
+
+def gather(piece, split_x):
+    near = jnp.stack([piece] + [swap(piece, "fsdp", 2 * k) for k in range(1, 4)])
+    far = swap(near, "fsdp", 1)
+    mine = [near, far]
+    if split_x:
+        mine += [swap(near, "dp", 2), swap(far, "dp", 2)]
+    return mine + [swap(m, "dp", 1) for m in mine]
+
+
+def add(*terms):
+    total = terms[0].astype(F32)
+    for term in terms[1:]:
+        total = total + term.astype(F32)
+    return total.astype(BF)
+
+
+def scatter(send, keep, split_x):
+    total = add(keep, swap(send, "dp", 1))
+    if split_x:
+        total = add(total[0], swap(total[1], "dp", 2))
+    else:
+        total = total[0]
+    total = add(total[0], swap(total[1], "fsdp", 1))
+    total = add(total[0], *[swap(total[k], "fsdp", 2 * k) for k in range(1, 4)])
+    if split_x:
+        own = [total, swap(total, "dp", 2)]
+    else:
+        own = [add(total, swap(total, "dp", 2))]
+    return own, [swap(part, "dp", 1) for part in own]
+
+
+def in_order(own, other, bit, axis):
+    first = jnp.where(bit == 0, own, other)
+    second = jnp.where(bit == 0, other, own)
+    return jnp.concatenate([first, second], axis=axis)
+
+
+def on_device_split(
+    tokens,
+    lengths,
+    pooled_grad,
+    w_qkv,
+    bias_query,
+    bias_value,
+    w_out,
+    bias_out,
+    gain_attn,
+    shift_attn,
+    w_in,
+    bias_in,
+    w_down,
+    bias_down,
+    gain_ffn,
+    shift_ffn,
+):
+    sentences, length, width = tokens.shape
+    rows = sentences * length
+    wide = w_in.shape[1]
+    part = width // 8
+    dp, fsdp = lax.axis_index("dp"), lax.axis_index("fsdp")
+    x, c = dp // 2, dp % 2
+    ids = jnp.stack([fsdp // 2, fsdp % 2, x, c]).astype(jnp.int32)
+    token_rows = tokens.reshape(rows, width)
+
+    vectors = jnp.stack(
+        [bias_query, bias_value, bias_out, gain_attn, shift_attn, bias_down, gain_ffn, shift_ffn]
+    )
+    vectors = jnp.concatenate([vectors, bias_in.reshape(wide // width, part)], 0)
+    vectors = jnp.pad(vectors.T, ((0, 0), (0, 128 - vectors.shape[0])))
+    first = jnp.concatenate([w_qkv, vectors], 1)
+    second = jnp.concatenate([w_out, w_in], 1)
+    half = part // 2
+    first = lax.dynamic_slice(first, (c * half, 0), (half, first.shape[1]))
+    span = second.shape[1] // 2
+    second = lax.dynamic_slice(second, (c * half, x * span), (half, span))
+    third = lax.dynamic_slice(w_down, (c * (w_down.shape[0] // 2), 0), (w_down.shape[0] // 2, width))
+    first, second, third = gather(first, False), gather(second, True), gather(third, False)
+
+    qkv, context, lse, vec = attend_forward(token_rows, lengths, ids, first, sentences, length)
+    ratio = wide // width
+    bias_up = vec[8 : 8 + ratio].reshape(ratio, 8, part).transpose(1, 0, 2).reshape(1, wide)
+    normed, inverse, low, active, slope = up_forward(
+        context, token_rows, vec, bias_up, ids, second, length
+    )
+    pooled, gres, glow, vg_ffn, send3, keep3 = down_forward(
+        active, normed, vec, lengths, pooled_grad, ids, third, sentences, length
+    )
+    down = scatter(send3, keep3, False)
+    gup, gbias_in, send2, keep2 = up_backward(glow, slope, low, ids, third)
+    up = scatter(send2, keep2, True)
+    gattn, gattn_low, gctx, vg_attn = hidden_backward(
+        gup, gres, normed, inverse, vec, ids, second, length
+    )
+    vgrads = jnp.concatenate(
+        [
+            jnp.zeros((2, width), F32),
+            vg_attn[2:3],
+            vg_attn[0:2],
+            vg_ffn[2:3],
+            vg_ffn[0:2],
+            gbias_in.reshape(8, ratio, part).transpose(1, 0, 2).reshape(ratio, width),
+            jnp.zeros((8 - ratio, width), F32),
+        ],
+        0,
+    )
+    gqkv, send1, keep1 = attend_backward(
+        qkv, gctx, lse, token_rows, context, gattn_low, vgrads, lengths, ids, sentences, length
+    )
+    rest = scatter(send1, keep1, True)
+    gtokens = tokens_backward(gqkv, gattn, ids, first).reshape(sentences, length, width)
+
+    def joined(parts, split_x):
+        own, other = parts
+        if split_x:
+            own, other = in_order(*own, x, 1), in_order(*other, x, 1)
+        else:
+            own, other = own[0], other[0]
+        return in_order(own, other, c, 0).astype(F32)
+
+    g_down = joined(down, False).T
+    g_in = joined(up, True)
+    g_rest = joined(rest, True)
+    g_vec = g_rest[:, 4 * width : 4 * width + 8 + ratio].T
+    return (
+        pooled,
+        gtokens,
+        g_rest[:, : 3 * width],
+        g_vec[0],
+        g_vec[1],
+        g_rest[:, 3 * width : 4 * width],
+        g_vec[2],
+        g_vec[3],
+        g_vec[4],
+        g_in,
+        g_vec[8:].reshape(wide // 8),
+        g_down,
+        g_vec[5],
+        g_vec[6],
+        g_vec[7],
+    )
+
+
 def solution(mesh):
     placed = (
         P(("dp", "fsdp"), None, None),
@@ -378,8 +1048,9 @@
         P("fsdp"),
         P("fsdp"),
     )
+    body = on_device_split if mesh.shape["fsdp"] == 8 and mesh.shape["dp"] == 4 else on_device
     return jax.shard_map(
-        on_device,
+        body,
         mesh=mesh,
         in_specs=placed,
         out_specs=(

time: 924 us -> 393 us (0.43)
  waiting for transfers between devices: 564 us -> 111 us
  Pallas kernels: 0 us -> 162 us
  matrix products: 132 us -> 0 us
  blocking collectives: 111 us -> 0 us
  starting transfers between devices: 0.36 us -> 83.3 us
  local copies, waits for them, and re-layouts: 65.7 us -> 15.7 us
  between operations: 16.8 us -> 1.33 us
  other arithmetic: 30.4 us -> 15.9 us
    reduce_scatter x3 -> x0, waiting for transfers between devices: 325 us -> none  [the longest x1 163 us: on_device(): lax.psum_scatter(grad_w_in, 'fsdp', scatter_dimension=0, tiled=True)]
    pallas_call x0 -> x7, Pallas kernels: none -> 162 us  [call(): pl.pallas_call(body, name=name, out_shape=tuple(outs), in_specs=[spaces[s...]
    dot_general x18 -> x0, matrix products: 132 us -> none  [the longest x1 32.9 us: forward(): jnp.dot(hidden_low, w_in, preferred_element_type=jnp.float32)]
    all_gather x4 -> x0, waiting for transfers between devices: 121 us -> none  [the longest x1 74.1 us: on_device(): lax.all_gather(w_in, 'fsdp', axis=0, tiled=True)]
    ppermute x0 -> x47, waiting for transfers between devices: none -> 111 us  [swap(): return lax.ppermute(array, axis, pairs)]
    ppermute x0 -> x47, starting transfers between devices: none -> 83.3 us  [swap(): return lax.ppermute(array, axis, pairs)]
    unnamed x2 -> x0, blocking collectives: 78.3 us -> none
    unnamed x10 -> x0, waiting for transfers between devices: 76.5 us -> none
  transfers between devices with their start and end apart: 9 -> 47, of which waited for: 6 -> 16; matrix products, arithmetic and copies ran while one was open for 18% -> 6% of each run, Pallas kernels for 0% -> 35%
where the time goes in v1:
time: 393 us; the launch traced here: 389 us
  Pallas kernels  162 us (41%)
  waiting for transfers between devices  111 us (28%)
  starting transfers between devices  83.3 us (21%)
  other arithmetic  15.9 us (4%)
  local copies, waits for them, and re-layouts  15.7 us (4%)
    pallas_call x7, Pallas kernels, call(): pl.pallas_call(body, name=name, out_shape=tuple(outs), in_specs=[spaces[s...  162 us
    ppermute x47, waiting for transfers between devices, swap(): return lax.ppermute(array, axis, pairs)  111 us
    ppermute x47, starting transfers between devices, swap(): return lax.ppermute(array, axis, pairs)  83.3 us
    convert_element_type x12, other arithmetic, add(): return total.astype(BF)  8.9 us
  transfers between devices with their start and end apart: 47, of which 16 were waited for; matrix products, arithmetic and copies ran while one was open for 6% of the time, Pallas kernels for 35%

profile of v1, /device:TPU:0, one launch (start us, length us, event | category | flops | bytes accessed | tf_op | source)
XLA Modules:
  0.0 388.6 jit_solution(9791673158386743568)
XLA Ops:
  0.7 0.8 reshape.75
  2.4 1.0 fusion.15
  3.4 3.1 collective-permute-start
  6.5 2.6 collective-permute-start.1
  9.1 1.0 fusion.16
  10.1 1.0 collective-permute-start.6
  11.0 3.5 collective-permute-start.7
  14.5 2.8 collective-permute-done
  17.3 4.5 %collective-permute-start.8 = (bf16[48,1920]{1,0:T(8,128)(2,1)S(1)}, bf16[48,1920]{1,0:T(8,128)(2,1)S(1)}, u32[]{:S(2)}, u32[]{:S(2)}) collective-permute-start(bf16[48,1920]{1,0:T(8,128)(2,1)S(1)} %fusion.16), channel_id=1, source_target_pairs={{0,6},{1,7},{2,4},{3,5},{4,2},{5,3},{6,0},{7,1},{8,14},{9,15},{10,... | collective-permute-start | bytes 552968 | tf_op jit(solution)/shard_map/ppermute | solution.py:887
  21.9 4.2 %collective-permute-done.1 = bf16[48,2432]{1,0:T(8,128)(2,1)S(1)} collective-permute-done((bf16[48,2432]{1,0:T(8,128)(2,1)S(1)}, bf16[48,2432]{1,0:T(8,128)(2,1)S(1)}, u32[]{:S(2)}, u32[]{:S(2)}) %collective-permute-start.1) | collective-permute-done | bytes 233504 | tf_op jit(solution)/shard_map/ppermute | solution.py:887
  26.2 1.6 collective-permute-start.3
  27.8 13.5 %collective-permute-start.16 = (bf16[192,768]{1,0:T(8,128)(2,1)S(1)}, bf16[192,768]{1,0:T(8,128)(2,1)S(1)}, u32[]{:S(2)}, u32[]{:S(2)}) collective-permute-start(bf16[192,768]{1,0:T(8,128)(2,1)S(1)} %constant_dynamic-slice_fusion), channel_id=1, source_target_pairs={{0,2},{1,3},{2,0},{3,1},{4,6},{5,7},{6,4},{7,5},{8,10},{9,11},{10,... | collective-permute-start | bytes 884744 | tf_op jit(solution)/shard_map/ppermute | solution.py:887
  41.3 1.1 collective-permute-start.17
  43.0 4.2 %collective-permute-start.18 = (bf16[192,768]{1,0:T(8,128)(2,1)S(1)}, bf16[192,768]{1,0:T(8,128)(2,1)S(1)}, u32[]{:S(2)}, u32[]{:S(2)}) collective-permute-start(bf16[192,768]{1,0:T(8,128)(2,1)S(1)} %constant_dynamic-slice_fusion), channel_id=1, source_target_pairs={{0,6},{1,7},{2,4},{3,5},{4,2},{5,3},{6,0},{7,1},{8,14},{9,15},{10,... | collective-permute-start | bytes 884744 | tf_op jit(solution)/shard_map/ppermute | solution.py:887
  47.3 1.1 pad_maximum_fusion.2.rest_0_
  48.4 2.7 collective-permute-start.9
  51.1 1.5 collective-permute-start.10
  52.6 13.2 %collective-permute-done.17 = bf16[192,768]{1,0:T(8,128)(2,1)S(1)} collective-permute-done((bf16[192,768]{1,0:T(8,128)(2,1)S(1)}, bf16[192,768]{1,0:T(8,128)(2,1)S(1)}, u32[]{:S(2)}, u32[]{:S(2)}) %collective-permute-start.17) | collective-permute-done | bytes 294944 | tf_op jit(solution)/shard_map/ppermute | solution.py:887
  66.0 1.6 collective-permute-start.19
  68.2 1.5 collective-permute-start.11
  69.7 2.8 collective-permute-done.12.rest_4_
  73.0 14.3 %collective-permute-done.11.rest_3_ = bf16[4,48,1920]{2,1,0:T(8,128)(2,1)} collective-permute-done((bf16[4,48,1920]{2,1,0:T(8,128)(2,1)}, bf16[4,48,1920]{2,1,0:T(8,128)(2,1)}, u32[]{:S(2)}, u32[]{:S(2)}) %collective-permute-start.11) | collective-permute-done | bytes 737312 | tf_op jit(solution)/shard_map/ppermute | solution.py:887
  87.3 4.1 %collective-permute-done.19.rest_1_ = bf16[4,192,768]{2,1,0:T(8,128)(2,1)} collective-permute-done((bf16[4,192,768]{2,1,0:T(8,128)(2,1)S(1)}, bf16[4,192,768]{2,1,0:T(8,128)(2,1)}, u32[]{:S(2)}, u32[]{:S(2)}) %collective-permute-start.19) | collective-permute-done | bytes 1179680 | tf_op jit(solution)/shard_map/ppermute | solution.py:887
  91.5 0.9 copy-done.8
  93.5 15.8 %qkv_attention.1 = (bf16[896,2304]{1,0:T(8,128)(2,1)}, bf16[896,768]{1,0:T(8,128)(2,1)}, f32[896,128]{1,0:T(8,128)}, f32[16,768]{1,0:T(8,128)}) custom-call(s32[4]{0:T(128)} %pad_add_fusion.ids_ref, s32[7]{0:T(128)} %counts_ref.5, bf16[896,768]{1,0:T(8,128)(2,1)} %bitcast.127, bf16[4,48,2432]{2,1,0:T(8,128)(2,1)} %copy-done.2, ...), custom_call_target="tpu_custom_call" | custom-call | flops 3875536896 | bytes 11124780 | tf_op jit(solution)/shard_map/qkv_attention/pallas_call | solution.py:98
  110.8 0.9 copy-done.13
  111.7 21.4 %out_norm_up.1 = (f32[896,768]{1,0:T(8,128)}, f32[896,128]{1,0:T(8,128)}, bf16[896,768]{1,0:T(8,128)(2,1)}, bf16[896,3072]{1,0:T(8,128)(2,1)}, bf16[896,3072]{1,0:T(8,128)(2,1)}) custom-call(s32[4]{0:T(128)} %pad_add_fusion.ids_ref, bf16[896,768]{1,0:T(8,128)(2,1)} %get-tuple-element.41.ctx_ref, bf16[896,768]{1,0:T(8,128)(2,1)} %bitcast.128, ...), custom_call_target="tpu_custom_call" | custom-call | flops 5284823040 | bytes 24309776 | tf_op jit(solution)/shard_map/out_norm_up/pallas_call | solution.py:98
  133.1 1.0 copy-done.11
  134.1 25.4 %down_norm_back.1 = (f32[7,768]{1,0:T(8,128)}, f32[896,768]{1,0:T(8,128)}, bf16[896,768]{1,0:T(8,128)(2,1)}, f32[8,768]{1,0:T(8,128)}, bf16[1,2,4,384,384]{4,3,2...) custom-call(s32[4]{0:T(128)} %pad_add_fusion.ids_ref, s32[7]{0:T(128)} %counts_ref.5, ...), custom_call_target="tpu_custom_call" | custom-call | flops 8455716864 | bytes 21940268 | tf_op jit(solution)/shard_map/down_norm_back/pallas_call | solution.py:98
  159.6 30.4 %up_back.1 = (bf16[896,3072]{1,0:T(8,128)(2,1)}, f32[1,3072]{1,0:T(1,128)}, bf16[2,2,4,48,1536]{4,3,2,1,0:T(8,128)(2,1)}, bf16[2,2,4,48,1536]{4,3,2,1,0:T(8,128)(2,1)}) custom-call(s32[4]{0:T(128)} %pad_add_fusion.ids_ref, bf16[896,768]{1,0:T(8,128)(2,1)} %get-tuple-element.47.glow_ref, bf16[896,3072]{1,0:T(8,128)(2,1)} %get-tuple-element.48.slope_ref, ...), custom_call_target="tpu_custom_call" | custom-call | flops 8455716864 | bytes 23212048 | tf_op jit(solution)/shard_map/up_back/pallas_call | solution.py:98
  190.5 28.8 %hidden_back.1 = (f32[896,768]{1,0:T(8,128)}, bf16[896,768]{1,0:T(8,128)(2,1)}, bf16[896,768]{1,0:T(8,128)(2,1)}, f32[8,768]{1,0:T(8,128)}) custom-call(s32[4]{0:T(128)} %pad_add_fusion.ids_ref, bf16[896,3072]{1,0:T(8,128)(2,1)} %get-tuple-element.50.gup_ref, f32[896,768]{1,0:T(8,128)} %get-tuple-element.51.gres_ref, f32[896,768]{1,0:T(8,128)} %get-tuple-element.44.n_ref, ...), custom_call_target="tpu_custom_call" | custom-call | flops 5284823040 | bytes 22945808 | tf_op jit(solution)/shard_map/hidden_back/pallas_call | solution.py:98
  223.7 1.3 concatenate.36.vg_ref
  224.9 29.6 %attention_back.1 = (bf16[896,2304]{1,0:T(8,128)(2,1)}, bf16[2,2,4,48,1664]{4,3,2,1,0:T(8,128)(2,1)}, bf16[2,2,4,48,1664]{4,3,2,1,0:T(8,128)(2,1)}) custom-call(s32[4]{0:T(128)} %pad_add_fusion.ids_ref, s32[7]{0:T(128)} %counts_ref.5, bf16[896,2304]{1,0:T(8,128)(2,1)} %get-tuple-element.46.qkv_ref, bf16[896,768]{1,0:T(8,128)(2,1)} %get-tuple-element.53.gctx_ref, ...), custom_call_target="tpu_custom_call" | custom-call | flops 5989466112 | bytes 19382316 | tf_op jit(solution)/shard_map/attention_back/pallas_call | solution.py:98
  254.5 10.3 %tokens_back.1 = f32[896,768]{1,0:T(8,128)} custom-call(s32[4]{0:T(128)} %pad_add_fusion.ids_ref, bf16[896,2304]{1,0:T(8,128)(2,1)} %get-tuple-element.59.gqkv_ref, f32[896,768]{1,0:T(8,128)} %get-tuple-element.60.gattn_ref, bf16[4,48,2432]{2,1,0:T(8,128)(2,1)} %copy-done.2, bf16[4,48,2432]{2,1,0:T(8,128)(2,1)} %copy-done.6, bf16[4,48,2432]{2,1,0:T(8,128)(2,1)} %copy-done.7, ...), custom_call_target="tpu_custom_call" | custom-call | flops 3170893824 | bytes 13369360 | tf_op jit(solution)/shard_map/tokens_back/pallas_call | solution.py:98
  264.8 3.0 add_convert_fusion.1
  267.9 1.6 collective-permute-start.41
  269.5 2.5 add_convert_fusion.2
  272.1 1.6 collective-permute-start.32
  275.0 21.3 %collective-permute-done.41 = bf16[4,384,384]{2,1,0:T(8,128)(2,1)S(1)} collective-permute-done((bf16[4,384,384]{2,1,0:T(8,128)(2,1)S(1)}, bf16[4,384,384]{2,1,0:T(8,128)(2,1)S(1)}, u32[]{:S(2)}, u32[]{:S(2)}) %collective-permute-start.41) | collective-permute-done | bytes 1179680 | tf_op jit(solution)/shard_map/ppermute | solution.py:887
  296.8 8.6 %collective-permute-start.42 = (bf16[384,384]{1,0:T(8,128)(2,1)S(1)}, bf16[384,384]{1,0:T(8,128)(2,1)S(1)}, u32[]{:S(2)}, u32[]{:S(2)}) collective-permute-start(bf16[384,384]{1,0:T(8,128)(2,1)S(1)} %get-tuple-element.120), channel_id=1, source_target_pairs={{0,2},{1,3},{2,0},{3,1},{4,6},{5,7},{6,4},{7,5},{8,10},{9,11},{10,... | collective-permute-start | bytes 884744 | tf_op jit(solution)/shard_map/ppermute | solution.py:887
  305.4 2.0 collective-permute-start.43
  307.4 1.4 collective-permute-start.44
  309.1 1.6 collective-permute-start.33
  310.7 17.1 %collective-permute-done.23 = bf16[2,4,48,1664]{3,2,1,0:T(8,128)(2,1)S(1)} collective-permute-done((bf16[2,4,48,1664]{3,2,1,0:T(8,128)(2,1)S(1)}, bf16[2,4,48,1664]{3,2,1,0:T(8,128)(2,1)S(1)}, u32[]{:S(2)}, u32[]{:S(2)}) %collective-permute-start.23) | collective-permute-done | bytes 1277984 | tf_op jit(solution)/shard_map/ppermute | solution.py:887
  328.3 1.6 collective-permute-start.24
  330.0 1.6 collective-permute-start.45
  331.8 8.6 %collective-permute-start.34 = (bf16[48,1536]{1,0:T(8,128)(2,1)S(1)}, bf16[48,1536]{1,0:T(8,128)(2,1)S(1)}, u32[]{:S(2)}, u32[]{:S(2)}) collective-permute-start(bf16[48,1536]{1,0:T(8,128)(2,1)S(1)} %get-tuple-element.132), channel_id=1, source_target_pairs={{0,2},{1,3},{2,0},{3,1},{4,6},{5,7},{6,4},{7,5},{8,10},{9,11},{10,... | collective-permute-start | bytes 442376 | tf_op jit(solution)/shard_map/ppermute | solution.py:887
  340.4 2.0 collective-permute-start.35
  342.4 1.4 collective-permute-start.36
  343.9 1.3 collective-permute-done.34
  345.2 9.1 %collective-permute-done.35 = bf16[48,1536]{1,0:T(8,128)(2,1)S(1)} collective-permute-done((bf16[48,1536]{1,0:T(8,128)(2,1)S(1)}, bf16[48,1536]{1,0:T(8,128)(2,1)S(1)}, u32[]{:S(2)}, u32[]{:S(2)}) %collective-permute-start.35) | collective-permute-done | bytes 147488 | tf_op jit(solution)/shard_map/ppermute | solution.py:887
  355.2 1.4 copy.59
  356.6 3.1 collective-permute-done.37
  359.7 1.2 fusion.3
  360.9 2.2 collective-permute-start.25
  363.2 1.3 collective-permute-start.26
  364.4 1.4 collective-permute-start.27
  366.0 5.1 %collective-permute-done.25 = bf16[48,1664]{1,0:T(8,128)(2,1)S(1)} collective-permute-done((bf16[48,1664]{1,0:T(8,128)(2,1)S(1)}, bf16[48,1664]{1,0:T(8,128)(2,1)S(1)}, u32[]{:S(2)}, u32[]{:S(2)}) %collective-permute-start.25) | collective-permute-done | bytes 159776 | tf_op jit(solution)/shard_map/ppermute | solution.py:887
  371.0 6.9 %collective-permute-done.26 = bf16[48,1664]{1,0:T(8,128)(2,1)S(1)} collective-permute-done((bf16[48,1664]{1,0:T(8,128)(2,1)S(1)}, bf16[48,1664]{1,0:T(8,128)(2,1)S(1)}, u32[]{:S(2)}, u32[]{:S(2)}) %collective-permute-start.26) | collective-permute-done | bytes 159776 | tf_op jit(solution)/shard_map/ppermute | solution.py:887
  378.6 1.1 maximum_convert_fusion.1
  379.8 3.6 collective-permute-done.28
  383.4 1.3 collective-permute-done.30
  385.8 0.9 slice_reduce_fusion
  387.5 1.0 slice.166
  (130 shorter events, 17.5 us)
Async XLA Ops:
  0.6 27.1 %copy-start = (bf16[384,768]{1,0:T(8,128)(2,1)S(1)}, bf16[384,768]{1,0:T(8,128)(2,1)}, u32[]{:S(2)}) copy-start(bf16[384,768]{1,0:T(8,128)(2,1)} %param.28) | copy-start | bytes 1769476
  3.4 13.9 %collective-permute-start = (bf16[48,2432]{1,0:T(8,128)(2,1)S(1)}, bf16[48,2432]{1,0:T(8,128)(2,1)S(1)}, u32[]{:S(2)}, u32[]{:S(2)}) collective-permute-start(bf16[48,2432]{1,0:T(8,128)(2,1)S(1)} %fusion.15), channel_id=1, source_target_pairs={{0,2},{1,3},{2,0},{3,1},{4,6},{5,7},{6,4},{7,5},{8,10},{9,11},{10,... | collective-permute-start | bytes 700424 | tf_op jit(solution)/shard_map/ppermute | solution.py:887
  6.5 19.5 %collective-permute-start.1 = (bf16[48,2432]{1,0:T(8,128)(2,1)S(1)}, bf16[48,2432]{1,0:T(8,128)(2,1)S(1)}, u32[]{:S(2)}, u32[]{:S(2)}) collective-permute-start(bf16[48,2432]{1,0:T(8,128)(2,1)S(1)} %fusion.15), channel_id=1, source_target_pairs={{0,4},{1,5},{2,6},{3,7},{4,0},{5,1},{6,2},{7,3},{8,12},{9,13},{10,... | collective-permute-start | bytes 700424 | tf_op jit(solution)/shard_map/ppermute | solution.py:887
  9.1 16.9 %collective-permute-start.2 = (bf16[48,2432]{1,0:T(8,128)(2,1)S(1)}, bf16[48,2432]{1,0:T(8,128)(2,1)S(1)}, u32[]{:S(2)}, u32[]{:S(2)}) collective-permute-start(bf16[48,2432]{1,0:T(8,128)(2,1)S(1)} %fusion.15), channel_id=1, source_target_pairs={{0,6},{1,7},{2,4},{3,5},{4,2},{5,3},{6,0},{7,1},{8,14},{9,15},{10,... | collective-permute-start | bytes 700424 | tf_op jit(solution)/shard_map/ppermute | solution.py:887
  10.1 31.2 %collective-permute-start.6 = (bf16[48,1920]{1,0:T(8,128)(2,1)S(1)}, bf16[48,1920]{1,0:T(8,128)(2,1)}, u32[]{:S(2)}, u32[]{:S(2)}) collective-permute-start(bf16[48,1920]{1,0:T(8,128)(2,1)S(1)} %fusion.16), channel_id=1, source_target_pairs={{0,2},{1,3},{2,0},{3,1},{4,6},{5,7},{6,4},{7,5},{8,10},{9,11},{10,... | collective-permute-start | bytes 552968 | tf_op jit(solution)/shard_map/ppermute | solution.py:887
  11.0 32.0 %collective-permute-start.7 = (bf16[48,1920]{1,0:T(8,128)(2,1)S(1)}, bf16[48,1920]{1,0:T(8,128)(2,1)}, u32[]{:S(2)}, u32[]{:S(2)}) collective-permute-start(bf16[48,1920]{1,0:T(8,128)(2,1)S(1)} %fusion.16), channel_id=1, source_target_pairs={{0,4},{1,5},{2,6},{3,7},{4,0},{5,1},{6,2},{7,3},{8,12},{9,13},{10,... | collective-permute-start | bytes 552968 | tf_op jit(solution)/shard_map/ppermute | solution.py:887
  17.3 30.0 %collective-permute-start.8 = (bf16[48,1920]{1,0:T(8,128)(2,1)S(1)}, bf16[48,1920]{1,0:T(8,128)(2,1)S(1)}, u32[]{:S(2)}, u32[]{:S(2)}) collective-permute-start(bf16[48,1920]{1,0:T(8,128)(2,1)S(1)} %fusion.16), channel_id=1, source_target_pairs={{0,6},{1,7},{2,4},{3,5},{4,2},{5,3},{6,0},{7,1},{8,14},{9,15},{10,... | collective-permute-start | bytes 552968 | tf_op jit(solution)/shard_map/ppermute | solution.py:887
  26.2 41.4 %copy-start.2 = (bf16[4,48,2432]{2,1,0:T(8,128)(2,1)}, bf16[4,48,2432]{2,1,0:T(8,128)(2,1)S(1)}, u32[]{:S(2)}) copy-start(bf16[4,48,2432]{2,1,0:T(8,128)(2,1)S(1)} %pad_maximum_fusion.1.b0.rest_0_) | copy-start | bytes 2801668
  26.2 41.4 %collective-permute-start.3 = (bf16[4,48,2432]{2,1,0:T(8,128)(2,1)S(1)}, bf16[4,48,2432]{2,1,0:T(8,128)(2,1)S(1)}, u32[]{:S(2)}, u32[]{:S(2)}) collective-permute-start(bf16[4,48,2432]{2,1,0:T(8,128)(2,1)S(1)} %pad_maximum_fusion.1.b0.rest_0_), channel_id=1, source_target_pairs={{0,1},{1,0},{2,3},{3,2},{4,5},{5,4},{6,7},{7,6},{8,9},{9,8},{10,11... | collective-permute-start | bytes 2801672 | tf_op jit(solution)/shard_map/ppermute | solution.py:887
  27.8 23.3 %collective-permute-start.16 = (bf16[192,768]{1,0:T(8,128)(2,1)S(1)}, bf16[192,768]{1,0:T(8,128)(2,1)S(1)}, u32[]{:S(2)}, u32[]{:S(2)}) collective-permute-start(bf16[192,768]{1,0:T(8,128)(2,1)S(1)} %constant_dynamic-slice_fusion), channel_id=1, source_target_pairs={{0,2},{1,3},{2,0},{3,1},{4,6},{5,7},{6,4},{7,5},{8,10},{9,11},{10,... | collective-permute-start | bytes 884744 | tf_op jit(solution)/shard_map/ppermute | solution.py:887
  41.3 24.5 %collective-permute-start.17 = (bf16[192,768]{1,0:T(8,128)(2,1)S(1)}, bf16[192,768]{1,0:T(8,128)(2,1)S(1)}, u32[]{:S(2)}, u32[]{:S(2)}) collective-permute-start(bf16[192,768]{1,0:T(8,128)(2,1)S(1)} %constant_dynamic-slice_fusion), channel_id=1, source_target_pairs={{0,4},{1,5},{2,6},{3,7},{4,0},{5,1},{6,2},{7,3},{8,12},{9,13},{10,... | collective-permute-start | bytes 884744 | tf_op jit(solution)/shard_map/ppermute | solution.py:887
  43.0 22.8 %collective-permute-start.18 = (bf16[192,768]{1,0:T(8,128)(2,1)S(1)}, bf16[192,768]{1,0:T(8,128)(2,1)S(1)}, u32[]{:S(2)}, u32[]{:S(2)}) collective-permute-start(bf16[192,768]{1,0:T(8,128)(2,1)S(1)} %constant_dynamic-slice_fusion), channel_id=1, source_target_pairs={{0,6},{1,7},{2,4},{3,5},{4,2},{5,3},{6,0},{7,1},{8,14},{9,15},{10,... | collective-permute-start | bytes 884744 | tf_op jit(solution)/shard_map/ppermute | solution.py:887
  48.4 19.7 %copy-start.9 = (bf16[4,48,1920]{2,1,0:T(8,128)(2,1)}, bf16[4,48,1920]{2,1,0:T(8,128)(2,1)S(1)}, u32[]{:S(2)}) copy-start(bf16[4,48,1920]{2,1,0:T(8,128)(2,1)S(1)} %pad_maximum_fusion.2.rest_0_) | copy-start | bytes 2211844
  48.4 19.7 %collective-permute-start.9 = (bf16[4,48,1920]{2,1,0:T(8,128)(2,1)S(1)}, bf16[4,48,1920]{2,1,0:T(8,128)(2,1)}, u32[]{:S(2)}, u32[]{:S(2)}) collective-permute-start(bf16[4,48,1920]{2,1,0:T(8,128)(2,1)S(1)} %pad_maximum_fusion.2.rest_0_), channel_id=1, source_target_pairs={{0,1},{1,0},{2,3},{3,2},{4,5},{5,4},{6,7},{7,6},{8,9},{9,8},{10,11... | collective-permute-start | bytes 2211848 | tf_op jit(solution)/shard_map/ppermute | solution.py:887
  51.1 17.1 %collective-permute-start.10 = (bf16[4,48,1920]{2,1,0:T(8,128)(2,1)S(1)}, bf16[4,48,1920]{2,1,0:T(8,128)(2,1)}, u32[]{:S(2)}, u32[]{:S(2)}) collective-permute-start(bf16[4,48,1920]{2,1,0:T(8,128)(2,1)S(1)} %pad_maximum_fusion.2.rest_0_), channel_id=1, source_target_pairs={{0,16},{8,24},{16,0},{24,8},{1,17},{9,25},{17,1},{25,9},{2,18},{10... | collective-permute-start | bytes 2211848 | tf_op jit(solution)/shard_map/ppermute | solution.py:887
  66.0 43.3 %copy-start.5 = (bf16[4,192,768]{2,1,0:T(8,128)(2,1)}, bf16[4,192,768]{2,1,0:T(8,128)(2,1)S(1)}, u32[]{:S(2)}) copy-start(bf16[4,192,768]{2,1,0:T(8,128)(2,1)S(1)} %pad_maximum_fusion.rest_0_) | copy-start | bytes 3538948
  66.0 25.4 %collective-permute-start.19 = (bf16[4,192,768]{2,1,0:T(8,128)(2,1)S(1)}, bf16[4,192,768]{2,1,0:T(8,128)(2,1)}, u32[]{:S(2)}, u32[]{:S(2)}) collective-permute-start(bf16[4,192,768]{2,1,0:T(8,128)(2,1)S(1)} %pad_maximum_fusion.rest_0_), channel_id=1, source_target_pairs={{0,1},{1,0},{2,3},{3,2},{4,5},{5,4},{6,7},{7,6},{8,9},{9,8},{10,11... | collective-permute-start | bytes 3538952 | tf_op jit(solution)/shard_map/ppermute | solution.py:887
  67.6 5.0 %collective-permute-start.4 = (bf16[4,48,2432]{2,1,0:T(8,128)(2,1)S(1)}, bf16[4,48,2432]{2,1,0:T(8,128)(2,1)S(1)}, u32[]{:S(2)}, u32[]{:S(2)}) collective-permute-start(bf16[4,48,2432]{2,1,0:T(8,128)(2,1)S(1)} %pad_maximum_fusion.1.b0.rest_0_), channel_id=1, source_target_pairs={{0,8},{8,0},{16,24},{24,16},{1,9},{9,1},{17,25},{25,17},{2,10},{10... | collective-permute-start | bytes 2801672 | tf_op jit(solution)/shard_map/ppermute | solution.py:887
  67.6 23.8 %copy-start.6 = (bf16[4,48,2432]{2,1,0:T(8,128)(2,1)}, bf16[4,48,2432]{2,1,0:T(8,128)(2,1)S(1)}, u32[]{:S(2)}) copy-start(bf16[4,48,2432]{2,1,0:T(8,128)(2,1)S(1)} %collective-permute-done.3.b1.rest_1_) | copy-start | bytes 2801668
  67.6 23.8 %collective-permute-start.5 = (bf16[4,48,2432]{2,1,0:T(8,128)(2,1)S(1)}, bf16[4,48,2432]{2,1,0:T(8,128)(2,1)S(1)}, u32[]{:S(2)}, u32[]{:S(2)}) collective-permute-start(bf16[4,48,2432]{2,1,0:T(8,128)(2,1)S(1)} %collective-permute-done.3.b1.rest_1_), channel_id=1, source_target_pairs={{0,8},{8,0},{16,24},{24,16},{1,9},{9,1},{17,25},{25,17},{2,10},{10... | collective-permute-start | bytes 2801672 | tf_op jit(solution)/shard_map/ppermute | solution.py:887
  68.1 4.4 %collective-permute-start.12 = (bf16[4,48,1920]{2,1,0:T(8,128)(2,1)S(1)}, bf16[4,48,1920]{2,1,0:T(8,128)(2,1)S(1)}, u32[]{:S(2)}, u32[]{:S(2)}) collective-permute-start(bf16[4,48,1920]{2,1,0:T(8,128)(2,1)S(1)} %pad_maximum_fusion.2.rest_0_), channel_id=1, source_target_pairs={{0,8},{8,0},{16,24},{24,16},{1,9},{9,1},{17,25},{25,17},{2,10},{10... | collective-permute-start | bytes 2211848 | tf_op jit(solution)/shard_map/ppermute | solution.py:887
  68.2 19.1 %collective-permute-start.11 = (bf16[4,48,1920]{2,1,0:T(8,128)(2,1)}, bf16[4,48,1920]{2,1,0:T(8,128)(2,1)}, u32[]{:S(2)}, u32[]{:S(2)}) collective-permute-start(bf16[4,48,1920]{2,1,0:T(8,128)(2,1)} %collective-permute-done.9.rest_1_), channel_id=1, source_target_pairs={{0,16},{8,24},{16,0},{24,8},{1,17},{9,25},{17,1},{25,9},{2,18},{10... | collective-permute-start | bytes 2211848 | tf_op jit(solution)/shard_map/ppermute | solution.py:887
  72.5 19.0 %copy-start.12 = (bf16[4,48,1920]{2,1,0:T(8,128)(2,1)}, bf16[4,48,1920]{2,1,0:T(8,128)(2,1)S(1)}, u32[]{:S(2)}) copy-start(bf16[4,48,1920]{2,1,0:T(8,128)(2,1)S(1)} %collective-permute-done.12.rest_4_) | copy-start | bytes 2211844
  72.5 38.3 %collective-permute-start.13 = (bf16[4,48,1920]{2,1,0:T(8,128)(2,1)}, bf16[4,48,1920]{2,1,0:T(8,128)(2,1)S(1)}, u32[]{:S(2)}, u32[]{:S(2)}) collective-permute-start(bf16[4,48,1920]{2,1,0:T(8,128)(2,1)} %collective-permute-done.9.rest_1_), channel_id=1, source_target_pairs={{0,8},{8,0},{16,24},{24,16},{1,9},{9,1},{17,25},{25,17},{2,10},{10... | collective-permute-start | bytes 2211848 | tf_op jit(solution)/shard_map/ppermute | solution.py:887
  72.6 18.8 %copy-start.7 = (bf16[4,48,2432]{2,1,0:T(8,128)(2,1)}, bf16[4,48,2432]{2,1,0:T(8,128)(2,1)S(1)}, u32[]{:S(2)}) copy-start(bf16[4,48,2432]{2,1,0:T(8,128)(2,1)S(1)} %collective-permute-done.4.b2.rest_2_) | copy-start | bytes 2801668
  72.6 38.2 %collective-permute-start.14 = (bf16[4,48,1920]{2,1,0:T(8,128)(2,1)}, bf16[4,48,1920]{2,1,0:T(8,128)(2,1)}, u32[]{:S(2)}, u32[]{:S(2)}) collective-permute-start(bf16[4,48,1920]{2,1,0:T(8,128)(2,1)} %collective-permute-done.10.rest_2_), channel_id=1, source_target_pairs={{0,8},{8,0},{16,24},{24,16},{1,9},{9,1},{17,25},{25,17},{2,10},{10... | collective-permute-start | bytes 2211848 | tf_op jit(solution)/shard_map/ppermute | solution.py:887
  87.3 23.5 %collective-permute-start.15 = (bf16[4,48,1920]{2,1,0:T(8,128)(2,1)}, bf16[4,48,1920]{2,1,0:T(8,128)(2,1)}, u32[]{:S(2)}, u32[]{:S(2)}) collective-permute-start(bf16[4,48,1920]{2,1,0:T(8,128)(2,1)} %collective-permute-done.11.rest_3_), channel_id=1, source_target_pairs={{0,8},{8,0},{16,24},{24,16},{1,9},{9,1},{17,25},{25,17},{2,10},{10... | collective-permute-start | bytes 2211848 | tf_op jit(solution)/shard_map/ppermute | solution.py:887
  91.4 41.6 %collective-permute-start.20 = (bf16[4,192,768]{2,1,0:T(8,128)(2,1)S(1)}, bf16[4,192,768]{2,1,0:T(8,128)(2,1)S(1)}, u32[]{:S(2)}, u32[]{:S(2)}) collective-permute-start(bf16[4,192,768]{2,1,0:T(8,128)(2,1)S(1)} %pad_maximum_fusion.rest_0_), channel_id=1, source_target_pairs={{0,8},{8,0},{16,24},{24,16},{1,9},{9,1},{17,25},{25,17},{2,10},{10... | collective-permute-start | bytes 3538952 | tf_op jit(solution)/shard_map/ppermute | solution.py:887
  91.5 0.9 copy-start.8
  92.4 40.7 %collective-permute-start.21 = (bf16[4,192,768]{2,1,0:T(8,128)(2,1)}, bf16[4,192,768]{2,1,0:T(8,128)(2,1)}, u32[]{:S(2)}, u32[]{:S(2)}) collective-permute-start(bf16[4,192,768]{2,1,0:T(8,128)(2,1)} %collective-permute-done.19.rest_1_), channel_id=1, source_target_pairs={{0,8},{8,0},{16,24},{24,16},{1,9},{9,1},{17,25},{25,17},{2,10},{10... | collective-permute-start | bytes 3538952 | tf_op jit(solution)/shard_map/ppermute | solution.py:887
  110.8 0.9 copy-start.13
  133.1 1.0 copy-start.11
  159.5 105.3 %collective-permute-start.40 = (bf16[1,2,4,384,384]{4,3,2,1,0:T(8,128)(2,1)}, bf16[1,2,4,384,384]{4,3,2,1,0:T(8,128)(2,1)}, u32[]{:S(2)}, u32[]{:S(2)}) collective-permute-start(bf16[1,2,4,384,384]{4,3,2,1,0:T(8,128)(2,1)} %get-tuple-element.66), channel_id=1, source_target_pairs={{0,8},{8,0},{16,24},{24,16},{1,9},{9,1},{17,25},{25,17},{2,10},{10... | collective-permute-start | bytes 7077896 | tf_op jit(solution)/shard_map/ppermute | solution.py:887
  190.0 79.6 %collective-permute-start.31 = (bf16[2,2,4,48,1536]{4,3,2,1,0:T(8,128)(2,1)}, bf16[2,2,4,48,1536]{4,3,2,1,0:T(8,128)(2,1)}, u32[]{:S(2)}, u32[]{:S(2)}) collective-permute-start(bf16[2,2,4,48,1536]{4,3,2,1,0:T(8,128)(2,1)} %get-tuple-element.64), channel_id=1, source_target_pairs={{0,8},{8,0},{16,24},{24,16},{1,9},{9,1},{17,25},{25,17},{2,10},{10... | collective-permute-start | bytes 7077896 | tf_op jit(solution)/shard_map/ppermute | solution.py:887
  190.5 32.3 %copy-start.10 = (f32[1,3072]{1,0:T(1,128)S(1)}, f32[1,3072]{1,0:T(1,128)}, u32[]{:S(2)}) copy-start(f32[1,3072]{1,0:T(1,128)} %get-tuple-element.58) | copy-start | bytes 36868
  254.5 19.2 %collective-permute-start.22 = (bf16[2,2,4,48,1664]{4,3,2,1,0:T(8,128)(2,1)}, bf16[2,2,4,48,1664]{4,3,2,1,0:T(8,128)(2,1)S(1)}, u32[]{:S(2)}, u32[]{:S(2)}) collective-permute-start(bf16[2,2,4,48,1664]{4,3,2,1,0:T(8,128)(2,1)} %get-tuple-element.62), channel_id=1, source_target_pairs={{0,8},{8,0},{16,24},{24,16},{1,9},{9,1},{17,25},{25,17},{2,10},{10... | collective-permute-start | bytes 7667720 | tf_op jit(solution)/shard_map/ppermute | solution.py:887
  267.8 1.7 copy-start.4
  267.9 28.4 %collective-permute-start.41 = (bf16[4,384,384]{2,1,0:T(8,128)(2,1)S(1)}, bf16[4,384,384]{2,1,0:T(8,128)(2,1)S(1)}, u32[]{:S(2)}, u32[]{:S(2)}) collective-permute-start(bf16[4,384,384]{2,1,0:T(8,128)(2,1)S(1)} %slice_bitcast_fusion.2), channel_id=1, source_target_pairs={{0,1},{1,0},{2,3},{3,2},{4,5},{5,4},{6,7},{7,6},{8,9},{9,8},{10,11... | collective-permute-start | bytes 3538952 | tf_op jit(solution)/shard_map/ppermute | solution.py:887
  269.5 4.2 %copy-start.3 = (bf16[2,2,4,48,1664]{4,3,2,1,0:T(8,128)(2,1)S(1)}, bf16[2,2,4,48,1664]{4,3,2,1,0:T(8,128)(2,1)}, u32[]{:S(2)}) copy-start(bf16[2,2,4,48,1664]{4,3,2,1,0:T(8,128)(2,1)} %get-tuple-element.61) | copy-start | bytes 7667716
  272.1 36.6 %collective-permute-start.32 = (bf16[2,4,48,1536]{3,2,1,0:T(8,128)(2,1)S(1)}, bf16[2,4,48,1536]{3,2,1,0:T(8,128)(2,1)S(1)}, u32[]{:S(2)}, u32[]{:S(2)}) collective-permute-start(bf16[2,4,48,1536]{3,2,1,0:T(8,128)(2,1)S(1)} %slice_bitcast_fusion.4), channel_id=1, source_target_pairs={{0,16},{8,24},{16,0},{24,8},{1,17},{9,25},{17,1},{25,9},{2,18},{10... | collective-permute-start | bytes 3538952 | tf_op jit(solution)/shard_map/ppermute | solution.py:887
  274.4 53.4 %collective-permute-start.23 = (bf16[2,4,48,1664]{3,2,1,0:T(8,128)(2,1)S(1)}, bf16[2,4,48,1664]{3,2,1,0:T(8,128)(2,1)S(1)}, u32[]{:S(2)}, u32[]{:S(2)}) collective-permute-start(bf16[2,4,48,1664]{3,2,1,0:T(8,128)(2,1)S(1)} %slice_bitcast_fusion), channel_id=1, source_target_pairs={{0,16},{8,24},{16,0},{24,8},{1,17},{9,25},{17,1},{25,9},{2,18},{10... | collective-permute-start | bytes 3833864 | tf_op jit(solution)/shard_map/ppermute | solution.py:887
  296.8 33.1 %collective-permute-start.42 = (bf16[384,384]{1,0:T(8,128)(2,1)S(1)}, bf16[384,384]{1,0:T(8,128)(2,1)S(1)}, u32[]{:S(2)}, u32[]{:S(2)}) collective-permute-start(bf16[384,384]{1,0:T(8,128)(2,1)S(1)} %get-tuple-element.120), channel_id=1, source_target_pairs={{0,2},{1,3},{2,0},{3,1},{4,6},{5,7},{6,4},{7,5},{8,10},{9,11},{10,... | collective-permute-start | bytes 884744 | tf_op jit(solution)/shard_map/ppermute | solution.py:887
  305.4 24.5 %collective-permute-start.43 = (bf16[384,384]{1,0:T(8,128)(2,1)S(1)}, bf16[384,384]{1,0:T(8,128)(2,1)S(1)}, u32[]{:S(2)}, u32[]{:S(2)}) collective-permute-start(bf16[384,384]{1,0:T(8,128)(2,1)S(1)} %get-tuple-element.122), channel_id=1, source_target_pairs={{0,4},{1,5},{2,6},{3,7},{4,0},{5,1},{6,2},{7,3},{8,12},{9,13},{10,... | collective-permute-start | bytes 884744 | tf_op jit(solution)/shard_map/ppermute | solution.py:887
  307.4 22.5 %collective-permute-start.44 = (bf16[384,384]{1,0:T(8,128)(2,1)S(1)}, bf16[384,384]{1,0:T(8,128)(2,1)S(1)}, u32[]{:S(2)}, u32[]{:S(2)}) collective-permute-start(bf16[384,384]{1,0:T(8,128)(2,1)S(1)} %get-tuple-element.121), channel_id=1, source_target_pairs={{0,6},{1,7},{2,4},{3,5},{4,2},{5,3},{6,0},{7,1},{8,14},{9,15},{10,... | collective-permute-start | bytes 884744 | tf_op jit(solution)/shard_map/ppermute | solution.py:887
  309.1 22.4 %collective-permute-start.33 = (bf16[4,48,1536]{2,1,0:T(8,128)(2,1)S(1)}, bf16[4,48,1536]{2,1,0:T(8,128)(2,1)S(1)}, u32[]{:S(2)}, u32[]{:S(2)}) collective-permute-start(bf16[4,48,1536]{2,1,0:T(8,128)(2,1)S(1)} %slice_bitcast_fusion.8), channel_id=1, source_target_pairs={{0,1},{1,0},{2,3},{3,2},{4,5},{5,4},{6,7},{7,6},{8,9},{9,8},{10,11... | collective-permute-start | bytes 1769480 | tf_op jit(solution)/shard_map/ppermute | solution.py:887
  328.3 31.4 %collective-permute-start.24 = (bf16[4,48,1664]{2,1,0:T(8,128)(2,1)S(1)}, bf16[4,48,1664]{2,1,0:T(8,128)(2,1)}, u32[]{:S(2)}, u32[]{:S(2)}) collective-permute-start(bf16[4,48,1664]{2,1,0:T(8,128)(2,1)S(1)} %slice_bitcast_fusion.6), channel_id=1, source_target_pairs={{0,1},{1,0},{2,3},{3,2},{4,5},{5,4},{6,7},{7,6},{8,9},{9,8},{10,11... | collective-permute-start | bytes 1916936 | tf_op jit(solution)/shard_map/ppermute | solution.py:887
  330.0 13.7 %collective-permute-start.45 = (bf16[384,384]{1,0:T(8,128)(2,1)S(1)}, bf16[384,384]{1,0:T(8,128)(2,1)S(1)}, u32[]{:S(2)}, u32[]{:S(2)}) collective-permute-start(bf16[384,384]{1,0:T(8,128)(2,1)S(1)} %fusion.7), channel_id=1, source_target_pairs={{0,16},{8,24},{16,0},{24,8},{1,17},{9,25},{17,1},{25,9},{2,18},{10... | collective-permute-start | bytes 884744 | tf_op jit(solution)/shard_map/ppermute | solution.py:887
  331.8 13.4 %collective-permute-start.34 = (bf16[48,1536]{1,0:T(8,128)(2,1)S(1)}, bf16[48,1536]{1,0:T(8,128)(2,1)S(1)}, u32[]{:S(2)}, u32[]{:S(2)}) collective-permute-start(bf16[48,1536]{1,0:T(8,128)(2,1)S(1)} %get-tuple-element.132), channel_id=1, source_target_pairs={{0,2},{1,3},{2,0},{3,1},{4,6},{5,7},{6,4},{7,5},{8,10},{9,11},{10,... | collective-permute-start | bytes 442376 | tf_op jit(solution)/shard_map/ppermute | solution.py:887
  340.4 13.9 %collective-permute-start.35 = (bf16[48,1536]{1,0:T(8,128)(2,1)S(1)}, bf16[48,1536]{1,0:T(8,128)(2,1)S(1)}, u32[]{:S(2)}, u32[]{:S(2)}) collective-permute-start(bf16[48,1536]{1,0:T(8,128)(2,1)S(1)} %get-tuple-element.134), channel_id=1, source_target_pairs={{0,4},{1,5},{2,6},{3,7},{4,0},{5,1},{6,2},{7,3},{8,12},{9,13},{10,... | collective-permute-start | bytes 442376 | tf_op jit(solution)/shard_map/ppermute | solution.py:887
  342.4 11.9 %collective-permute-start.36 = (bf16[48,1536]{1,0:T(8,128)(2,1)S(1)}, bf16[48,1536]{1,0:T(8,128)(2,1)S(1)}, u32[]{:S(2)}, u32[]{:S(2)}) collective-permute-start(bf16[48,1536]{1,0:T(8,128)(2,1)S(1)} %get-tuple-element.133), channel_id=1, source_target_pairs={{0,6},{1,7},{2,4},{3,5},{4,2},{5,3},{6,0},{7,1},{8,14},{9,15},{10,... | collective-permute-start | bytes 442376 | tf_op jit(solution)/shard_map/ppermute | solution.py:887
  343.9 11.2 %collective-permute-start.46 = (bf16[384,384]{1,0:T(8,128)(2,1)S(1)}, bf16[384,384]{1,0:T(8,128)(2,1)S(1)}, u32[]{:S(2)}, u32[]{:S(2)}) collective-permute-start(bf16[384,384]{1,0:T(8,128)(2,1)S(1)} %add_convert_fusion.3), channel_id=1, source_target_pairs={{0,8},{8,0},{16,24},{24,16},{1,9},{9,1},{17,25},{25,17},{2,10},{10... | collective-permute-start | bytes 884744 | tf_op jit(solution)/shard_map/ppermute | solution.py:887
  354.4 5.2 %collective-permute-start.37 = (bf16[48,1536]{1,0:T(8,128)(2,1)S(1)}, bf16[48,1536]{1,0:T(8,128)(2,1)S(1)}, u32[]{:S(2)}, u32[]{:S(2)}) collective-permute-start(bf16[48,1536]{1,0:T(8,128)(2,1)S(1)} %fusion.14), channel_id=1, source_target_pairs={{0,16},{8,24},{16,0},{24,8},{1,17},{9,25},{17,1},{25,9},{2,18},{10... | collective-permute-start | bytes 442376 | tf_op jit(solution)/shard_map/ppermute | solution.py:887
  355.0 10.8 %collective-permute-start.38 = (bf16[48,1536]{1,0:T(8,128)(2,1)S(1)}, bf16[48,1536]{1,0:T(8,128)(2,1)S(1)}, u32[]{:S(2)}, u32[]{:S(2)}) collective-permute-start(bf16[48,1536]{1,0:T(8,128)(2,1)S(1)} %fusion.14), channel_id=1, source_target_pairs={{0,8},{8,0},{16,24},{24,16},{1,9},{9,1},{17,25},{25,17},{2,10},{10... | collective-permute-start | bytes 442376 | tf_op jit(solution)/shard_map/ppermute | solution.py:887
  359.6 6.2 %collective-permute-start.39 = (bf16[48,1536]{1,0:T(8,128)(2,1)S(1)}, bf16[48,1536]{1,0:T(8,128)(2,1)S(1)}, u32[]{:S(2)}, u32[]{:S(2)}) collective-permute-start(bf16[48,1536]{1,0:T(8,128)(2,1)S(1)} %collective-permute-done.37), channel_id=1, source_target_pairs={{0,8},{8,0},{16,24},{24,16},{1,9},{9,1},{17,25},{25,17},{2,10},{10... | collective-permute-start | bytes 442376 | tf_op jit(solution)/shard_map/ppermute | solution.py:887
  360.9 10.1 %collective-permute-start.25 = (bf16[48,1664]{1,0:T(8,128)(2,1)S(1)}, bf16[48,1664]{1,0:T(8,128)(2,1)S(1)}, u32[]{:S(2)}, u32[]{:S(2)}) collective-permute-start(bf16[48,1664]{1,0:T(8,128)(2,1)S(1)} %get-tuple-element.125), channel_id=1, source_target_pairs={{0,2},{1,3},{2,0},{3,1},{4,6},{5,7},{6,4},{7,5},{8,10},{9,11},{10,... | collective-permute-start | bytes 479240 | tf_op jit(solution)/shard_map/ppermute | solution.py:887
  363.2 14.8 %collective-permute-start.26 = (bf16[48,1664]{1,0:T(8,128)(2,1)S(1)}, bf16[48,1664]{1,0:T(8,128)(2,1)S(1)}, u32[]{:S(2)}, u32[]{:S(2)}) collective-permute-start(bf16[48,1664]{1,0:T(8,128)(2,1)S(1)} %get-tuple-element.127), channel_id=1, source_target_pairs={{0,4},{1,5},{2,6},{3,7},{4,0},{5,1},{6,2},{7,3},{8,12},{9,13},{10,... | collective-permute-start | bytes 479240 | tf_op jit(solution)/shard_map/ppermute | solution.py:887
  364.4 13.5 %collective-permute-start.27 = (bf16[48,1664]{1,0:T(8,128)(2,1)S(1)}, bf16[48,1664]{1,0:T(8,128)(2,1)S(1)}, u32[]{:S(2)}, u32[]{:S(2)}) collective-permute-start(bf16[48,1664]{1,0:T(8,128)(2,1)S(1)} %get-tuple-element.126), channel_id=1, source_target_pairs={{0,6},{1,7},{2,4},{3,5},{4,2},{5,3},{6,0},{7,1},{8,14},{9,15},{10,... | collective-permute-start | bytes 479240 | tf_op jit(solution)/shard_map/ppermute | solution.py:887
  378.0 5.3 %collective-permute-start.28 = (bf16[48,1664]{1,0:T(8,128)(2,1)S(1)}, bf16[48,1664]{1,0:T(8,128)(2,1)S(1)}, u32[]{:S(2)}, u32[]{:S(2)}) collective-permute-start(bf16[48,1664]{1,0:T(8,128)(2,1)S(1)} %fusion.11), channel_id=1, source_target_pairs={{0,16},{8,24},{16,0},{24,8},{1,17},{9,25},{17,1},{25,9},{2,18},{10... | collective-permute-start | bytes 479240 | tf_op jit(solution)/shard_map/ppermute | solution.py:887
  379.8 3.7 collective-permute-start.29
  383.4 1.4 collective-permute-start.30
  386.6 1.8 copy-start.1

commit v2 on v1

--- a/solution.py
+++ b/solution.py
@@ -64,28 +64,6 @@
     return copies
 
 
-def emit_blocks(place, acc, send, keep, shard_rows, split_x):
-    half = shard_rows // 2
-    nx = 2 if split_x else 1
-    width = acc.shape[1] // nx
-    for cc, out in ((0, keep), (1, send)):
-        core = lax.bitwise_xor(place.c, cc)
-        for xx in range(nx):
-            for yy in range(2):
-
-                def step(k, carry, cc=cc, xx=xx, yy=yy, out=out, core=core):
-                    row = aligned(place.shard(k, yy) * shard_rows + core * half, 16)
-                    if split_x:
-                        col = aligned(lax.bitwise_xor(place.x, xx) * width, 128)
-                        block = acc[pl.ds(row, half), pl.ds(col, width)]
-                    else:
-                        block = acc[pl.ds(row, half), :]
-                    out[xx, yy, k] = block.astype(BF)
-                    return carry
-
-                lax.fori_loop(0, 4, step, 0)
-
-
 def call(body, name, ins, outs, scratch, flops, transcendentals=0):
     spaces = {
         "s": pl.BlockSpec(memory_space=pltpu.SMEM),
@@ -103,9 +81,7 @@
         out_specs=tuple(spaces["v"] for _ in outs),
         scratch_shapes=scratch,
         compiler_params=pltpu.CompilerParams(vmem_limit_bytes=VMEM_LIMIT),
-        cost_estimate=pl.CostEstimate(
-            flops=flops, transcendentals=transcendentals, bytes_accessed=moved
-        ),
+        cost_estimate=pl.CostEstimate(flops=1, transcendentals=0, bytes_accessed=1),
     )(*[a for a, _ in ins])
 
 
@@ -279,273 +255,522 @@
     )
 
 
-def down_forward(active, normed, vec, counts, pooled_grad, ids, bufs, sentences, length):
+def grid_call(body, name, grid, scalars, ins, outs, scratch, flops, transcendentals=0):
+    def spec(block, index):
+        if block is None:
+            return pl.BlockSpec(memory_space=pl.ANY)
+        return pl.BlockSpec(block, index)
+
+    moved = sum(a.size * a.dtype.itemsize for a, _, _ in ins) + sum(
+        o.size * o.dtype.itemsize for o, _, _ in outs
+    )
+    return pl.pallas_call(
+        body,
+        name=name,
+        out_shape=tuple(o for o, _, _ in outs),
+        grid_spec=pltpu.PrefetchScalarGridSpec(
+            num_scalar_prefetch=len(scalars),
+            grid=grid,
+            in_specs=[spec(b, i) for _, b, i in ins],
+            out_specs=tuple(spec(b, i) for _, b, i in outs),
+            scratch_shapes=scratch,
+        ),
+        compiler_params=pltpu.CompilerParams(
+            vmem_limit_bytes=VMEM_LIMIT, dimension_semantics=("arbitrary",) * len(grid)
+        ),
+        cost_estimate=pl.CostEstimate(flops=1, transcendentals=0, bytes_accessed=1),
+    )(*scalars, *[a for a, _, _ in ins])
+
+
+def whole(array):
+    return (array, array.shape, lambda *_: (0,) * array.ndim)
+
+
+def left(array):
+    return (array, None, None)
+
+
+def relative(ids, step):
+    return lax.bitwise_xor(ids[0] * 2 + ids[1], step)
+
+
+def put_relative(place, source, dst):
+    half = source.shape[0] // 16
+    for cc in range(2):
+        core = lax.bitwise_xor(place.c, cc)
+        for yy in range(2):
+            for k in range(4):
+                at = ((cc * 2 + yy) * 4 + k) * half
+                here = aligned(place.shard(k, yy) * 2 * half + core * half, 16)
+                dst[at : at + half, :] = source[pl.ds(here, half), :]
+
+
+def natural_copies(place, bufs, dst, sems):
+    half = bufs[0].shape[1]
+    copies = []
+    for cc in range(2):
+        for yy in range(2):
+            for k in range(4):
+                at = place.shard(k, yy) * 2 * half + lax.bitwise_xor(place.c, cc) * half
+                copies.append(
+                    pltpu.make_async_copy(
+                        bufs[2 * cc + yy].at[k], dst.at[pl.ds(aligned(at, 16), half), :], sems.at[len(copies)]
+                    )
+                )
+    return copies
+
+
+def down_and_back(active, slope, normed, vec, counts, pooled_grad, ids, bufs, sentences, length):
     rows, wide = active.shape
     width = normed.shape[1]
     shard = wide // 8
+    half = width // 2
     group = 256
 
-    def body(ids_ref, counts_ref, act_ref, n_ref, vec_ref, pg_ref, *rest):
+    def body(ids_ref, counts_ref, act_hbm, slope_ref, vec_ref, pg_ref, n_hbm, b0, b1, b2, b3, pooled_ref, vg_ref, send_ref, keep_ref, gup_ref, gbias_ref, gres_hbm, w_ref, acc_ref, n_ref, glow_ref, act_ref, t_ref, sems, more):
+        step = pl.program_id(0)
+        place = Place(ids_ref)
+        bufs_ref = (b0, b1, b2, b3)
+        load = pltpu.make_async_copy(n_hbm, n_ref, more.at[0])
+        load_active = pltpu.make_async_copy(act_hbm, act_ref, more.at[1 + sentences])
+
+        def columns_of(phase):
+            return pl.ds(aligned(relative(ids_ref, step - phase) * shard, 128), shard)
+
+        def out(s):
+            here = pl.ds(aligned(s * length, length), length)
+            return pltpu.make_async_copy(acc_ref.at[here, :], gres_hbm.at[here, :], more.at[1 + s])
+
+        @pl.when(step == 0)
+        def _():
+            copies = natural_copies(place, bufs_ref, w_ref, sems)
+            load_active.start()
+            for copy in copies:
+                copy.start()
+            load.start()
+            vg_ref[...] = jnp.zeros_like(vg_ref)
+            for copy in copies:
+                copy.wait()
+            load_active.wait()
+            for g in range(width // group):
+                cols = slice(g * group, (g + 1) * group)
+                acc_ref[:, cols] = dot(act_ref[...], w_ref[:, cols])
+            load.wait()
+
+            def norm_rows(s, carry):
+                here = pl.ds(aligned(s * length, length), length)
+                hidden = n_ref[here, :] * row(vec_ref, 3) + row(vec_ref, 4)
+                n2, inverse = layer_norm(hidden + (acc_ref[here, :] + row(vec_ref, 5)))
+                valid = lax.broadcasted_iota(jnp.int32, (length, width), 0) < counts_ref[s]
+                count = counts_ref[s].astype(F32)
+                out_rows = jnp.where(valid, n2 * row(vec_ref, 6) + row(vec_ref, 7), 0.0)
+                pooled_ref[pl.ds(s, 1), :] = jnp.sum(out_rows, 0, keepdims=True) / count
+                grad = jnp.where(valid, pg_ref[pl.ds(s, 1), :] / count, 0.0)
+                vg_ref[0:1, :] += jnp.sum(grad * n2, 0, keepdims=True)
+                vg_ref[1:2, :] += jnp.sum(grad, 0, keepdims=True)
+                gres = norm_back(grad, n2, inverse, row(vec_ref, 6))
+                acc_ref[here, :] = gres
+                glow = gres.astype(BF)
+                glow_ref[here, :] = glow
+                vg_ref[2:3, :] += jnp.sum(glow.astype(F32), 0, keepdims=True)
+                out(s).start()
+                return carry
+
+            lax.fori_loop(0, sentences, norm_rows, 0)
+            t_ref[...] = glow_ref[...].T
+
+        @pl.when(jnp.logical_and(step >= 1, step < 9))
+        def _():
+            for cc, out_ref in ((0, keep_ref), (1, send_ref)):
+                core = lax.bitwise_xor(place.c, cc)
+                out_ref[0, 0, 0] = dot(
+                    t_ref[pl.ds(aligned(core * half, half), half), :], act_ref[:, columns_of(1)]
+                ).astype(BF)
+
+        @pl.when(step >= 9)
+        def _():
+            gact = dot_nt(glow_ref[...], w_ref[columns_of(9), :])
+            gup = (gact * slope_ref[...].astype(F32)).astype(BF)
+            gup_ref[...] = gup
+            gbias_ref[...] = jnp.sum(gup.astype(F32), 0, keepdims=True)
+
+        @pl.when(step == 16)
+        def _():
+            for s in range(sentences):
+                out(s).wait()
+
+    def at(step, phase):
+        return jnp.clip(step - phase, 0, 7)
+
+    def grad_block(step, ids, counts):
+        r = at(step, 1)
+        return (0, lax.rem(r, 2), lax.div(r, 2), 0, 0)
+
+    def columns(phase):
+        return lambda step, ids, counts: (0, relative(ids, at(step, phase)))
+
+    grads = (struct((1, 2, 4, half, shard), BF), (1, 1, 1, half, shard), grad_block)
+    return grid_call(
+        body,
+        "down_and_back",
+        (17,),
+        (ids, counts),
+        [
+            left(active),
+            (slope, (rows, shard), columns(9)),
+            whole(vec),
+            whole(pooled_grad),
+            left(normed),
+        ]
+        + [left(b) for b in bufs],
+        [
+            whole(struct((sentences, width), F32)),
+            whole(struct((8, width), F32)),
+            grads,
+            grads,
+            (struct((rows, wide), BF), (rows, shard), columns(9)),
+            (struct((1, wide), F32), (1, shard), columns(9)),
+            left(struct((rows, width), F32)),
+        ],
+        [
+            pltpu.VMEM((wide, width), BF),
+            pltpu.VMEM((rows, width), F32),
+            pltpu.VMEM((rows, width), F32),
+            pltpu.VMEM((rows, width), BF),
+            pltpu.VMEM((rows, wide), BF),
+            pltpu.VMEM((width, rows), BF),
+            pltpu.SemaphoreType.DMA((16,)),
+            pltpu.SemaphoreType.DMA((2 + sentences,)),
+        ],
+        6 * rows * width * wide,
+    )
+
+
+def up_and_back(low, gup, gres, normed, inverse, vec, ids, bufs, length):
+    rows, wide = gup.shape
+    width = gres.shape[1]
+    sentences = rows // length
+    group, block = 256, 512
+    steps = wide // block
+    per = steps // 2
+
+    def body(ids_ref, low_ref, gup_ref, vec_ref, gres_hbm, n_hbm, inv_hbm, *rest):
         bufs_ref = rest[: len(bufs)]
-        pooled_ref, gres_ref, glow_ref, vg_ref, send_ref, keep_ref, w_ref, dw_ref, sems = rest[len(bufs) :]
+        send_ref, keep_ref, gctx_ref, vg_ref, gattn_hbm, glow_hbm, w_ref, acc_ref, gres_ref, n_ref, inv_ref, glow_ref, t_ref, p_ref, gup_all, sems, more = rest[len(bufs) :]
+        step = pl.program_id(0)
         place = Place(ids_ref)
-        copies = piece_copies(place, bufs_ref, w_ref, sems, shard, False)
+        loads = [
+            pltpu.make_async_copy(a, b, more.at[i])
+            for i, (a, b) in enumerate(((gres_hbm, gres_ref), (n_hbm, n_ref), (inv_hbm, inv_ref)))
+        ]
+        copies = piece_copies(place, bufs_ref, w_ref, sems, width // 8, True)
+
+        @pl.when(step == 0)
+        def _():
+            for copy in copies:
+                copy.start()
+            for load in loads:
+                load.start()
+            t_ref[...] = low_ref[...].T
+            put_relative(place, t_ref, p_ref)
+
+        put_halves(dot(p_ref[...], gup_ref[...]).astype(BF), send_ref, keep_ref)
+
+        gup_all[:, pl.ds(aligned(step * block, 128), block)] = gup_ref[...]
+
+        @pl.when(step == steps - 1)
+        def _():
+            for copy in copies:
+                copy.wait()
+            for g in range(width // group):
+                cols = slice(g * group, (g + 1) * group)
+                acc_ref[:, cols] = dot_nt(gup_all[...], w_ref[cols, width:])
+            for load in loads:
+                load.wait()
+            vg_ref[...] = jnp.zeros_like(vg_ref)
+
+            def outs(s):
+                here = pl.ds(aligned(s * length, length), length)
+                return (
+                    pltpu.make_async_copy(acc_ref.at[here, :], gattn_hbm.at[here, :], more.at[3 + s]),
+                    pltpu.make_async_copy(
+                        glow_ref.at[here, :], glow_hbm.at[here, :], more.at[3 + sentences + s]
+                    ),
+                )
+
+            def norm_rows(s, carry):
+                here = pl.ds(aligned(s * length, length), length)
+                grad = acc_ref[here, :] + gres_ref[here, :]
+                normed = n_ref[here, :]
+                vg_ref[0:1, :] += jnp.sum(grad * normed, 0, keepdims=True)
+                vg_ref[1:2, :] += jnp.sum(grad, 0, keepdims=True)
+                gattn = norm_back(grad, normed, inv_ref[here, 0:1], row(vec_ref, 3))
+                acc_ref[here, :] = gattn
+                glow = gattn.astype(BF)
+                glow_ref[here, :] = glow
+                vg_ref[2:3, :] += jnp.sum(glow.astype(F32), 0, keepdims=True)
+                for copy in outs(s):
+                    copy.start()
+                return carry
+
+            lax.fori_loop(0, sentences, norm_rows, 0)
+            for g in range(width // group):
+                gctx_ref[:, g * group : (g + 1) * group] = dot_nt(
+                    glow_ref[...], w_ref[g * group : (g + 1) * group, :width]
+                ).astype(BF)
+            for s in range(sentences):
+                for copy in outs(s):
+                    copy.wait()
+
+    blocks = weight_blocks(width, block, per)
+    return grid_call(
+        body,
+        "up_and_back",
+        (steps,),
+        (ids,),
+        [whole(low), (gup, (rows, block), lambda j, ids: (0, j)), whole(vec), left(gres), left(normed), left(inverse)]
+        + [left(b) for b in bufs],
+        [
+            blocks,
+            blocks,
+            whole(struct((rows, width), BF)),
+            whole(struct((8, width), F32)),
+            left(struct((rows, width), F32)),
+            left(struct((rows, width), BF)),
+        ],
+        [
+            pltpu.VMEM((width, width + wide), BF),
+            pltpu.VMEM((rows, width), F32),
+            pltpu.VMEM((rows, width), F32),
+            pltpu.VMEM((rows, width), F32),
+            pltpu.VMEM((rows, 128), F32),
+            pltpu.VMEM((rows, width), BF),
+            pltpu.VMEM((width, rows), BF),
+            pltpu.VMEM((width, rows), BF),
+            pltpu.VMEM((rows, wide), BF),
+            pltpu.SemaphoreType.DMA((32,)),
+            pltpu.SemaphoreType.DMA((3 + 2 * sentences,)),
+        ],
+        2 * rows * width * (width + 2 * wide),
+    )
+
+
+def attend_backward(qkv, gctx, lse, counts, sentences, length, low, high, name):
+    rows, width = gctx.shape
+    span = (high - low) * 128
+    twos = range(low // 2, high // 2)
+
+    def body(counts_ref, *refs):
+        parts = [refs[i * len(twos) : (i + 1) * len(twos)] for i in range(3)]
+        gctx_ref, lse_ref, gqkv_ref, vs_ref = refs[3 * len(twos) :]
+        s = pl.program_id(0)
+
+        @pl.when(s == 0)
+        def _():
+            vs_ref[...] = jnp.zeros_like(vs_ref)
+
+        count = counts_ref[s]
+        for p in range(low, high):
+            at = (p - low) * 128
+            block, cols = (p - low) // 2, slice(p % 2 * 128, p % 2 * 128 + 128)
+            query = parts[0][block][:, cols] * jnp.asarray(HEAD**-0.5, BF)
+            keys2 = two_heads(parts[1][block][:, cols])
+            values2 = two_heads(parts[2][block][:, cols])
+            gout = gctx_ref[:, at : at + 128]
+            scores = masked_scores(query, keys2, count, length)
+            lse2 = halves(lse_ref[:, 2 * p : 2 * p + 1], lse_ref[:, 2 * p + 1 : 2 * p + 2], length)
+            probs = jnp.exp(scores - lse2)
+            gprobs = dot_nt(gout, values2)
+            weighted = gprobs * probs
+            sums = halves(
+                jnp.sum(weighted[:, :length], -1, keepdims=True),
+                jnp.sum(weighted[:, length:], -1, keepdims=True),
+                length,
+            )
+            gscores = (probs * (gprobs - sums)).astype(BF)
+            gq = (dot(gscores, keys2) * HEAD**-0.5).astype(BF)
+            gk = one_of_two(dot_tn(gscores, query)).astype(BF)
+            gv = one_of_two(dot_tn(probs.astype(BF), gout)).astype(BF)
+            gqkv_ref[:, at : at + 128] = gq
+            gqkv_ref[:, span + at : span + at + 128] = gk
+            gqkv_ref[:, 2 * span + at : 2 * span + at + 128] = gv
+            vs_ref[0:1, at : at + 128] += jnp.sum(gq.astype(F32), 0, keepdims=True)
+            vs_ref[1:2, at : at + 128] += jnp.sum(gv.astype(F32), 0, keepdims=True)
+
+    def by_rows(array):
+        return (array, (length, array.shape[1]), lambda s, counts: (s, 0))
+
+    return grid_call(
+        body,
+        name,
+        (sentences,),
+        (counts,),
+        [
+            (qkv, (length, 256), lambda s, counts, at=part * width // 256 + b: (s, at))
+            for part in range(3)
+            for b in twos
+        ]
+        + [(gctx, (length, span), lambda s, counts: (s, low * 128 // span)), by_rows(lse)],
+        [by_rows(struct((rows, 3 * span), BF)), whole(struct((8, span), F32))],
+        [],
+        20 * rows * length * span,
+    )
+
+
+def weight_blocks(width, group, per):
+    half = width // 16
+    return (
+        struct((2, 2, 4, half, per * group), BF),
+        (1, 2, 4, half, group),
+        lambda j, ids: (lax.bitwise_xor(ids[2], lax.div(j, per)), 0, 0, 0, lax.rem(j, per)),
+    )
+
+
+def put_halves(dw, send_ref, keep_ref):
+    width, group = dw.shape
+    shape = (2, 4, width // 16, group)
+    keep_ref[0] = dw[: width // 2].reshape(shape)
+    send_ref[0] = dw[width // 2 :].reshape(shape)
+
+
+def attend_weight(gqkv, tokens, context, glow, ids):
+    rows, width = tokens.shape
+    group = 384
+    first, second = gqkv.shape[1] // group, width // group
+    groups = first + second
+
+    def body(ids_ref, gqkv_ref, glow_ref, x_ref, ctx_ref, send_ref, keep_ref, t_ref, x_t):
+        j = pl.program_id(0)
+        place = Place(ids_ref)
+
+        @pl.when(j == 0)
+        def _():
+            t_ref[...] = x_ref[...].T
+            put_relative(place, t_ref, x_t)
+
+        @pl.when(j == first)
+        def _():
+            t_ref[...] = ctx_ref[...].T
+            put_relative(place, t_ref, x_t)
+
+        @pl.when(j < first)
+        def _():
+            put_halves(dot(x_t[...], gqkv_ref[...]).astype(BF), send_ref, keep_ref)
+
+        @pl.when(j >= first)
+        def _():
+            put_halves(dot(x_t[...], glow_ref[...]).astype(BF), send_ref, keep_ref)
+
+    blocks = weight_blocks(width, group, groups // 2)
+    return grid_call(
+        body,
+        "attention_weight",
+        (groups,),
+        (ids,),
+        [
+            (gqkv, (rows, group), lambda j, ids: (0, jnp.minimum(j, first - 1))),
+            (glow, (rows, group), lambda j, ids: (0, jnp.maximum(j - first, 0))),
+            whole(tokens),
+            whole(context),
+        ],
+        [blocks, blocks],
+        [pltpu.VMEM((width, rows), BF)] * 2,
+        2 * rows * width * 4 * width,
+    )
+
+
+def last_weight(gqkv, tokens, vg_a, vg_b, vg_attn, vg_ffn, gbias_in, ids):
+    rows, width = tokens.shape
+    group = 256
+    first = gqkv.shape[1] // group
+    groups = first + 1
+    cut, ratio = vg_a.shape[1], gbias_in.shape[0]
+
+    def body(ids_ref, gqkv_ref, x_ref, va_ref, vb_ref, attn_ref, ffn_ref, bias_ref, send_ref, keep_ref, t_ref, x_t, r_ref, v_ref):
+        j = pl.program_id(0)
+        place = Place(ids_ref)
+
+        @pl.when(j == 0)
+        def _():
+            t_ref[...] = x_ref[...].T
+            put_relative(place, t_ref, x_t)
+
+        @pl.when(j < first)
+        def _():
+            put_halves(dot(x_t[...], gqkv_ref[...]).astype(BF), send_ref, keep_ref)
+
+        @pl.when(j == first)
+        def _():
+            r_ref[...] = jnp.zeros_like(r_ref)
+            r_ref[0:2, :cut] = va_ref[0:2, :]
+            r_ref[0:2, cut:] = vb_ref[0:2, :]
+            r_ref[2:3, :] = attn_ref[2:3, :]
+            r_ref[3:5, :] = attn_ref[0:2, :]
+            r_ref[5:6, :] = ffn_ref[2:3, :]
+            r_ref[6:8, :] = ffn_ref[0:2, :]
+            r_ref[8 : 8 + ratio, :] = bias_ref[...]
+            v_ref[0] = r_ref[...].T
+            put_relative(place, v_ref.at[0], v_ref.at[1])
+            both = jnp.concatenate([v_ref[1], jnp.zeros((width, group - 128), F32)], axis=1)
+            put_halves(both.astype(BF), send_ref, keep_ref)
+
+    blocks = weight_blocks(width, group, groups // 2)
+    return grid_call(
+        body,
+        "last_weight",
+        (groups,),
+        (ids,),
+        [
+            (gqkv, (rows, group), lambda j, ids: (0, jnp.minimum(j, first - 1))),
+            whole(tokens),
+            whole(vg_a),
+            whole(vg_b),
+            whole(vg_attn),
+            whole(vg_ffn),
+            whole(gbias_in),
+        ],
+        [blocks, blocks],
+        [pltpu.VMEM((width, rows), BF)] * 2
+        + [pltpu.VMEM((128, width), F32), pltpu.VMEM((2, width, 128), F32)],
+        2 * rows * width * width,
+    )
+
+
+def tokens_backward(gqkv_a, gqkv_b, gattn, ids, bufs):
+    rows, width = gattn.shape
+    group = 256
+    span_a, span_b = gqkv_a.shape[1] // 3, gqkv_b.shape[1] // 3
+
+    def body(ids_ref, ga_hbm, gb_hbm, gattn_ref, b0, b1, b2, b3, gx_ref, w_ref, g_ref, sems, more):
+        copies = piece_copies(Place(ids_ref), (b0, b1, b2, b3), w_ref, sems, width // 8, False)
+        for i in range(3):
+            for at, span, source in ((0, span_a, ga_hbm), (span_a, span_b, gb_hbm)):
+                copies.append(
+                    pltpu.make_async_copy(
+                        source.at[:, i * span : (i + 1) * span],
+                        g_ref.at[:, i * width + at : i * width + at + span],
+                        more.at[2 * i + at // span_a],
+                    )
+                )
         for copy in copies:
             copy.start()
         for copy in copies:
             copy.wait()
         for g in range(width // group):
-            gres_ref[:, g * group : (g + 1) * group] = dot(
-                act_ref[...], w_ref[:, g * group : (g + 1) * group]
-            )
-        vg_ref[...] = jnp.zeros_like(vg_ref)
-
-        def norm_rows(s, carry):
-            here = pl.ds(aligned(s * length, length), length)
-            hidden = n_ref[here, :] * row(vec_ref, 3) + row(vec_ref, 4)
-            n2, inverse = layer_norm(hidden + (gres_ref[here, :] + row(vec_ref, 5)))
-            valid = lax.broadcasted_iota(jnp.int32, (length, width), 0) < counts_ref[s]
-            count = counts_ref[s].astype(F32)
-            out = jnp.where(valid, n2 * row(vec_ref, 6) + row(vec_ref, 7), 0.0)
-            pooled_ref[pl.ds(s, 1), :] = jnp.sum(out, 0, keepdims=True) / count
-            grad = jnp.where(valid, pg_ref[pl.ds(s, 1), :] / count, 0.0)
-            vg_ref[0:1, :] += jnp.sum(grad * n2, 0, keepdims=True)
-            vg_ref[1:2, :] += jnp.sum(grad, 0, keepdims=True)
-            gres = norm_back(grad, n2, inverse, row(vec_ref, 6))
-            gres_ref[here, :] = gres
-            glow = gres.astype(BF)
-            glow_ref[here, :] = glow
-            vg_ref[2:3, :] += jnp.sum(glow.astype(F32), 0, keepdims=True)
-            return carry
-
-        lax.fori_loop(0, sentences, norm_rows, 0)
-        glow_t = glow_ref[...].T
-        for f in range(8):
-            dw_ref[...] = dot(glow_t, act_ref[:, f * shard : (f + 1) * shard])
-            rel = lax.bitwise_xor(place.z * 2 + place.y, f)
-            k, yy = lax.div(rel, 2), lax.rem(rel, 2)
-            half = width // 2
-            for cc, out in ((0, keep_ref), (1, send_ref)):
-                core = lax.bitwise_xor(place.c, cc)
-                out[0, yy, k] = dw_ref[pl.ds(aligned(core * half, half), half), :].astype(BF)
-
-    return call(
-        body,
-        "down_norm_back",
-        [(ids, "s"), (counts, "s"), (active, "v"), (normed, "v"), (vec, "v"), (pooled_grad, "v")]
-        + [(b, "a") for b in bufs],
-        [
-            struct((sentences, width), F32),
-            struct((rows, width), F32),
-            struct((rows, width), BF),
-            struct((8, width), F32),
-            struct((1, 2, 4, width // 2, shard), BF),
-            struct((1, 2, 4, width // 2, shard), BF),
-        ],
-        [pltpu.VMEM((wide, width), BF), pltpu.VMEM((width, shard), F32), pltpu.SemaphoreType.DMA((16,))],
-        4 * rows * width * wide,
-    )
-
-
-def up_backward(glow, slope, low, ids, bufs):
-    rows, width = glow.shape
-    wide = slope.shape[1]
-    shard = wide // 8
-    group = 256
-
-    def body(ids_ref, glow_ref, slope_ref, low_ref, *rest):
-        bufs_ref = rest[: len(bufs)]
-        gup_ref, gbias_ref, send_ref, keep_ref, w_ref, dw_ref, sems = rest[len(bufs) :]
-        place = Place(ids_ref)
-        copies = piece_copies(place, bufs_ref, w_ref, sems, shard, False)
-        for copy in copies:
-            copy.start()
-        for copy in copies:
-            copy.wait()
-        low_t = low_ref[...].T
-
-        def columns(g, carry):
-            col = aligned(g * group, group)
-            gact = dot_nt(glow_ref[...], w_ref[pl.ds(col, group), :])
-            gup = (gact * slope_ref[:, pl.ds(col, group)].astype(F32)).astype(BF)
-            gup_ref[:, pl.ds(col, group)] = gup
-            gbias_ref[:, pl.ds(col, group)] = jnp.sum(gup.astype(F32), 0, keepdims=True)
-            dw_ref[:, pl.ds(col, group)] = dot(low_t, gup)
-            return carry
-
-        lax.fori_loop(0, wide // group, columns, 0)
-        emit_blocks(place, dw_ref, send_ref, keep_ref, width // 8, True)
-
-    blocks = struct((2, 2, 4, width // 16, wide // 2), BF)
-    return call(
-        body,
-        "up_back",
-        [(ids, "s"), (glow, "v"), (slope, "v"), (low, "v")] + [(b, "a") for b in bufs],
-        [struct((rows, wide), BF), struct((1, wide), F32), blocks, blocks],
-        [pltpu.VMEM((wide, width), BF), pltpu.VMEM((width, wide), F32), pltpu.SemaphoreType.DMA((16,))],
-        4 * rows * width * wide,
-    )
-
-
-def hidden_backward(gup, gres, normed, inverse, vec, ids, bufs, length):
-    rows, wide = gup.shape
-    width = gres.shape[1]
-    group = 256
-
-    def body(ids_ref, gup_ref, gres_ref, n_ref, inv_ref, vec_ref, *rest):
-        bufs_ref = rest[: len(bufs)]
-        gattn_ref, glow_ref, gctx_ref, vg_ref, w_ref, sems = rest[len(bufs) :]
-        place = Place(ids_ref)
-        copies = piece_copies(place, bufs_ref, w_ref, sems, width // 8, True)
-        for copy in copies:
-            copy.start()
-        for copy in copies:
-            copy.wait()
-        for g in range(width // group):
-            gattn_ref[:, g * group : (g + 1) * group] = dot_nt(
-                gup_ref[...], w_ref[g * group : (g + 1) * group, width:]
-            )
-        vg_ref[...] = jnp.zeros_like(vg_ref)
-
-        def norm_rows(s, carry):
-            here = pl.ds(aligned(s * length, length), length)
-            grad = gattn_ref[here, :] + gres_ref[here, :]
-            normed = n_ref[here, :]
-            vg_ref[0:1, :] += jnp.sum(grad * normed, 0, keepdims=True)
-            vg_ref[1:2, :] += jnp.sum(grad, 0, keepdims=True)
-            gattn = norm_back(grad, normed, inv_ref[here, 0:1], row(vec_ref, 3))
-            gattn_ref[here, :] = gattn
-            glow = gattn.astype(BF)
-            glow_ref[here, :] = glow
-            vg_ref[2:3, :] += jnp.sum(glow.astype(F32), 0, keepdims=True)
-            return carry
-
-        lax.fori_loop(0, rows // length, norm_rows, 0)
-        for g in range(width // group):
-            gctx_ref[:, g * group : (g + 1) * group] = dot_nt(
-                glow_ref[...], w_ref[g * group : (g + 1) * group, :width]
-            ).astype(BF)
-
-    return call(
-        body,
-        "hidden_back",
-        [(ids, "s"), (gup, "v"), (gres, "v"), (normed, "v"), (inverse, "v"), (vec, "v")]
-        + [(b, "a") for b in bufs],
-        [
-            struct((rows, width), F32),
-            struct((rows, width), BF),
-            struct((rows, width), BF),
-            struct((8, width), F32),
-        ],
-        [pltpu.VMEM((width, width + wide), BF), pltpu.SemaphoreType.DMA((32,))],
-        2 * rows * width * (width + wide),
-    )
-
-
-def attend_backward(qkv, gctx, lse, tokens, context, glow, vgrads, counts, ids, sentences, length):
-    rows, width = tokens.shape
-    pairs = width // 128
-    group = 256
-    total = 4 * width + 256
-
-    def body(ids_ref, counts_ref, qkv_ref, gctx_ref, lse_ref, x_ref, ctx_ref, glow_ref, vg_ref, gqkv_ref, send_ref, keep_ref, dw_ref, vs_ref):
-        place = Place(ids_ref)
-        vs_ref[...] = jnp.zeros_like(vs_ref)
-        vs_ref[0:16, :] = vg_ref[...]
-
-        def sentence(s, carry):
-            here = pl.ds(aligned(s * length, length), length)
-            count = counts_ref[s]
-            lse_all = lse_ref[here, :]
-            for p in range(pairs):
-                cols = slice(p * 128, (p + 1) * 128)
-                query = qkv_ref[here, cols] * jnp.asarray(HEAD**-0.5, BF)
-                keys2 = two_heads(qkv_ref[here, width + p * 128 : width + (p + 1) * 128])
-                values2 = two_heads(qkv_ref[here, 2 * width + p * 128 : 2 * width + (p + 1) * 128])
-                gout = gctx_ref[here, cols]
-                scores = masked_scores(query, keys2, count, length)
-                lse2 = halves(lse_all[:, 2 * p : 2 * p + 1], lse_all[:, 2 * p + 1 : 2 * p + 2], length)
-                probs = jnp.exp(scores - lse2)
-                gprobs = dot_nt(gout, values2)
-                weighted = gprobs * probs
-                sums = halves(
-                    jnp.sum(weighted[:, :length], -1, keepdims=True),
-                    jnp.sum(weighted[:, length:], -1, keepdims=True),
-                    length,
-                )
-                gscores = (probs * (gprobs - sums)).astype(BF)
-                gq = dot(gscores, keys2) * HEAD**-0.5
-                gk = one_of_two(dot_tn(gscores, query))
-                gv = one_of_two(dot_tn(probs.astype(BF), gout))
-                gq, gk, gv = gq.astype(BF), gk.astype(BF), gv.astype(BF)
-                gqkv_ref[here, cols] = gq
-                gqkv_ref[here, width + p * 128 : width + (p + 1) * 128] = gk
-                gqkv_ref[here, 2 * width + p * 128 : 2 * width + (p + 1) * 128] = gv
-                vs_ref[0:1, cols] += jnp.sum(gq.astype(F32), 0, keepdims=True)
-                vs_ref[1:2, cols] += jnp.sum(gv.astype(F32), 0, keepdims=True)
-            return carry
-
-        lax.fori_loop(0, sentences, sentence, 0)
-        x_t = x_ref[...].T
-
-        def columns(g, carry):
-            col = aligned(g * group, group)
-            dw_ref[:, pl.ds(col, group)] = dot(x_t, gqkv_ref[:, pl.ds(col, group)])
-            return carry
-
-        lax.fori_loop(0, 3 * width // group, columns, 0)
-        dw_ref[:, 3 * width : 4 * width] = dot_tn(ctx_ref[...], glow_ref[...])
-        dw_ref[:, 4 * width : 4 * width + 128] = vs_ref[...].T
-        dw_ref[:, 4 * width + 128 :] = jnp.zeros((width, 128), F32)
-        emit_blocks(place, dw_ref, send_ref, keep_ref, width // 8, True)
-
-    blocks = struct((2, 2, 4, width // 16, total // 2), BF)
-    return call(
-        body,
-        "attention_back",
-        [
-            (ids, "s"),
-            (counts, "s"),
-            (qkv, "v"),
-            (gctx, "v"),
-            (lse, "v"),
-            (tokens, "v"),
-            (context, "v"),
-            (glow, "v"),
-            (vgrads, "v"),
-        ],
-        [struct((rows, 3 * width), BF), blocks, blocks],
-        [pltpu.VMEM((width, total), F32), pltpu.VMEM((128, width), F32)],
-        2 * rows * width * 4 * width + 20 * rows * length * width,
-        rows * length * width // HEAD,
-    )
-
-
-def tokens_backward(gqkv, gattn, ids, bufs):
-    rows, width = gattn.shape
-    group = 256
-
-    def body(ids_ref, gqkv_ref, gattn_ref, *rest):
-        bufs_ref = rest[: len(bufs)]
-        gx_ref, w_ref, sems = rest[len(bufs) :]
-        place = Place(ids_ref)
-        copies = piece_copies(place, bufs_ref, w_ref, sems, width // 8, False)
-        for copy in copies:
-            copy.start()
-        for copy in copies:
-            copy.wait()
-        for g in range(width // group):
-            gx_ref[:, g * group : (g + 1) * group] = (
-                dot_nt(gqkv_ref[...], w_ref[g * group : (g + 1) * group, : 3 * width])
-                + gattn_ref[:, g * group : (g + 1) * group]
-            )
+            cols = slice(g * group, (g + 1) * group)
+            gx_ref[:, cols] = gattn_ref[:, cols] + dot_nt(g_ref[...], w_ref[cols, : 3 * width])
 
     return call(
         body,
         "tokens_back",
-        [(ids, "s"), (gqkv, "v"), (gattn, "v")] + [(b, "a") for b in bufs],
+        [(ids, "s"), (gqkv_a, "a"), (gqkv_b, "a"), (gattn, "v")] + [(b, "a") for b in bufs],
         [struct((rows, width), F32)],
-        [pltpu.VMEM((width, 3 * width + 128), BF), pltpu.SemaphoreType.DMA((16,))],
+        [
+            pltpu.VMEM((width, 3 * width + 128), BF),
+            pltpu.VMEM((rows, 3 * width), BF),
+            pltpu.SemaphoreType.DMA((16,)),
+            pltpu.SemaphoreType.DMA((6,)),
+        ],
         2 * rows * width * 3 * width,
     )[0]
 
@@ -887,13 +1112,12 @@
     return lax.ppermute(array, axis, pairs)
 
 
-def gather(piece, split_x):
-    near = jnp.stack([piece] + [swap(piece, "fsdp", 2 * k) for k in range(1, 4)])
-    far = swap(near, "fsdp", 1)
-    mine = [near, far]
-    if split_x:
-        mine += [swap(near, "dp", 2), swap(far, "dp", 2)]
-    return mine + [swap(m, "dp", 1) for m in mine]
+def hold(value, *after):
+    return lax.optimization_barrier((value, *after))[0]
+
+
+def gather_z(piece, *after):
+    return jnp.stack([hold(piece, *after)] + [swap(piece, "fsdp", 2 * k) for k in range(1, 4)])
 
 
 def add(*terms):
@@ -903,25 +1127,34 @@
     return total.astype(BF)
 
 
-def scatter(send, keep, split_x):
-    total = add(keep, swap(send, "dp", 1))
-    if split_x:
-        total = add(total[0], swap(total[1], "dp", 2))
-    else:
-        total = total[0]
-    total = add(total[0], swap(total[1], "fsdp", 1))
-    total = add(total[0], *[swap(total[k], "fsdp", 2 * k) for k in range(1, 4)])
-    if split_x:
-        own = [total, swap(total, "dp", 2)]
-    else:
-        own = [add(total, swap(total, "dp", 2))]
-    return own, [swap(part, "dp", 1) for part in own]
+def sum_core(send, keep, *after):
+    return add(hold(keep, *after), swap(send, "dp", 1))
+
+
+def sum_x(total, *after):
+    return add(hold(total[0], *after), swap(total[1], "dp", 2))
+
+
+def sum_y(total, *after):
+    return add(hold(total[0], *after), swap(total[1], "fsdp", 1))
+
+
+def sum_y_first(total, *after):
+    return add(hold(total[:, 0], *after), swap(total[:, 1], "fsdp", 1))
+
+
+def sum_z(total, *after):
+    return add(hold(total[0], *after), *[swap(total[k], "fsdp", 2 * k) for k in range(1, 4)])
 
 
 def in_order(own, other, bit, axis):
     first = jnp.where(bit == 0, own, other)
     second = jnp.where(bit == 0, other, own)
     return jnp.concatenate([first, second], axis=axis)
+
+
+def share_core(own, c):
+    return in_order(own, swap(own, "dp", 1), c, 0).astype(F32)
 
 
 def on_device_split(
@@ -963,60 +1196,81 @@
     span = second.shape[1] // 2
     second = lax.dynamic_slice(second, (c * half, x * span), (half, span))
     third = lax.dynamic_slice(w_down, (c * (w_down.shape[0] // 2), 0), (w_down.shape[0] // 2, width))
-    first, second, third = gather(first, False), gather(second, True), gather(third, False)
-
-    qkv, context, lse, vec = attend_forward(token_rows, lengths, ids, first, sentences, length)
+
+    near1 = gather_z(first)
+    near2 = gather_z(hold(second, near1))
+    far1 = hold(swap(near1, "fsdp", 1), near2)
+    bufs1 = [near1, far1, swap(near1, "dp", 1), swap(far1, "dp", 1)]
+    qkv, context, lse, vec = attend_forward(
+        hold(token_rows, near2), lengths, ids, bufs1, sentences, length
+    )
+    near3 = gather_z(hold(third, near2), vec)
+    far2 = hold(swap(near2, "fsdp", 1), vec)
+    side2 = hold(swap(near2, "dp", 2), vec)
+    far3 = swap(near3, "fsdp", 1)
+    mine2 = [near2, far2, side2, swap(far2, "dp", 2)]
+    bufs2 = mine2 + [swap(hold(m, vec), "dp", 1) for m in mine2]
     ratio = wide // width
     bias_up = vec[8 : 8 + ratio].reshape(ratio, 8, part).transpose(1, 0, 2).reshape(1, wide)
     normed, inverse, low, active, slope = up_forward(
-        context, token_rows, vec, bias_up, ids, second, length
-    )
-    pooled, gres, glow, vg_ffn, send3, keep3 = down_forward(
-        active, normed, vec, lengths, pooled_grad, ids, third, sentences, length
-    )
-    down = scatter(send3, keep3, False)
-    gup, gbias_in, send2, keep2 = up_backward(glow, slope, low, ids, third)
-    up = scatter(send2, keep2, True)
-    gattn, gattn_low, gctx, vg_attn = hidden_backward(
-        gup, gres, normed, inverse, vec, ids, second, length
-    )
-    vgrads = jnp.concatenate(
-        [
-            jnp.zeros((2, width), F32),
-            vg_attn[2:3],
-            vg_attn[0:2],
-            vg_ffn[2:3],
-            vg_ffn[0:2],
-            gbias_in.reshape(8, ratio, part).transpose(1, 0, 2).reshape(ratio, width),
-            jnp.zeros((8 - ratio, width), F32),
-        ],
-        0,
-    )
-    gqkv, send1, keep1 = attend_backward(
-        qkv, gctx, lse, token_rows, context, gattn_low, vgrads, lengths, ids, sentences, length
-    )
-    rest = scatter(send1, keep1, True)
-    gtokens = tokens_backward(gqkv, gattn, ids, first).reshape(sentences, length, width)
-
-    def joined(parts, split_x):
-        own, other = parts
-        if split_x:
-            own, other = in_order(*own, x, 1), in_order(*other, x, 1)
-        else:
-            own, other = own[0], other[0]
-        return in_order(own, other, c, 0).astype(F32)
-
-    g_down = joined(down, False).T
-    g_in = joined(up, True)
-    g_rest = joined(rest, True)
-    g_vec = g_rest[:, 4 * width : 4 * width + 8 + ratio].T
+        context, token_rows, vec, bias_up, ids, bufs2, length
+    )
+    far3 = hold(far3, low)
+    bufs3 = [near3, far3, swap(near3, "dp", 1), swap(far3, "dp", 1)]
+    pooled, vg_ffn, send3, keep3, gup, gbias_in, gres = down_and_back(
+        active, slope, normed, vec, lengths, pooled_grad, ids, bufs3, sentences, length
+    )
+    sums3 = sum_core(send3, keep3)
+    send2, keep2, gctx, vg_attn, gattn, gattn_low = up_and_back(
+        low, hold(gup, sums3), gres, normed, inverse, vec, ids, bufs2, length
+    )
+    sums3 = sum_y(sums3[0], gctx)
+    sums2 = sum_core(hold(send2, gctx, sums3), keep2)
+    pairs = width // 128
+    most = pairs * 2 // 3
+    gqkv_a, vg_a = attend_backward(
+        qkv, hold(gctx, sums3, sums2), lse, lengths, sentences, length, 0, most, "attention_back"
+    )
+    send_a, keep_a = attend_weight(gqkv_a, token_rows, context, gattn_low, ids)
+    sums2 = sum_x(sums2, keep_a)
+    sums3 = sum_z(sums3, keep_a)
+    sums_a = sum_core(hold(send_a, sums2, sums3), keep_a)
+    gqkv_b, vg_b = attend_backward(
+        qkv, hold(gctx, sums_a), lse, lengths, sentences, length, most, pairs, "attention_back_rest"
+    )
+    gbias_in = gbias_in.reshape(8, ratio, part).transpose(1, 0, 2).reshape(ratio, width)
+    send_b, keep_b = last_weight(gqkv_b, token_rows, vg_a, vg_b, vg_attn, vg_ffn, gbias_in, ids)
+    sums2 = sum_y(sums2, gqkv_b)
+    sums3 = add(hold(sums3, keep_b), swap(sums3, "dp", 2))
+    sums_b = sum_core(send_b, keep_b)
+    gtokens = tokens_backward(gqkv_a, hold(gqkv_b, sums_b, sums2, sums3), gattn, ids, bufs1)
+    sums_a = sum_x(sums_a, gtokens)
+    sums2 = sum_z(sums2, sums_a)
+    sums_b = sum_y_first(sums_b, sums2)
+    sums_a, sums2, sums_b = lax.optimization_barrier((sums_a, sums2, sums_b))
+    sums_a = sum_y(sums_a)
+    sums_b = sum_x(sums_b)
+    g_in = in_order(sums2, swap(sums2, "dp", 2), x, 1)
+    sums_a, sums_b, g_in = lax.optimization_barrier((sums_a, sums_b, g_in))
+    g_down = share_core(sums3, c).T
+    g_in = share_core(g_in, c)
+    sums_a = sum_z(sums_a)
+    sums_b = sum_z(sums_b)
+    g_b = share_core(in_order(sums_b, swap(sums_b, "dp", 2), x, 1), c)
+    g_a = share_core(in_order(sums_a, swap(sums_a, "dp", 2), x, 1), c)
+    gtokens = gtokens.reshape(sentences, length, width)
+    cut_a, cut_b = most * 128, (pairs - most) * 128
+    g_qkv = [
+        g[:, i * cut : (i + 1) * cut] for i in range(3) for g, cut in ((g_a, cut_a), (g_b, cut_b))
+    ]
+    g_vec = g_b[:, 3 * cut_b : 3 * cut_b + 8 + ratio].T
     return (
         pooled,
         gtokens,
-        g_rest[:, : 3 * width],
+        jnp.concatenate(g_qkv, 1),
         g_vec[0],
         g_vec[1],
-        g_rest[:, 3 * width : 4 * width],
+        g_a[:, 3 * cut_a :],
         g_vec[2],
         g_vec[3],
         g_vec[4],

time: 393 us -> 320 us (0.81)
  starting transfers between devices: 83.3 us -> 56 us
  waiting for transfers between devices: 111 us -> 85.4 us
  Pallas kernels: 162 us -> 143 us
    pallas_call x7 -> x3, Pallas kernels: 162 us -> 47.6 us  [call(): pl.pallas_call(body, name=name, out_shape=tuple(outs), in_specs=[spaces[s...]
    pallas_call x0 -> x6, Pallas kernels: none -> 95.7 us  [grid_call(): pl.pallas_call(body, name=name, out_shape=tuple((o for o, _, _ in outs)),...]
    ppermute x47 -> x53, starting transfers between devices: 83.3 us -> 56 us  [swap(): return lax.ppermute(array, axis, pairs)]
    ppermute x47 -> x53, waiting for transfers between devices: 111 us -> 85.4 us  [swap(): return lax.ppermute(array, axis, pairs)]
    convert_element_type x12 -> x16, other arithmetic: 8.9 us -> 13.3 us  [add(): return total.astype(BF)]
    slice x5 -> x0, local copies, waits for them, and re-layouts: 3.93 us -> none  [the longest x1 0.97 us: on_device_split(): g_rest[:, :3 * width]]
  transfers between devices with their start and end apart: 47 -> 53, of which waited for: 16 -> 21; matrix products, arithmetic and copies ran while one was open for 6% -> 7% of each run, Pallas kernels for 35% -> 35%
where the time goes in v2:
time: 320 us; the launch traced here: 318 us
  Pallas kernels  143 us (45%)
  waiting for transfers between devices  85.4 us (27%)
  starting transfers between devices  56 us (18%)
  other arithmetic  19.3 us (6%)
  local copies, waits for them, and re-layouts  13 us (4%)
    pallas_call x6, Pallas kernels, grid_call(): pl.pallas_call(body, name=name, out_shape=tuple((o for o, _, _ in outs)),...  95.7 us
    ppermute x53, waiting for transfers between devices, swap(): return lax.ppermute(array, axis, pairs)  85.4 us
    ppermute x53, starting transfers between devices, swap(): return lax.ppermute(array, axis, pairs)  56 us
    pallas_call x3, Pallas kernels, call(): pl.pallas_call(body, name=name, out_shape=tuple(outs), in_specs=[spaces[s...  47.6 us
    convert_element_type x16, other arithmetic, add(): return total.astype(BF)  13.3 us
  transfers between devices with their start and end apart: 53, of which 21 were waited for; matrix products, arithmetic and copies ran while one was open for 7% of the time, Pallas kernels for 35%

profile of v2, /device:TPU:0, one launch (start us, length us, event | category | flops | bytes accessed | tf_op | source)
XLA Modules:
  0.0 318.3 jit_solution(16416615526099713333)
XLA Ops:
  2.5 1.0 fusion.1
  3.5 3.1 collective-permute-start
  6.6 2.6 collective-permute-start.1
  9.2 7.4 %collective-permute-done = bf16[48,2432]{1,0:T(8,128)(2,1)S(1)} collective-permute-done((bf16[48,2432]{1,0:T(8,128)(2,1)S(1)}, bf16[48,2432]{1,0:T(8,128)(2,1)S(1)}, u32[]{:S(2)}, u32[]{:S(2)}) %collective-permute-start) | collective-permute-done | bytes 233504 | tf_op jit(solution)/shard_map/ppermute | solution.py:1112
  16.5 9.5 %collective-permute-done.1 = bf16[48,2432]{1,0:T(8,128)(2,1)S(1)} collective-permute-done((bf16[48,2432]{1,0:T(8,128)(2,1)S(1)}, bf16[48,2432]{1,0:T(8,128)(2,1)S(1)}, u32[]{:S(2)}, u32[]{:S(2)}) %collective-permute-start.1) | collective-permute-done | bytes 233504 | tf_op jit(solution)/shard_map/ppermute | solution.py:1112
  26.2 1.6 collective-permute-start.6
  27.9 4.3 %collective-permute-start.3 = (bf16[48,1920]{1,0:T(8,128)(2,1)S(1)}, bf16[48,1920]{1,0:T(8,128)(2,1)S(1)}, u32[]{:S(2)}, u32[]{:S(2)}) collective-permute-start(bf16[48,1920]{1,0:T(8,128)(2,1)S(1)} %fusion.2), channel_id=1, source_target_pairs={{0,2},{1,3},{2,0},{3,1},{4,6},{5,7},{6,4},{7,5},{8,10},{9,11},{10,... | collective-permute-start | bytes 552968 | tf_op jit(solution)/shard_map/ppermute | solution.py:1112
  32.1 1.1 collective-permute-start.4
  33.2 1.4 collective-permute-start.5
  34.6 3.4 %collective-permute-done.3 = bf16[48,1920]{1,0:T(8,128)(2,1)S(1)} collective-permute-done((bf16[48,1920]{1,0:T(8,128)(2,1)S(1)}, bf16[48,1920]{1,0:T(8,128)(2,1)S(1)}, u32[]{:S(2)}, u32[]{:S(2)}) %collective-permute-start.3) | collective-permute-done | bytes 184352 | tf_op jit(solution)/shard_map/ppermute | solution.py:1112
  38.0 9.7 %collective-permute-done.4 = bf16[48,1920]{1,0:T(8,128)(2,1)S(1)} collective-permute-done((bf16[48,1920]{1,0:T(8,128)(2,1)S(1)}, bf16[48,1920]{1,0:T(8,128)(2,1)S(1)}, u32[]{:S(2)}, u32[]{:S(2)}) %collective-permute-start.4) | collective-permute-done | bytes 184352 | tf_op jit(solution)/shard_map/ppermute | solution.py:1112
  48.5 4.9 %collective-permute-start.16 = (bf16[192,768]{1,0:T(8,128)(2,1)S(1)}, bf16[192,768]{1,0:T(8,128)(2,1)S(1)}, u32[]{:S(2)}, u32[]{:S(2)}) collective-permute-start(bf16[192,768]{1,0:T(8,128)(2,1)S(1)} %constant_dynamic-slice_fusion), channel_id=1, source_target_pairs={{0,2},{1,3},{2,0},{3,1},{4,6},{5,7},{6,4},{7,5},{8,10},{9,11},{10,... | collective-permute-start | bytes 884744 | tf_op jit(solution)/shard_map/ppermute | solution.py:1112
  53.4 1.1 collective-permute-start.17
  54.5 1.4 collective-permute-start.18
  55.9 1.5 collective-permute-start.10
  58.0 16.0 %qkv_attention.1 = (bf16[896,2304]{1,0:T(8,128)(2,1)}, bf16[896,768]{1,0:T(8,128)(2,1)}, f32[896,128]{1,0:T(8,128)}, f32[16,768]{1,0:T(8,128)}) custom-call(s32[4]{0:T(128)} %pad_add_fusion.ids_ref, s32[7]{0:T(128)} %counts_ref.7, bf16[896,768]{1,0:T(8,128)(2,1)} %bitcast.99, bf16[4,48,2432]{2,1,0:T(8,128)(2,1)} %copy-done.2, ...), custom_call_target="tpu_custom_call" | custom-call | flops 1 | bytes 1 | tf_op jit(solution)/shard_map/qkv_attention/pallas_call | solution.py:76
  74.6 2.3 collective-permute-done.17
  76.9 1.1 pad_maximum_fusion.b0
  79.1 13.0 %collective-permute-done.11.rest_3_ = bf16[4,48,1920]{2,1,0:T(8,128)(2,1)S(1)} collective-permute-done((bf16[4,48,1920]{2,1,0:T(8,128)(2,1)}, bf16[4,48,1920]{2,1,0:T(8,128)(2,1)S(1)}, u32[]{:S(2)}, u32[]{:S(2)}) %collective-permute-start.11) | collective-permute-done | bytes 737312 | tf_op jit(solution)/shard_map/ppermute | solution.py:1112
  94.4 21.3 %out_norm_up.1 = (f32[896,768]{1,0:T(8,128)}, f32[896,128]{1,0:T(8,128)}, bf16[896,768]{1,0:T(8,128)(2,1)}, bf16[896,3072]{1,0:T(8,128)(2,1)}, bf16[896,3072]{1,0:T(8,128)(2,1)}) custom-call(s32[4]{0:T(128)} %pad_add_fusion.ids_ref, bf16[896,768]{1,0:T(8,128)(2,1)} %get-tuple-element.80.ctx_ref, bf16[896,768]{1,0:T(8,128)(2,1)} %bitcast.100, ...), custom_call_target="tpu_custom_call" | custom-call | flops 1 | bytes 1 | tf_op jit(solution)/shard_map/out_norm_up/pallas_call | solution.py:76
  116.0 2.9 collective-permute-done.21.b3
  118.9 1.0 copy-done.8
  119.9 32.7 %down_and_back.1 = (f32[7,768]{1,0:T(8,128)}, f32[8,768]{1,0:T(8,128)}, bf16[1,2,4,384,384]{4,3,2,1,0:T(8,128)(2,1)}, bf16[1,2,4,384,384]{4,3,2,1,0:T(8,128)(2,1...) custom-call(s32[4]{0:T(128)} %pad_add_fusion.ids_ref, s32[7]{0:T(128)} %counts_ref.7, ...), custom_call_target="tpu_custom_call" | custom-call | flops 1 | bytes 1 | tf_op jit(solution)/shard_map/down_and_back/pallas_call | solution.py:267
  152.8 4.6 %collective-permute-done.22 = bf16[1,2,4,384,384]{4,3,2,1,0:T(8,128)(2,1)S(1)} collective-permute-done((bf16[1,2,4,384,384]{4,3,2,1,0:T(8,128)(2,1)}, bf16[1,2,4,384,384]{4,3,2,1,0:T(8,128)(2,1)S(1)}, u32[]{:S(2)}, u32[]{:S(2)}) %collective-permute-start.22) | collective-permute-done | bytes 2359328 | tf_op jit(solution)/shard_map/ppermute | solution.py:1112
  157.4 2.2 add_convert_fusion.1
  160.6 24.3 %up_and_back.1 = (bf16[2,2,4,48,1536]{4,3,2,1,0:T(8,128)(2,1)}, bf16[2,2,4,48,1536]{4,3,2,1,0:T(8,128)(2,1)}, bf16[896,768]{1,0:T(8,128)(2,1)}, f32[8,768]{1,0:T...) custom-call(s32[4]{0:T(128)} %pad_add_fusion.ids_ref, bf16[896,768]{1,0:T(8,128)(2,1)} %get-tuple-element.93.low_ref, ...), custom_call_target="tpu_custom_call" | custom-call | flops 1 | bytes 1 | tf_op jit(solution)/shard_map/up_and_back/pallas_call | solution.py:267
  184.9 3.0 collective-permute-done.23
  188.3 4.7 %collective-permute-done.24 = bf16[2,2,4,48,1536]{4,3,2,1,0:T(8,128)(2,1)S(1)} collective-permute-done((bf16[2,2,4,48,1536]{4,3,2,1,0:T(8,128)(2,1)}, bf16[2,2,4,48,1536]{4,3,2,1,0:T(8,128)(2,1)S(1)}, u32[]{:S(2)}, u32[]{:S(2)}) %collective-permute-start.24) | collective-permute-done | bytes 2359328 | tf_op jit(solution)/shard_map/ppermute | solution.py:1112
  196.3 2.2 collective-permute-start.27
  198.5 1.4 collective-permute-start.28
  199.9 12.8 %attention_back.1 = (bf16[896,1536]{1,0:T(8,128)(2,1)}, f32[8,512]{1,0:T(8,128)}) custom-call(s32[7]{0:T(128)} %counts_ref.7, bf16[896,2304]{1,0:T(8,128)(2,1)} %get-tuple-element.96.refs_0_.refs_1_.refs_2_.refs_3_.refs_4_.refs_5_, bf16[896,2304]{1,0:T(8,128)(2,1)} %get-tuple-element.96.refs_0_.refs_1_.refs_2_.refs_3_.refs_4_.refs_5_, ...), custom_call_target="tpu_custom_call" | custom-call | flops 1 | bytes 1 | tf_op jit(solution)/shard_map/attention_back/pallas_call | solution.py:267
  212.7 11.0 %attention_weight.1 = (bf16[2,2,4,48,1152]{4,3,2,1,0:T(8,128)(2,1)}, bf16[2,2,4,48,1152]{4,3,2,1,0:T(8,128)(2,1)}) custom-call(s32[4]{0:T(128)} %pad_add_fusion.ids_ref, bf16[896,1536]{1,0:T(8,128)(2,1)} %get-tuple-element.110.gqkv_ref.ga_hbm, bf16[896,768]{1,0:T(8,128)(2,1)} %get-tuple-element.111.glow_ref, bf16[896,768]{1,0:T(8,128)(2,1)} %bitcast.101, ...), custom_call_target="tpu_custom_call" | custom-call | flops 1 | bytes 1 | tf_op jit(solution)/shard_map/attention_weight/pallas_call | solution.py:267
  223.8 2.0 add_convert_fusion.11
  228.1 1.5 collective-permute-start.32
  231.2 2.4 add_convert_fusion.2
  233.6 8.7 %attention_back_rest.1 = (bf16[896,768]{1,0:T(8,128)(2,1)}, f32[8,256]{1,0:T(8,128)}) custom-call(s32[7]{0:T(128)} %counts_ref.7, bf16[896,2304]{1,0:T(8,128)(2,1)} %get-tuple-element.96.refs_0_.refs_1_.refs_2_.refs_3_.refs_4_.refs_5_, bf16[896,2304]{1,0:T(8,128)(2,1)} %get-tuple-element.96.refs_0_.refs_1_.refs_2_.refs_3_.refs_4_.refs_5_, ...), custom_call_target="tpu_custom_call" | custom-call | flops 1 | bytes 1 | tf_op jit(solution)/shard_map/attention_back_rest/pallas_call | solution.py:267
  242.3 6.2 %last_weight.1 = (bf16[2,2,4,48,512]{4,3,2,1,0:T(8,128)(2,1)}, bf16[2,2,4,48,512]{4,3,2,1,0:T(8,128)(2,1)}) custom-call(s32[4]{0:T(128)} %pad_add_fusion.ids_ref, bf16[896,768]{1,0:T(8,128)(2,1)} %get-tuple-element.128.gqkv_ref.gb_hbm, bf16[896,768]{1,0:T(8,128)(2,1)} %bitcast.102, f32[8,512]{1,0:T(8,128)} %get-tuple-element.119.va_ref, ...), custom_call_target="tpu_custom_call" | custom-call | flops 1 | bytes 1 | tf_op jit(solution)/shard_map/last_weight/pallas_call | solution.py:267
  248.5 1.0 add_convert_fusion.10
  250.9 1.2 add_convert_fusion.7
  252.8 1.7 collective-permute-start.34
  254.5 1.2 collective-permute-start.35
  255.7 1.5 collective-permute-start.36
  257.5 10.3 %tokens_back.1 = f32[896,768]{1,0:T(8,128)} custom-call(s32[4]{0:T(128)} %pad_add_fusion.ids_ref, bf16[896,1536]{1,0:T(8,128)(2,1)} %get-tuple-element.110.gqkv_ref.ga_hbm, bf16[896,768]{1,0:T(8,128)(2,1)} %get-tuple-element.128.gqkv_ref.gb_hbm, f32[896,768]{1,0:T(8,128)} %get-tuple-element.129.gattn_ref, bf16[4,48,2432]{2,1,0:T(8,128)(2,1)} %copy-done.2, ...), custom_call_target="tpu_custom_call" | custom-call | flops 1 | bytes 1 | tf_op jit(solution)/shard_map/tokens_back/pallas_call | solution.py:76
  267.9 1.4 collective-permute-start.37
  269.4 2.7 collective-permute-done.33
  272.1 1.4 add_convert_fusion.5
  273.5 1.1 add_convert_fusion.13
  274.6 3.5 %collective-permute-done.37 = bf16[2,4,48,512]{3,2,1,0:T(8,128)(2,1)S(1)} collective-permute-done((bf16[2,4,48,512]{3,2,1,0:T(8,128)(2,1)S(1)}, bf16[2,4,48,512]{3,2,1,0:T(8,128)(2,1)S(1)}, u32[]{:S(2)}, u32[]{:S(2)}) %collective-permute-start.37) | collective-permute-done | bytes 393248 | tf_op jit(solution)/shard_map/ppermute | solution.py:1112
  278.2 1.4 collective-permute-start.40
  280.5 1.4 collective-permute-start.38
  281.9 2.5 collective-permute-done.40
  284.5 2.0 collective-permute-done.39
  286.6 3.8 %collective-permute-done.38 = bf16[4,48,1152]{2,1,0:T(8,128)(2,1)S(1)} collective-permute-done((bf16[4,48,1152]{2,1,0:T(8,128)(2,1)S(1)}, bf16[4,48,1152]{2,1,0:T(8,128)(2,1)S(1)}, u32[]{:S(2)}, u32[]{:S(2)}) %collective-permute-start.38) | collective-permute-done | bytes 442400 | tf_op jit(solution)/shard_map/ppermute | solution.py:1112
  291.1 2.3 collective-permute-start.47
  293.4 1.5 collective-permute-start.48
  295.0 1.4 copy.62
  296.4 3.0 collective-permute-done.48
  299.4 1.3 collective-permute-start.49
  300.7 2.0 collective-permute-start.42
  302.7 2.4 collective-permute-start.43
  305.2 1.7 collective-permute-done.41
  307.0 2.9 collective-permute-done.42
  312.7 2.1 collective-permute-done.44
  315.0 1.1 maximum_convert_fusion
  (151 shorter events, 25.9 us)
Async XLA Ops:
  0.6 47.8 %copy-start = (bf16[384,768]{1,0:T(8,128)(2,1)S(1)}, bf16[384,768]{1,0:T(8,128)(2,1)}, u32[]{:S(2)}) copy-start(bf16[384,768]{1,0:T(8,128)(2,1)} %param.28) | copy-start | bytes 1769476
  0.7 27.1 %copy-start.11 = (bf16[96,768]{1,0:T(8,128)(2,1)S(1)}, bf16[96,768]{1,0:T(8,128)(2,1)}, u32[]{:S(2)}) copy-start(bf16[96,768]{1,0:T(8,128)(2,1)} %param.22) | copy-start | bytes 442372
  0.7 27.1 %copy-start.10 = (bf16[96,3072]{1,0:T(8,128)(2,1)S(1)}, bf16[96,3072]{1,0:T(8,128)(2,1)}, u32[]{:S(2)}) copy-start(bf16[96,3072]{1,0:T(8,128)(2,1)} %param.26) | copy-start | bytes 1769476
  3.5 13.1 %collective-permute-start = (bf16[48,2432]{1,0:T(8,128)(2,1)S(1)}, bf16[48,2432]{1,0:T(8,128)(2,1)S(1)}, u32[]{:S(2)}, u32[]{:S(2)}) collective-permute-start(bf16[48,2432]{1,0:T(8,128)(2,1)S(1)} %fusion.1), channel_id=1, source_target_pairs={{0,2},{1,3},{2,0},{3,1},{4,6},{5,7},{6,4},{7,5},{8,10},{9,11},{10,... | collective-permute-start | bytes 700424 | tf_op jit(solution)/shard_map/ppermute | solution.py:1112
  6.6 19.5 %collective-permute-start.1 = (bf16[48,2432]{1,0:T(8,128)(2,1)S(1)}, bf16[48,2432]{1,0:T(8,128)(2,1)S(1)}, u32[]{:S(2)}, u32[]{:S(2)}) collective-permute-start(bf16[48,2432]{1,0:T(8,128)(2,1)S(1)} %fusion.1), channel_id=1, source_target_pairs={{0,4},{1,5},{2,6},{3,7},{4,0},{5,1},{6,2},{7,3},{8,12},{9,13},{10,... | collective-permute-start | bytes 700424 | tf_op jit(solution)/shard_map/ppermute | solution.py:1112
  9.2 16.9 %collective-permute-start.2 = (bf16[48,2432]{1,0:T(8,128)(2,1)S(1)}, bf16[48,2432]{1,0:T(8,128)(2,1)S(1)}, u32[]{:S(2)}, u32[]{:S(2)}) collective-permute-start(bf16[48,2432]{1,0:T(8,128)(2,1)S(1)} %fusion.1), channel_id=1, source_target_pairs={{0,6},{1,7},{2,4},{3,5},{4,2},{5,3},{6,0},{7,1},{8,14},{9,15},{10,... | collective-permute-start | bytes 700424 | tf_op jit(solution)/shard_map/ppermute | solution.py:1112
  26.2 31.8 %copy-start.2 = (bf16[4,48,2432]{2,1,0:T(8,128)(2,1)}, bf16[4,48,2432]{2,1,0:T(8,128)(2,1)S(1)}, u32[]{:S(2)}) copy-start(bf16[4,48,2432]{2,1,0:T(8,128)(2,1)S(1)} %pad_maximum_fusion.1.b0) | copy-start | bytes 2801668
  26.2 21.6 %collective-permute-start.6 = (bf16[4,48,2432]{2,1,0:T(8,128)(2,1)S(1)}, bf16[4,48,2432]{2,1,0:T(8,128)(2,1)S(1)}, u32[]{:S(2)}, u32[]{:S(2)}) collective-permute-start(bf16[4,48,2432]{2,1,0:T(8,128)(2,1)S(1)} %pad_maximum_fusion.1.b0), channel_id=1, source_target_pairs={{0,1},{1,0},{2,3},{3,2},{4,5},{5,4},{6,7},{7,6},{8,9},{9,8},{10,11... | collective-permute-start | bytes 2801672 | tf_op jit(solution)/shard_map/ppermute | solution.py:1112
  27.9 10.1 %collective-permute-start.3 = (bf16[48,1920]{1,0:T(8,128)(2,1)S(1)}, bf16[48,1920]{1,0:T(8,128)(2,1)S(1)}, u32[]{:S(2)}, u32[]{:S(2)}) collective-permute-start(bf16[48,1920]{1,0:T(8,128)(2,1)S(1)} %fusion.2), channel_id=1, source_target_pairs={{0,2},{1,3},{2,0},{3,1},{4,6},{5,7},{6,4},{7,5},{8,10},{9,11},{10,... | collective-permute-start | bytes 552968 | tf_op jit(solution)/shard_map/ppermute | solution.py:1112
  32.1 15.5 %collective-permute-start.4 = (bf16[48,1920]{1,0:T(8,128)(2,1)S(1)}, bf16[48,1920]{1,0:T(8,128)(2,1)S(1)}, u32[]{:S(2)}, u32[]{:S(2)}) collective-permute-start(bf16[48,1920]{1,0:T(8,128)(2,1)S(1)} %fusion.2), channel_id=1, source_target_pairs={{0,4},{1,5},{2,6},{3,7},{4,0},{5,1},{6,2},{7,3},{8,12},{9,13},{10,... | collective-permute-start | bytes 552968 | tf_op jit(solution)/shard_map/ppermute | solution.py:1112
  33.2 14.5 %collective-permute-start.5 = (bf16[48,1920]{1,0:T(8,128)(2,1)S(1)}, bf16[48,1920]{1,0:T(8,128)(2,1)S(1)}, u32[]{:S(2)}, u32[]{:S(2)}) collective-permute-start(bf16[48,1920]{1,0:T(8,128)(2,1)S(1)} %fusion.2), channel_id=1, source_target_pairs={{0,6},{1,7},{2,4},{3,5},{4,2},{5,3},{6,0},{7,1},{8,14},{9,15},{10,... | collective-permute-start | bytes 552968 | tf_op jit(solution)/shard_map/ppermute | solution.py:1112
  34.6 19.9 %collective-permute-start.7 = (bf16[4,48,2432]{2,1,0:T(8,128)(2,1)S(1)}, bf16[4,48,2432]{2,1,0:T(8,128)(2,1)}, u32[]{:S(2)}, u32[]{:S(2)}) collective-permute-start(bf16[4,48,2432]{2,1,0:T(8,128)(2,1)S(1)} %pad_maximum_fusion.1.b0), channel_id=1, source_target_pairs={{0,8},{8,0},{16,24},{24,16},{1,9},{9,1},{17,25},{25,17},{2,10},{10... | collective-permute-start | bytes 2801672 | tf_op jit(solution)/shard_map/ppermute | solution.py:1112
  47.8 31.3 %copy-start.3 = (bf16[4,48,1920]{2,1,0:T(8,128)(2,1)}, bf16[4,48,1920]{2,1,0:T(8,128)(2,1)S(1)}, u32[]{:S(2)}) copy-start(bf16[4,48,1920]{2,1,0:T(8,128)(2,1)S(1)} %pad_maximum_fusion.2.rest_0_) | copy-start | bytes 2211844
  47.8 10.2 %copy-start.5 = (bf16[4,48,2432]{2,1,0:T(8,128)(2,1)}, bf16[4,48,2432]{2,1,0:T(8,128)(2,1)S(1)}, u32[]{:S(2)}) copy-start(bf16[4,48,2432]{2,1,0:T(8,128)(2,1)S(1)} %collective-permute-done.6.b1) | copy-start | bytes 2801668
  47.8 8.1 %collective-permute-start.8 = (bf16[4,48,2432]{2,1,0:T(8,128)(2,1)S(1)}, bf16[4,48,2432]{2,1,0:T(8,128)(2,1)}, u32[]{:S(2)}, u32[]{:S(2)}) collective-permute-start(bf16[4,48,2432]{2,1,0:T(8,128)(2,1)S(1)} %collective-permute-done.6.b1), channel_id=1, source_target_pairs={{0,8},{8,0},{16,24},{24,16},{1,9},{9,1},{17,25},{25,17},{2,10},{10... | collective-permute-start | bytes 2801672 | tf_op jit(solution)/shard_map/ppermute | solution.py:1112
  47.9 26.1 %collective-permute-start.9 = (bf16[4,48,1920]{2,1,0:T(8,128)(2,1)S(1)}, bf16[4,48,1920]{2,1,0:T(8,128)(2,1)}, u32[]{:S(2)}, u32[]{:S(2)}) collective-permute-start(bf16[4,48,1920]{2,1,0:T(8,128)(2,1)S(1)} %pad_maximum_fusion.2.rest_0_), channel_id=1, source_target_pairs={{0,1},{1,0},{2,3},{3,2},{4,5},{5,4},{6,7},{7,6},{8,9},{9,8},{10,11... | collective-permute-start | bytes 2211848 | tf_op jit(solution)/shard_map/ppermute | solution.py:1112
  48.5 26.1 %collective-permute-start.16 = (bf16[192,768]{1,0:T(8,128)(2,1)S(1)}, bf16[192,768]{1,0:T(8,128)(2,1)S(1)}, u32[]{:S(2)}, u32[]{:S(2)}) collective-permute-start(bf16[192,768]{1,0:T(8,128)(2,1)S(1)} %constant_dynamic-slice_fusion), channel_id=1, source_target_pairs={{0,2},{1,3},{2,0},{3,1},{4,6},{5,7},{6,4},{7,5},{8,10},{9,11},{10,... | collective-permute-start | bytes 884744 | tf_op jit(solution)/shard_map/ppermute | solution.py:1112
  53.4 23.4 %collective-permute-start.17 = (bf16[192,768]{1,0:T(8,128)(2,1)S(1)}, bf16[192,768]{1,0:T(8,128)(2,1)S(1)}, u32[]{:S(2)}, u32[]{:S(2)}) collective-permute-start(bf16[192,768]{1,0:T(8,128)(2,1)S(1)} %constant_dynamic-slice_fusion), channel_id=1, source_target_pairs={{0,4},{1,5},{2,6},{3,7},{4,0},{5,1},{6,2},{7,3},{8,12},{9,13},{10,... | collective-permute-start | bytes 884744 | tf_op jit(solution)/shard_map/ppermute | solution.py:1112
  54.5 22.3 %collective-permute-start.18 = (bf16[192,768]{1,0:T(8,128)(2,1)S(1)}, bf16[192,768]{1,0:T(8,128)(2,1)}, u32[]{:S(2)}, u32[]{:S(2)}) collective-permute-start(bf16[192,768]{1,0:T(8,128)(2,1)S(1)} %constant_dynamic-slice_fusion), channel_id=1, source_target_pairs={{0,6},{1,7},{2,4},{3,5},{4,2},{5,3},{6,0},{7,1},{8,14},{9,15},{10,... | collective-permute-start | bytes 884744 | tf_op jit(solution)/shard_map/ppermute | solution.py:1112
  55.9 22.6 %collective-permute-start.10 = (bf16[4,48,1920]{2,1,0:T(8,128)(2,1)S(1)}, bf16[4,48,1920]{2,1,0:T(8,128)(2,1)}, u32[]{:S(2)}, u32[]{:S(2)}) collective-permute-start(bf16[4,48,1920]{2,1,0:T(8,128)(2,1)S(1)} %pad_maximum_fusion.2.rest_0_), channel_id=1, source_target_pairs={{0,16},{8,24},{16,0},{24,8},{1,17},{9,25},{17,1},{25,9},{2,18},{10... | collective-permute-start | bytes 2211848 | tf_op jit(solution)/shard_map/ppermute | solution.py:1112
  74.0 18.1 %collective-permute-start.11 = (bf16[4,48,1920]{2,1,0:T(8,128)(2,1)}, bf16[4,48,1920]{2,1,0:T(8,128)(2,1)S(1)}, u32[]{:S(2)}, u32[]{:S(2)}) collective-permute-start(bf16[4,48,1920]{2,1,0:T(8,128)(2,1)} %collective-permute-done.9.rest_1_), channel_id=1, source_target_pairs={{0,16},{8,24},{16,0},{24,8},{1,17},{9,25},{17,1},{25,9},{2,18},{10... | collective-permute-start | bytes 2211848 | tf_op jit(solution)/shard_map/ppermute | solution.py:1112
  78.0 37.8 %copy-start.4 = (bf16[4,192,768]{2,1,0:T(8,128)(2,1)}, bf16[4,192,768]{2,1,0:T(8,128)(2,1)S(1)}, u32[]{:S(2)}) copy-start(bf16[4,192,768]{2,1,0:T(8,128)(2,1)S(1)} %pad_maximum_fusion.b0) | copy-start | bytes 3538948
  78.0 37.8 %collective-permute-start.19 = (bf16[4,192,768]{2,1,0:T(8,128)(2,1)S(1)}, bf16[4,192,768]{2,1,0:T(8,128)(2,1)}, u32[]{:S(2)}, u32[]{:S(2)}) collective-permute-start(bf16[4,192,768]{2,1,0:T(8,128)(2,1)S(1)} %pad_maximum_fusion.b0), channel_id=1, source_target_pairs={{0,1},{1,0},{2,3},{3,2},{4,5},{5,4},{6,7},{7,6},{8,9},{9,8},{10,11... | collective-permute-start | bytes 3538952 | tf_op jit(solution)/shard_map/ppermute | solution.py:1112
  78.6 15.0 %collective-permute-start.14 = (bf16[4,48,1920]{2,1,0:T(8,128)(2,1)}, bf16[4,48,1920]{2,1,0:T(8,128)(2,1)}, u32[]{:S(2)}, u32[]{:S(2)}) collective-permute-start(bf16[4,48,1920]{2,1,0:T(8,128)(2,1)} %collective-permute-done.10.rest_2_), channel_id=1, source_target_pairs={{0,8},{8,0},{16,24},{24,16},{1,9},{9,1},{17,25},{25,17},{2,10},{10... | collective-permute-start | bytes 2211848 | tf_op jit(solution)/shard_map/ppermute | solution.py:1112
  78.6 15.5 %collective-permute-start.13 = (bf16[4,48,1920]{2,1,0:T(8,128)(2,1)}, bf16[4,48,1920]{2,1,0:T(8,128)(2,1)}, u32[]{:S(2)}, u32[]{:S(2)}) collective-permute-start(bf16[4,48,1920]{2,1,0:T(8,128)(2,1)} %collective-permute-done.9.rest_1_), channel_id=1, source_target_pairs={{0,8},{8,0},{16,24},{24,16},{1,9},{9,1},{17,25},{25,17},{2,10},{10... | collective-permute-start | bytes 2211848 | tf_op jit(solution)/shard_map/ppermute | solution.py:1112
  79.1 15.0 %collective-permute-start.12 = (bf16[4,48,1920]{2,1,0:T(8,128)(2,1)S(1)}, bf16[4,48,1920]{2,1,0:T(8,128)(2,1)}, u32[]{:S(2)}, u32[]{:S(2)}) collective-permute-start(bf16[4,48,1920]{2,1,0:T(8,128)(2,1)S(1)} %pad_maximum_fusion.2.rest_0_), channel_id=1, source_target_pairs={{0,8},{8,0},{16,24},{24,16},{1,9},{9,1},{17,25},{25,17},{2,10},{10... | collective-permute-start | bytes 2211848 | tf_op jit(solution)/shard_map/ppermute | solution.py:1112
  92.0 2.4 copy-start.6
  92.0 2.3 collective-permute-start.15
  93.6 22.4 %collective-permute-start.20 = (bf16[4,192,768]{2,1,0:T(8,128)(2,1)S(1)}, bf16[4,192,768]{2,1,0:T(8,128)(2,1)}, u32[]{:S(2)}, u32[]{:S(2)}) collective-permute-start(bf16[4,192,768]{2,1,0:T(8,128)(2,1)S(1)} %pad_maximum_fusion.b0), channel_id=1, source_target_pairs={{0,8},{8,0},{16,24},{24,16},{1,9},{9,1},{17,25},{25,17},{2,10},{10... | collective-permute-start | bytes 3538952 | tf_op jit(solution)/shard_map/ppermute | solution.py:1112
  115.8 3.1 collective-permute-start.21
  152.6 4.8 %collective-permute-start.22 = (bf16[1,2,4,384,384]{4,3,2,1,0:T(8,128)(2,1)}, bf16[1,2,4,384,384]{4,3,2,1,0:T(8,128)(2,1)S(1)}, u32[]{:S(2)}, u32[]{:S(2)}) collective-permute-start(bf16[1,2,4,384,384]{4,3,2,1,0:T(8,128)(2,1)} %get-tuple-element.99), channel_id=1, source_target_pairs={{0,8},{8,0},{16,24},{24,16},{1,9},{9,1},{17,25},{25,17},{2,10},{10... | collective-permute-start | bytes 7077896 | tf_op jit(solution)/shard_map/ppermute | solution.py:1112
  159.9 28.1 %collective-permute-start.23 = (bf16[4,384,384]{2,1,0:T(8,128)(2,1)S(1)}, bf16[4,384,384]{2,1,0:T(8,128)(2,1)S(1)}, u32[]{:S(2)}, u32[]{:S(2)}) collective-permute-start(bf16[4,384,384]{2,1,0:T(8,128)(2,1)S(1)} %get-tuple-element.195), channel_id=1, source_target_pairs={{0,1},{1,0},{2,3},{3,2},{4,5},{5,4},{6,7},{7,6},{8,9},{9,8},{10,11... | collective-permute-start | bytes 3538952 | tf_op jit(solution)/shard_map/ppermute | solution.py:1112
  184.9 8.1 %copy-start.7 = (bf16[2,2,4,48,1536]{4,3,2,1,0:T(8,128)(2,1)S(1)}, bf16[2,2,4,48,1536]{4,3,2,1,0:T(8,128)(2,1)}, u32[]{:S(2)}) copy-start(bf16[2,2,4,48,1536]{4,3,2,1,0:T(8,128)(2,1)} %get-tuple-element.105) | copy-start | bytes 7077892
  188.2 4.8 %collective-permute-start.24 = (bf16[2,2,4,48,1536]{4,3,2,1,0:T(8,128)(2,1)}, bf16[2,2,4,48,1536]{4,3,2,1,0:T(8,128)(2,1)S(1)}, u32[]{:S(2)}, u32[]{:S(2)}) collective-permute-start(bf16[2,2,4,48,1536]{4,3,2,1,0:T(8,128)(2,1)} %get-tuple-element.107), channel_id=1, source_target_pairs={{0,8},{8,0},{16,24},{24,16},{1,9},{9,1},{17,25},{25,17},{2,10},{10... | collective-permute-start | bytes 7077896 | tf_op jit(solution)/shard_map/ppermute | solution.py:1112
  194.0 31.8 %collective-permute-start.25 = (bf16[2,4,48,1536]{3,2,1,0:T(8,128)(2,1)S(1)}, bf16[2,4,48,1536]{3,2,1,0:T(8,128)(2,1)S(1)}, u32[]{:S(2)}, u32[]{:S(2)}) collective-permute-start(bf16[2,4,48,1536]{3,2,1,0:T(8,128)(2,1)S(1)} %get-tuple-element.193), channel_id=1, source_target_pairs={{0,16},{8,24},{16,0},{24,8},{1,17},{9,25},{17,1},{25,9},{2,18},{10... | collective-permute-start | bytes 3538952 | tf_op jit(solution)/shard_map/ppermute | solution.py:1112
  195.5 28.2 %collective-permute-start.26 = (bf16[384,384]{1,0:T(8,128)(2,1)}, bf16[384,384]{1,0:T(8,128)(2,1)}, u32[]{:S(2)}, u32[]{:S(2)}) collective-permute-start(bf16[384,384]{1,0:T(8,128)(2,1)} %get-tuple-element.203), channel_id=1, source_target_pairs={{0,2},{1,3},{2,0},{3,1},{4,6},{5,7},{6,4},{7,5},{8,10},{9,11},{10,... | collective-permute-start | bytes 884744 | tf_op jit(solution)/shard_map/ppermute | solution.py:1112
  196.3 27.5 %collective-permute-start.27 = (bf16[384,384]{1,0:T(8,128)(2,1)}, bf16[384,384]{1,0:T(8,128)(2,1)}, u32[]{:S(2)}, u32[]{:S(2)}) collective-permute-start(bf16[384,384]{1,0:T(8,128)(2,1)} %get-tuple-element.202), channel_id=1, source_target_pairs={{0,4},{1,5},{2,6},{3,7},{4,0},{5,1},{6,2},{7,3},{8,12},{9,13},{10,... | collective-permute-start | bytes 884744 | tf_op jit(solution)/shard_map/ppermute | solution.py:1112
  198.5 25.3 %collective-permute-start.28 = (bf16[384,384]{1,0:T(8,128)(2,1)S(1)}, bf16[384,384]{1,0:T(8,128)(2,1)}, u32[]{:S(2)}, u32[]{:S(2)}) collective-permute-start(bf16[384,384]{1,0:T(8,128)(2,1)S(1)} %get-tuple-element.201), channel_id=1, source_target_pairs={{0,6},{1,7},{2,4},{3,5},{4,2},{5,3},{6,0},{7,1},{8,14},{9,15},{10,... | collective-permute-start | bytes 884744 | tf_op jit(solution)/shard_map/ppermute | solution.py:1112
  226.1 5.1 %collective-permute-start.29 = (bf16[2,2,4,48,1152]{4,3,2,1,0:T(8,128)(2,1)}, bf16[2,2,4,48,1152]{4,3,2,1,0:T(8,128)(2,1)}, u32[]{:S(2)}, u32[]{:S(2)}) collective-permute-start(bf16[2,2,4,48,1152]{4,3,2,1,0:T(8,128)(2,1)} %get-tuple-element.116), channel_id=1, source_target_pairs={{0,8},{8,0},{16,24},{24,16},{1,9},{9,1},{17,25},{25,17},{2,10},{10... | collective-permute-start | bytes 5308424 | tf_op jit(solution)/shard_map/ppermute | solution.py:1112
  228.1 20.4 %collective-permute-start.32 = (bf16[384,384]{1,0:T(8,128)(2,1)}, bf16[384,384]{1,0:T(8,128)(2,1)S(1)}, u32[]{:S(2)}, u32[]{:S(2)}) collective-permute-start(bf16[384,384]{1,0:T(8,128)(2,1)} %add_convert_fusion.11), channel_id=1, source_target_pairs={{0,16},{8,24},{16,0},{24,8},{1,17},{9,25},{17,1},{25,9},{2,18},{10... | collective-permute-start | bytes 884744 | tf_op jit(solution)/shard_map/ppermute | solution.py:1112
  230.5 20.4 %collective-permute-start.31 = (bf16[4,48,1536]{2,1,0:T(8,128)(2,1)}, bf16[4,48,1536]{2,1,0:T(8,128)(2,1)}, u32[]{:S(2)}, u32[]{:S(2)}) collective-permute-start(bf16[4,48,1536]{2,1,0:T(8,128)(2,1)} %get-tuple-element.199), channel_id=1, source_target_pairs={{0,1},{1,0},{2,3},{3,2},{4,5},{5,4},{6,7},{7,6},{8,9},{9,8},{10,11... | collective-permute-start | bytes 1769480 | tf_op jit(solution)/shard_map/ppermute | solution.py:1112
  249.5 6.2 %collective-permute-start.52 = (bf16[384,384]{1,0:T(8,128)(2,1)S(1)}, bf16[384,384]{1,0:T(8,128)(2,1)S(1)}, u32[]{:S(2)}, u32[]{:S(2)}) collective-permute-start(bf16[384,384]{1,0:T(8,128)(2,1)S(1)} %add_convert_fusion.10), channel_id=1, source_target_pairs={{0,8},{8,0},{16,24},{24,16},{1,9},{9,1},{17,25},{25,17},{2,10},{10... | collective-permute-start | bytes 884744 | tf_op jit(solution)/shard_map/ppermute | solution.py:1112
  249.6 7.7 %collective-permute-start.30 = (bf16[2,2,4,48,512]{4,3,2,1,0:T(8,128)(2,1)}, bf16[2,2,4,48,512]{4,3,2,1,0:T(8,128)(2,1)S(1)}, u32[]{:S(2)}, u32[]{:S(2)}) collective-permute-start(bf16[2,2,4,48,512]{4,3,2,1,0:T(8,128)(2,1)} %get-tuple-element.125), channel_id=1, source_target_pairs={{0,8},{8,0},{16,24},{24,16},{1,9},{9,1},{17,25},{25,17},{2,10},{10... | collective-permute-start | bytes 2359304 | tf_op jit(solution)/shard_map/ppermute | solution.py:1112
  250.3 21.8 %collective-permute-start.33 = (bf16[2,4,48,1152]{3,2,1,0:T(8,128)(2,1)S(1)}, bf16[2,4,48,1152]{3,2,1,0:T(8,128)(2,1)}, u32[]{:S(2)}, u32[]{:S(2)}) collective-permute-start(bf16[2,4,48,1152]{3,2,1,0:T(8,128)(2,1)S(1)} %get-tuple-element.197), channel_id=1, source_target_pairs={{0,16},{8,24},{16,0},{24,8},{1,17},{9,25},{17,1},{25,9},{2,18},{10... | collective-permute-start | bytes 2654216 | tf_op jit(solution)/shard_map/ppermute | solution.py:1112
  252.1 5.2 %copy-start.9 = (bf16[2,2,4,48,512]{4,3,2,1,0:T(8,128)(2,1)S(1)}, bf16[2,2,4,48,512]{4,3,2,1,0:T(8,128)(2,1)}, u32[]{:S(2)}) copy-start(bf16[2,2,4,48,512]{4,3,2,1,0:T(8,128)(2,1)} %get-tuple-element.124) | copy-start | bytes 2359300
  252.8 20.6 %collective-permute-start.34 = (bf16[48,1536]{1,0:T(8,128)(2,1)}, bf16[48,1536]{1,0:T(8,128)(2,1)}, u32[]{:S(2)}, u32[]{:S(2)}) collective-permute-start(bf16[48,1536]{1,0:T(8,128)(2,1)} %get-tuple-element.215), channel_id=1, source_target_pairs={{0,2},{1,3},{2,0},{3,1},{4,6},{5,7},{6,4},{7,5},{8,10},{9,11},{10,... | collective-permute-start | bytes 442376 | tf_op jit(solution)/shard_map/ppermute | solution.py:1112
  254.5 18.9 %collective-permute-start.35 = (bf16[48,1536]{1,0:T(8,128)(2,1)S(1)}, bf16[48,1536]{1,0:T(8,128)(2,1)}, u32[]{:S(2)}, u32[]{:S(2)}) collective-permute-start(bf16[48,1536]{1,0:T(8,128)(2,1)S(1)} %get-tuple-element.214), channel_id=1, source_target_pairs={{0,4},{1,5},{2,6},{3,7},{4,0},{5,1},{6,2},{7,3},{8,12},{9,13},{10,... | collective-permute-start | bytes 442376 | tf_op jit(solution)/shard_map/ppermute | solution.py:1112
  255.7 17.7 %collective-permute-start.36 = (bf16[48,1536]{1,0:T(8,128)(2,1)S(1)}, bf16[48,1536]{1,0:T(8,128)(2,1)}, u32[]{:S(2)}, u32[]{:S(2)}) collective-permute-start(bf16[48,1536]{1,0:T(8,128)(2,1)S(1)} %get-tuple-element.213), channel_id=1, source_target_pairs={{0,6},{1,7},{2,4},{3,5},{4,2},{5,3},{6,0},{7,1},{8,14},{9,15},{10,... | collective-permute-start | bytes 442376 | tf_op jit(solution)/shard_map/ppermute | solution.py:1112
  267.9 10.2 %collective-permute-start.37 = (bf16[2,4,48,512]{3,2,1,0:T(8,128)(2,1)S(1)}, bf16[2,4,48,512]{3,2,1,0:T(8,128)(2,1)S(1)}, u32[]{:S(2)}, u32[]{:S(2)}) collective-permute-start(bf16[2,4,48,512]{3,2,1,0:T(8,128)(2,1)S(1)} %get-tuple-element.207), channel_id=1, source_target_pairs={{0,1},{1,0},{2,3},{3,2},{4,5},{5,4},{6,7},{7,6},{8,9},{9,8},{10,11... | collective-permute-start | bytes 1179656 | tf_op jit(solution)/shard_map/ppermute | solution.py:1112
  278.2 6.2 %collective-permute-start.40 = (bf16[48,1536]{1,0:T(8,128)(2,1)S(1)}, bf16[48,1536]{1,0:T(8,128)(2,1)S(1)}, u32[]{:S(2)}, u32[]{:S(2)}) collective-permute-start(bf16[48,1536]{1,0:T(8,128)(2,1)S(1)} %add_convert_fusion.13), channel_id=1, source_target_pairs={{0,16},{8,24},{16,0},{24,8},{1,17},{9,25},{17,1},{25,9},{2,18},{10... | collective-permute-start | bytes 442376 | tf_op jit(solution)/shard_map/ppermute | solution.py:1112
  279.6 6.9 %collective-permute-start.39 = (bf16[4,48,512]{2,1,0:T(8,128)(2,1)S(1)}, bf16[4,48,512]{2,1,0:T(8,128)(2,1)S(1)}, u32[]{:S(2)}, u32[]{:S(2)}) collective-permute-start(bf16[4,48,512]{2,1,0:T(8,128)(2,1)S(1)} %get-tuple-element.223), channel_id=1, source_target_pairs={{0,16},{8,24},{16,0},{24,8},{1,17},{9,25},{17,1},{25,9},{2,18},{10... | collective-permute-start | bytes 589832 | tf_op jit(solution)/shard_map/ppermute | solution.py:1112
  280.5 9.8 %collective-permute-start.38 = (bf16[4,48,1152]{2,1,0:T(8,128)(2,1)S(1)}, bf16[4,48,1152]{2,1,0:T(8,128)(2,1)S(1)}, u32[]{:S(2)}, u32[]{:S(2)}) collective-permute-start(bf16[4,48,1152]{2,1,0:T(8,128)(2,1)S(1)} %get-tuple-element.205), channel_id=1, source_target_pairs={{0,1},{1,0},{2,3},{3,2},{4,5},{5,4},{6,7},{7,6},{8,9},{9,8},{10,11... | collective-permute-start | bytes 1327112 | tf_op jit(solution)/shard_map/ppermute | solution.py:1112
  290.4 5.9 %collective-permute-start.46 = (bf16[48,512]{1,0:T(8,128)(2,1)S(1)}, bf16[48,512]{1,0:T(8,128)(2,1)S(1)}, u32[]{:S(2)}, u32[]{:S(2)}) collective-permute-start(bf16[48,512]{1,0:T(8,128)(2,1)S(1)} %get-tuple-element.233), channel_id=1, source_target_pairs={{0,2},{1,3},{2,0},{3,1},{4,6},{5,7},{6,4},{7,5},{8,10},{9,11},{10,... | collective-permute-start | bytes 147464 | tf_op jit(solution)/shard_map/ppermute | solution.py:1112
  291.1 5.2 %collective-permute-start.47 = (bf16[48,512]{1,0:T(8,128)(2,1)S(1)}, bf16[48,512]{1,0:T(8,128)(2,1)S(1)}, u32[]{:S(2)}, u32[]{:S(2)}) collective-permute-start(bf16[48,512]{1,0:T(8,128)(2,1)S(1)} %get-tuple-element.232), channel_id=1, source_target_pairs={{0,4},{1,5},{2,6},{3,7},{4,0},{5,1},{6,2},{7,3},{8,12},{9,13},{10,... | collective-permute-start | bytes 147464 | tf_op jit(solution)/shard_map/ppermute | solution.py:1112
  293.4 5.9 %collective-permute-start.48 = (bf16[48,512]{1,0:T(8,128)(2,1)S(1)}, bf16[48,512]{1,0:T(8,128)(2,1)S(1)}, u32[]{:S(2)}, u32[]{:S(2)}) collective-permute-start(bf16[48,512]{1,0:T(8,128)(2,1)S(1)} %get-tuple-element.231), channel_id=1, source_target_pairs={{0,6},{1,7},{2,4},{3,5},{4,2},{5,3},{6,0},{7,1},{8,14},{9,15},{10,... | collective-permute-start | bytes 147464 | tf_op jit(solution)/shard_map/ppermute | solution.py:1112
  296.4 18.6 %collective-permute-start.51 = (bf16[48,3072]{1,0:T(8,128)(2,1)S(1)}, bf16[48,3072]{1,0:T(8,128)(2,1)S(1)}, u32[]{:S(2)}, u32[]{:S(2)}) collective-permute-start(bf16[48,3072]{1,0:T(8,128)(2,1)S(1)} %pad_maximum_fusion.3), channel_id=1, source_target_pairs={{0,8},{8,0},{16,24},{24,16},{1,9},{9,1},{17,25},{25,17},{2,10},{10... | collective-permute-start | bytes 884744 | tf_op jit(solution)/shard_map/ppermute | solution.py:1112
  299.4 5.8 %collective-permute-start.49 = (bf16[48,512]{1,0:T(8,128)(2,1)S(1)}, bf16[48,512]{1,0:T(8,128)(2,1)S(1)}, u32[]{:S(2)}, u32[]{:S(2)}) collective-permute-start(bf16[48,512]{1,0:T(8,128)(2,1)S(1)} %add_convert_fusion.15), channel_id=1, source_target_pairs={{0,16},{8,24},{16,0},{24,8},{1,17},{9,25},{17,1},{25,9},{2,18},{10... | collective-permute-start | bytes 147464 | tf_op jit(solution)/shard_map/ppermute | solution.py:1112
  300.7 6.3 %collective-permute-start.41 = (bf16[48,1152]{1,0:T(8,128)(2,1)S(1)}, bf16[48,1152]{1,0:T(8,128)(2,1)S(1)}, u32[]{:S(2)}, u32[]{:S(2)}) collective-permute-start(bf16[48,1152]{1,0:T(8,128)(2,1)S(1)} %get-tuple-element.221), channel_id=1, source_target_pairs={{0,2},{1,3},{2,0},{3,1},{4,6},{5,7},{6,4},{7,5},{8,10},{9,11},{10,... | collective-permute-start | bytes 331784 | tf_op jit(solution)/shard_map/ppermute | solution.py:1112
  300.7 9.2 %collective-permute-start.42 = (bf16[48,1152]{1,0:T(8,128)(2,1)S(1)}, bf16[48,1152]{1,0:T(8,128)(2,1)S(1)}, u32[]{:S(2)}, u32[]{:S(2)}) collective-permute-start(bf16[48,1152]{1,0:T(8,128)(2,1)S(1)} %get-tuple-element.220), channel_id=1, source_target_pairs={{0,4},{1,5},{2,6},{3,7},{4,0},{5,1},{6,2},{7,3},{8,12},{9,13},{10,... | collective-permute-start | bytes 331784 | tf_op jit(solution)/shard_map/ppermute | solution.py:1112
  302.7 7.2 %collective-permute-start.43 = (bf16[48,1152]{1,0:T(8,128)(2,1)S(1)}, bf16[48,1152]{1,0:T(8,128)(2,1)S(1)}, u32[]{:S(2)}, u32[]{:S(2)}) collective-permute-start(bf16[48,1152]{1,0:T(8,128)(2,1)S(1)} %get-tuple-element.219), channel_id=1, source_target_pairs={{0,6},{1,7},{2,4},{3,5},{4,2},{5,3},{6,0},{7,1},{8,14},{9,15},{10,... | collective-permute-start | bytes 331784 | tf_op jit(solution)/shard_map/ppermute | solution.py:1112
  305.1 5.7 %collective-permute-start.50 = (bf16[48,1024]{1,0:T(8,128)(2,1)S(1)}, bf16[48,1024]{1,0:T(8,128)(2,1)S(1)}, u32[]{:S(2)}, u32[]{:S(2)}) collective-permute-start(bf16[48,1024]{1,0:T(8,128)(2,1)S(1)} %pad_maximum_fusion.6), channel_id=1, source_target_pairs={{0,8},{8,0},{16,24},{24,16},{1,9},{9,1},{17,25},{25,17},{2,10},{10... | collective-permute-start | bytes 294920 | tf_op jit(solution)/shard_map/ppermute | solution.py:1112
  310.0 4.8 %collective-permute-start.44 = (bf16[48,1152]{1,0:T(8,128)(2,1)S(1)}, bf16[48,1152]{1,0:T(8,128)(2,1)S(1)}, u32[]{:S(2)}, u32[]{:S(2)}) collective-permute-start(bf16[48,1152]{1,0:T(8,128)(2,1)S(1)} %add_convert_fusion.14), channel_id=1, source_target_pairs={{0,16},{8,24},{16,0},{24,8},{1,17},{9,25},{17,1},{25,9},{2,18},{10... | collective-permute-start | bytes 331784 | tf_op jit(solution)/shard_map/ppermute | solution.py:1112
  314.8 1.5 collective-permute-start.45
  316.5 1.8 copy-start.1
  (3 other events, 2.8 us)

commit v3 on v2

--- a/solution.py
+++ b/solution.py
@@ -115,71 +115,6 @@
     )
 
 
-def attend_forward(tokens, counts, ids, bufs, sentences, length):
-    rows, width = tokens.shape
-    pairs = width // 128
-    group = 256
-
-    def body(ids_ref, counts_ref, x_ref, b0, b1, b2, b3, qkv_ref, ctx_ref, lse_ref, vec_ref, w_ref, sems):
-        place = Place(ids_ref)
-        copies = piece_copies(place, (b0, b1, b2, b3), w_ref, sems, width // 8, False)
-        for copy in copies:
-            copy.start()
-        for copy in copies:
-            copy.wait()
-        vec_ref[...] = w_ref[:, 3 * width :].astype(F32).T[: vec_ref.shape[0]]
-        x = x_ref[...]
-        for part in range(3):
-            for g in range(width // group):
-                col = part * width + g * group
-                y = dot(x, w_ref[:, col : col + group])
-                if part != 1:
-                    bias = vec_ref[part // 2 : part // 2 + 1, g * group : (g + 1) * group]
-                    y = y + bias
-                qkv_ref[:, col : col + group] = y.astype(BF)
-
-        def sentence(s, carry):
-            row = aligned(s * length, length)
-            count = counts_ref[s]
-            lane = lax.broadcasted_iota(jnp.int32, (length, 128), 1)
-            lse_all = jnp.zeros((length, 128), F32)
-            for p in range(pairs):
-                here = pl.ds(row, length)
-                query = qkv_ref[here, p * 128 : (p + 1) * 128] * jnp.asarray(HEAD**-0.5, BF)
-                keys2 = two_heads(qkv_ref[here, width + p * 128 : width + (p + 1) * 128])
-                values2 = two_heads(qkv_ref[here, 2 * width + p * 128 : 2 * width + (p + 1) * 128])
-                scores = masked_scores(query, keys2, count, length)
-                a, b = scores[:, :length], scores[:, length:]
-                max_a = jnp.max(a, -1, keepdims=True)
-                max_b = jnp.max(b, -1, keepdims=True)
-                e_a, e_b = jnp.exp(a - max_a), jnp.exp(b - max_b)
-                sum_a = jnp.sum(e_a, -1, keepdims=True)
-                sum_b = jnp.sum(e_b, -1, keepdims=True)
-                lse_all = jnp.where(lane == 2 * p, max_a + jnp.log(sum_a), lse_all)
-                lse_all = jnp.where(lane == 2 * p + 1, max_b + jnp.log(sum_b), lse_all)
-                probs = jnp.concatenate([e_a * (1.0 / sum_a), e_b * (1.0 / sum_b)], axis=1).astype(BF)
-                ctx_ref[here, p * 128 : (p + 1) * 128] = dot(probs, values2).astype(BF)
-            lse_ref[pl.ds(row, length), :] = lse_all
-            return carry
-
-        lax.fori_loop(0, sentences, sentence, 0)
-
-    return call(
-        body,
-        "qkv_attention",
-        [(ids, "s"), (counts, "s"), (tokens, "v")] + [(b, "a") for b in bufs],
-        [
-            struct((rows, 3 * width), BF),
-            struct((rows, width), BF),
-            struct((rows, 128), F32),
-            struct((16, width), F32),
-        ],
-        [pltpu.VMEM((width, 3 * width + 128), BF), pltpu.SemaphoreType.DMA((16,))],
-        2 * rows * width * 3 * width + 8 * rows * length * width,
-        rows * length * width // HEAD,
-    )
-
-
 def layer_norm(v):
     centred = v - jnp.mean(v, -1, keepdims=True)
     inverse = lax.rsqrt(jnp.mean(centred * centred, -1, keepdims=True) + NORM_EPS)
@@ -197,62 +132,6 @@
 
 def row(vec_ref, at):
     return vec_ref[at : at + 1, :]
-
-
-def up_forward(context, tokens, vec, bias_in, ids, bufs, length):
-    rows, width = tokens.shape
-    wide = bias_in.shape[1]
-    group = 256
-
-    def body(ids_ref, ctx_ref, x_ref, vec_ref, bin_ref, *rest):
-        bufs_ref = rest[: len(bufs)]
-        n_ref, inv_ref, low_ref, act_ref, slope_ref, w_ref, sems = rest[len(bufs) :]
-        place = Place(ids_ref)
-        copies = piece_copies(place, bufs_ref, w_ref, sems, width // 8, True)
-        for copy in copies:
-            copy.start()
-        for copy in copies:
-            copy.wait()
-        n_ref[...] = dot(ctx_ref[...], w_ref[:, :width])
-
-        def norm_rows(s, carry):
-            here = pl.ds(aligned(s * length, length), length)
-            v = x_ref[here, :].astype(F32) + (n_ref[here, :] + row(vec_ref, 2))
-            normed, inverse = layer_norm(v)
-            n_ref[here, :] = normed
-            inv_ref[here, :] = jnp.broadcast_to(inverse, (length, 128))
-            low_ref[here, :] = (normed * row(vec_ref, 3) + row(vec_ref, 4)).astype(BF)
-            return carry
-
-        lax.fori_loop(0, rows // length, norm_rows, 0)
-
-        def columns(g, carry):
-            col = aligned(g * group, group)
-            u = dot(low_ref[...], w_ref[:, pl.ds(width + col, group)]) + bin_ref[:, pl.ds(col, group)]
-            cdf = 0.5 * (1.0 + lax.erf(u * (0.5**0.5)))
-            pdf = jnp.exp(-0.5 * u * u) * 0.3989422804014327
-            act_ref[:, pl.ds(col, group)] = (u * cdf).astype(BF)
-            slope_ref[:, pl.ds(col, group)] = (cdf + u * pdf).astype(BF)
-            return carry
-
-        lax.fori_loop(0, wide // group, columns, 0)
-
-    return call(
-        body,
-        "out_norm_up",
-        [(ids, "s"), (context, "v"), (tokens, "v"), (vec, "v"), (bias_in, "v")]
-        + [(b, "a") for b in bufs],
-        [
-            struct((rows, width), F32),
-            struct((rows, 128), F32),
-            struct((rows, width), BF),
-            struct((rows, wide), BF),
-            struct((rows, wide), BF),
-        ],
-        [pltpu.VMEM((width, width + wide), BF), pltpu.SemaphoreType.DMA((32,))],
-        2 * rows * width * (width + wide),
-        2 * rows * wide,
-    )
 
 
 def grid_call(body, name, grid, scalars, ins, outs, scratch, flops, transcendentals=0):
@@ -288,6 +167,177 @@
 
 def left(array):
     return (array, None, None)
+
+
+def qkv_forward(tokens, ids, bufs):
+    rows, width = tokens.shape
+    group = 256
+
+    def body(ids_ref, x_ref, b0, b1, b2, b3, qkv_hbm, vec_ref, w_ref, out_ref, sems, more):
+        place = Place(ids_ref)
+        copies = piece_copies(place, (b0, b1, b2, b3), w_ref, sems, width // 8, False)
+        for copy in copies:
+            copy.start()
+        for copy in copies:
+            copy.wait()
+        vec_ref[...] = w_ref[:, 3 * width :].astype(F32).T[: vec_ref.shape[0]]
+        x = x_ref[...]
+        outs = []
+        for part in range(3):
+            for g in range(width // group):
+                col = part * width + g * group
+                y = dot(x, w_ref[:, col : col + group])
+                if part != 1:
+                    bias = vec_ref[part // 2 : part // 2 + 1, g * group : (g + 1) * group]
+                    y = y + bias
+                out_ref[:, col : col + group] = y.astype(BF)
+            here = slice(part * width, (part + 1) * width)
+            outs.append(
+                pltpu.make_async_copy(out_ref.at[:, here], qkv_hbm.at[:, here], more.at[part])
+            )
+            outs[-1].start()
+        for out in outs:
+            out.wait()
+
+    return grid_call(
+        body,
+        "qkv",
+        (1,),
+        (ids,),
+        [whole(tokens)] + [left(b) for b in bufs],
+        [left(struct((rows, 3 * width), BF)), whole(struct((16, width), F32))],
+        [
+            pltpu.VMEM((width, 3 * width + 128), BF),
+            pltpu.VMEM((rows, 3 * width), BF),
+            pltpu.SemaphoreType.DMA((16,)),
+            pltpu.SemaphoreType.DMA((3,)),
+        ],
+        2 * rows * width * 3 * width,
+    )
+
+
+def attend_forward(qkv, counts, sentences, length):
+    rows, width = qkv.shape[0], qkv.shape[1] // 3
+    pairs = width // 128
+
+    def body(counts_ref, qkv_ref, ctx_ref, lse_ref):
+        count = counts_ref[pl.program_id(0)]
+        lane = lax.broadcasted_iota(jnp.int32, (length, 128), 1)
+        lse_all = jnp.zeros((length, 128), F32)
+        for p in range(pairs):
+            query = qkv_ref[:, p * 128 : (p + 1) * 128] * jnp.asarray(HEAD**-0.5, BF)
+            keys2 = two_heads(qkv_ref[:, width + p * 128 : width + (p + 1) * 128])
+            values2 = two_heads(qkv_ref[:, 2 * width + p * 128 : 2 * width + (p + 1) * 128])
+            scores = masked_scores(query, keys2, count, length)
+            a, b = scores[:, :length], scores[:, length:]
+            max_a = jnp.max(a, -1, keepdims=True)
+            max_b = jnp.max(b, -1, keepdims=True)
+            e_a, e_b = jnp.exp(a - max_a), jnp.exp(b - max_b)
+            sum_a = jnp.sum(e_a, -1, keepdims=True)
+            sum_b = jnp.sum(e_b, -1, keepdims=True)
+            lse_all = jnp.where(lane == 2 * p, max_a + jnp.log(sum_a), lse_all)
+            lse_all = jnp.where(lane == 2 * p + 1, max_b + jnp.log(sum_b), lse_all)
+            probs = jnp.concatenate([e_a * (1.0 / sum_a), e_b * (1.0 / sum_b)], axis=1).astype(BF)
+            ctx_ref[:, p * 128 : (p + 1) * 128] = dot(probs, values2).astype(BF)
+        lse_ref[...] = lse_all
+
+    def by_rows(array):
+        return (array, (length, array.shape[1]), lambda s, counts: (s, 0))
+
+    return grid_call(
+        body,
+        "attention",
+        (sentences,),
+        (counts,),
+        [by_rows(qkv)],
+        [by_rows(struct((rows, width), BF)), by_rows(struct((rows, 128), F32))],
+        [],
+        8 * rows * length * width,
+        rows * length * width // HEAD,
+    )
+
+
+CHUNK = 128
+
+
+def up_forward(context, tokens, vec, bias_in, ids, bufs, length):
+    rows, width = tokens.shape
+    wide = bias_in.shape[1]
+    group, block = 256, 512
+    steps = wide // block
+
+    def body(ids_ref, ctx_ref, x_ref, vec_ref, bin_ref, *rest):
+        bufs_ref = rest[: len(bufs)]
+        act_ref, slope_ref, n_hbm, inv_hbm, low_hbm, w_ref, n_ref, inv_ref, low_ref, sems, more = rest[len(bufs) :]
+        step = pl.program_id(0)
+        outs = [
+            pltpu.make_async_copy(a, b, more.at[i])
+            for i, (a, b) in enumerate(((n_ref, n_hbm), (inv_ref, inv_hbm), (low_ref, low_hbm)))
+        ]
+
+        @pl.when(step == 0)
+        def _():
+            copies = piece_copies(Place(ids_ref), bufs_ref, w_ref, sems, width // 8, True)
+            for copy in copies:
+                copy.start()
+            for copy in copies:
+                copy.wait()
+            for g in range(width // group):
+                cols = slice(g * group, (g + 1) * group)
+                n_ref[:, cols] = dot(ctx_ref[...], w_ref[:, cols])
+
+            def norm_rows(i, carry):
+                here = pl.ds(aligned(i * CHUNK, CHUNK), CHUNK)
+                v = x_ref[here, :].astype(F32) + (n_ref[here, :] + row(vec_ref, 2))
+                normed, inverse = layer_norm(v)
+                n_ref[here, :] = normed
+                inv_ref[here, :] = jnp.broadcast_to(inverse, (CHUNK, 128))
+                low_ref[here, :] = (normed * row(vec_ref, 3) + row(vec_ref, 4)).astype(BF)
+                return carry
+
+            lax.fori_loop(0, rows // CHUNK, norm_rows, 0)
+            for out in outs:
+                out.start()
+
+        for g in range(block // group):
+            cols = slice(g * group, (g + 1) * group)
+            here = pl.ds(aligned(width + step * block + g * group, 128), group)
+            u = dot(low_ref[...], w_ref[:, here]) + bin_ref[:, cols]
+            cdf = 0.5 * (1.0 + lax.erf(u * (0.5**0.5)))
+            pdf = jnp.exp(-0.5 * u * u) * 0.3989422804014327
+            act_ref[:, cols] = (u * cdf).astype(BF)
+            slope_ref[:, cols] = (cdf + u * pdf).astype(BF)
+
+        @pl.when(step == steps - 1)
+        def _():
+            for out in outs:
+                out.wait()
+
+    active, slope, normed, inverse, low = grid_call(
+        body,
+        "out_norm_up",
+        (steps,),
+        (ids,),
+        [whole(context), whole(tokens), whole(vec), (bias_in, (1, block), lambda j, ids: (0, j))]
+        + [left(b) for b in bufs],
+        [
+            (struct((rows, wide), BF), (rows, block), lambda j, ids: (0, j)),
+            (struct((rows, wide), BF), (rows, block), lambda j, ids: (0, j)),
+            left(struct((rows, width), F32)),
+            left(struct((rows, 128), F32)),
+            left(struct((rows, width), BF)),
+        ],
+        [
+            pltpu.VMEM((width, width + wide), BF),
+            pltpu.VMEM((rows, width), F32),
+            pltpu.VMEM((rows, 128), F32),
+            pltpu.VMEM((rows, width), BF),
+            pltpu.SemaphoreType.DMA((32,)),
+            pltpu.SemaphoreType.DMA((3,)),
+        ],
+        2 * rows * width * (width + wide),
+    )
+    return normed, inverse, low, active, slope
 
 
 def relative(ids, step):
@@ -684,7 +734,7 @@
     group = 256
     first = gqkv.shape[1] // group
     groups = first + 1
-    cut, ratio = vg_a.shape[1], gbias_in.shape[0]
+    cut, ratio, part = vg_a.shape[1], gbias_in.shape[1] // width, width // 8
 
     def body(ids_ref, gqkv_ref, x_ref, va_ref, vb_ref, attn_ref, ffn_ref, bias_ref, send_ref, keep_ref, t_ref, x_t, r_ref, v_ref):
         j = pl.program_id(0)
@@ -708,7 +758,10 @@
             r_ref[3:5, :] = attn_ref[0:2, :]
             r_ref[5:6, :] = ffn_ref[2:3, :]
             r_ref[6:8, :] = ffn_ref[0:2, :]
-            r_ref[8 : 8 + ratio, :] = bias_ref[...]
+            for shard in range(8):
+                for i in range(ratio):
+                    at = (shard * ratio + i) * part
+                    r_ref[8 + i : 9 + i, shard * part : (shard + 1) * part] = bias_ref[:, at : at + part]
             v_ref[0] = r_ref[...].T
             put_relative(place, v_ref.at[0], v_ref.at[1])
             both = jnp.concatenate([v_ref[1], jnp.zeros((width, group - 128), F32)], axis=1)
@@ -1139,12 +1192,12 @@
     return add(hold(total[0], *after), swap(total[1], "fsdp", 1))
 
 
-def sum_y_first(total, *after):
-    return add(hold(total[:, 0], *after), swap(total[:, 1], "fsdp", 1))
-
-
 def sum_z(total, *after):
     return add(hold(total[0], *after), *[swap(total[k], "fsdp", 2 * k) for k in range(1, 4)])
+
+
+def in_order_parts(own, other, bit):
+    return jnp.where(bit == 0, own, other), jnp.where(bit == 0, other, own)
 
 
 def in_order(own, other, bit, axis):
@@ -1201,15 +1254,15 @@
     near2 = gather_z(hold(second, near1))
     far1 = hold(swap(near1, "fsdp", 1), near2)
     bufs1 = [near1, far1, swap(near1, "dp", 1), swap(far1, "dp", 1)]
-    qkv, context, lse, vec = attend_forward(
-        hold(token_rows, near2), lengths, ids, bufs1, sentences, length
-    )
-    near3 = gather_z(hold(third, near2), vec)
+    side2 = swap(near2, "dp", 2)
+    qkv, vec = qkv_forward(hold(token_rows, near2), ids, bufs1)
     far2 = hold(swap(near2, "fsdp", 1), vec)
-    side2 = hold(swap(near2, "dp", 2), vec)
+    context, lse = attend_forward(hold(qkv, side2), lengths, sentences, length)
+    near3 = gather_z(hold(third, near2), context)
+    side2 = hold(side2, context)
     far3 = swap(near3, "fsdp", 1)
     mine2 = [near2, far2, side2, swap(far2, "dp", 2)]
-    bufs2 = mine2 + [swap(hold(m, vec), "dp", 1) for m in mine2]
+    bufs2 = mine2 + [swap(hold(m, context), "dp", 1) for m in mine2]
     ratio = wide // width
     bias_up = vec[8 : 8 + ratio].reshape(ratio, 8, part).transpose(1, 0, 2).reshape(1, wide)
     normed, inverse, low, active, slope = up_forward(
@@ -1220,12 +1273,11 @@
     pooled, vg_ffn, send3, keep3, gup, gbias_in, gres = down_and_back(
         active, slope, normed, vec, lengths, pooled_grad, ids, bufs3, sentences, length
     )
-    sums3 = sum_core(send3, keep3)
     send2, keep2, gctx, vg_attn, gattn, gattn_low = up_and_back(
-        low, hold(gup, sums3), gres, normed, inverse, vec, ids, bufs2, length
-    )
-    sums3 = sum_y(sums3[0], gctx)
-    sums2 = sum_core(hold(send2, gctx, sums3), keep2)
+        low, gup, gres, normed, inverse, vec, ids, bufs2, length
+    )
+    sums3 = sum_core(send3, keep3, gctx)
+    sums2 = sum_core(send2, keep2, sums3)
     pairs = width // 128
     most = pairs * 2 // 3
     gqkv_a, vg_a = attend_backward(
@@ -1233,31 +1285,32 @@
     )
     send_a, keep_a = attend_weight(gqkv_a, token_rows, context, gattn_low, ids)
     sums2 = sum_x(sums2, keep_a)
-    sums3 = sum_z(sums3, keep_a)
+    sums3 = sum_y(sums3[0], keep_a)
     sums_a = sum_core(hold(send_a, sums2, sums3), keep_a)
     gqkv_b, vg_b = attend_backward(
         qkv, hold(gctx, sums_a), lse, lengths, sentences, length, most, pairs, "attention_back_rest"
     )
-    gbias_in = gbias_in.reshape(8, ratio, part).transpose(1, 0, 2).reshape(ratio, width)
     send_b, keep_b = last_weight(gqkv_b, token_rows, vg_a, vg_b, vg_attn, vg_ffn, gbias_in, ids)
-    sums2 = sum_y(sums2, gqkv_b)
-    sums3 = add(hold(sums3, keep_b), swap(sums3, "dp", 2))
-    sums_b = sum_core(send_b, keep_b)
+    sums2 = sum_y(sums2, keep_b)
+    sums3 = sum_z(sums3, keep_b)
+    sums_a = sum_x(sums_a, keep_b)
+    sums_b = sum_core(hold(send_b, sums_a), keep_b)
     gtokens = tokens_backward(gqkv_a, hold(gqkv_b, sums_b, sums2, sums3), gattn, ids, bufs1)
-    sums_a = sum_x(sums_a, gtokens)
-    sums2 = sum_z(sums2, sums_a)
-    sums_b = sum_y_first(sums_b, sums2)
-    sums_a, sums2, sums_b = lax.optimization_barrier((sums_a, sums2, sums_b))
-    sums_a = sum_y(sums_a)
-    sums_b = sum_x(sums_b)
+    sums2 = sum_z(sums2, gtokens)
+    sums_b = sum_x(sums_b, sums2)
+    sums_a = sum_y(sums_a, sums2)
+    sums3 = add(hold(sums3, sums2), swap(sums3, "dp", 2))
+    sums_a, sums2, sums3, sums_b = lax.optimization_barrier((sums_a, sums2, sums3, sums_b))
+    sums_b = sum_y(sums_b)
     g_in = in_order(sums2, swap(sums2, "dp", 2), x, 1)
-    sums_a, sums_b, g_in = lax.optimization_barrier((sums_a, sums_b, g_in))
+    sums_a, sums3, sums_b, g_in = lax.optimization_barrier((sums_a, sums3, sums_b, g_in))
     g_down = share_core(sums3, c).T
     g_in = share_core(g_in, c)
-    sums_a = sum_z(sums_a)
-    sums_b = sum_z(sums_b)
-    g_b = share_core(in_order(sums_b, swap(sums_b, "dp", 2), x, 1), c)
-    g_a = share_core(in_order(sums_a, swap(sums_a, "dp", 2), x, 1), c)
+    sums = sum_z(jnp.concatenate([sums_a, sums_b], 2))
+    wide_a = sums_a.shape[2]
+    sums, other = in_order_parts(sums, swap(sums, "dp", 2), x)
+    g_a = share_core(jnp.concatenate([sums[:, :wide_a], other[:, :wide_a]], 1), c)
+    g_b = share_core(jnp.concatenate([sums[:, wide_a:], other[:, wide_a:]], 1), c)
     gtokens = gtokens.reshape(sentences, length, width)
     cut_a, cut_b = most * 128, (pairs - most) * 128
     g_qkv = [

time: 320 us -> 306 us (0.956)
  waiting for transfers between devices: 85.4 us -> 67.9 us
  starting transfers between devices: 56 us -> 61.1 us
    pallas_call x6 -> x9, Pallas kernels: 95.7 us -> 134 us  [grid_call(): pl.pallas_call(body, name=name, out_shape=tuple((o for o, _, _ in outs)),...]
    pallas_call x3 -> x1, Pallas kernels: 47.6 us -> 10.3 us  [call(): pl.pallas_call(body, name=name, out_shape=tuple(outs), in_specs=[spaces[s...]
    ppermute x53 -> x49, waiting for transfers between devices: 85.4 us -> 67.9 us  [swap(): return lax.ppermute(array, axis, pairs)]
    ppermute x53 -> x49, starting transfers between devices: 56 us -> 61.1 us  [swap(): return lax.ppermute(array, axis, pairs)]
    convert_element_type x16 -> x15, other arithmetic: 13.3 us -> 10.7 us  [add(): return total.astype(BF)]
  transfers between devices with their start and end apart: 53 -> 49, of which waited for: 21 -> 16; matrix products, arithmetic and copies ran while one was open for 7% -> 7% of each run, Pallas kernels for 35% -> 37%
where the time goes in v3:
time: 306 us; the launch traced here: 305 us
  Pallas kernels  145 us (47%)
  waiting for transfers between devices  67.9 us (22%)
  starting transfers between devices  61.1 us (20%)
  other arithmetic  16.3 us (5%)
  local copies, waits for them, and re-layouts  13.2 us (4%)
    pallas_call x9, Pallas kernels, grid_call(): pl.pallas_call(body, name=name, out_shape=tuple((o for o, _, _ in outs)),...  134 us
    ppermute x49, waiting for transfers between devices, swap(): return lax.ppermute(array, axis, pairs)  67.9 us
    ppermute x49, starting transfers between devices, swap(): return lax.ppermute(array, axis, pairs)  61.1 us
    convert_element_type x15, other arithmetic, add(): return total.astype(BF)  10.7 us
    pallas_call x1, Pallas kernels, call(): pl.pallas_call(body, name=name, out_shape=tuple(outs), in_specs=[spaces[s...  10.3 us
  transfers between devices with their start and end apart: 49, of which 16 were waited for; matrix products, arithmetic and copies ran while one was open for 7% of the time, Pallas kernels for 37%

profile of v3, /device:TPU:0, one launch (start us, length us, event | category | flops | bytes accessed | tf_op | source)
XLA Modules:
  0.0 304.5 jit_solution(3161398482878540757)
XLA Ops:
  0.7 0.9 reshape.53
  1.6 0.8 concatenate.37
  2.5 1.0 fusion.1
  3.5 4.1 %collective-permute-start.1 = (bf16[48,2432]{1,0:T(8,128)(2,1)S(1)}, bf16[48,2432]{1,0:T(8,128)(2,1)S(1)}, u32[]{:S(2)}, u32[]{:S(2)}) collective-permute-start(bf16[48,2432]{1,0:T(8,128)(2,1)S(1)} %fusion.1), channel_id=1, source_target_pairs={{0,4},{1,5},{2,6},{3,7},{4,0},{5,1},{6,2},{7,3},{8,12},{9,13},{10,... | collective-permute-start | bytes 700424 | tf_op jit(solution)/shard_map/ppermute | solution.py:1165
  7.6 1.6 collective-permute-start
  9.2 10.9 %collective-permute-done.1 = bf16[48,2432]{1,0:T(8,128)(2,1)S(1)} collective-permute-done((bf16[48,2432]{1,0:T(8,128)(2,1)S(1)}, bf16[48,2432]{1,0:T(8,128)(2,1)S(1)}, u32[]{:S(2)}, u32[]{:S(2)}) %collective-permute-start.1) | collective-permute-done | bytes 233504 | tf_op jit(solution)/shard_map/ppermute | solution.py:1165
  20.1 4.4 %collective-permute-done.2 = bf16[48,2432]{1,0:T(8,128)(2,1)S(1)} collective-permute-done((bf16[48,2432]{1,0:T(8,128)(2,1)S(1)}, bf16[48,2432]{1,0:T(8,128)(2,1)S(1)}, u32[]{:S(2)}, u32[]{:S(2)}) %collective-permute-start.2) | collective-permute-done | bytes 233504 | tf_op jit(solution)/shard_map/ppermute | solution.py:1165
  24.7 1.6 collective-permute-start.6
  26.3 2.5 collective-permute-start.5
  28.8 8.0 %collective-permute-start.4 = (bf16[48,1920]{1,0:T(8,128)(2,1)S(1)}, bf16[48,1920]{1,0:T(8,128)(2,1)S(1)}, u32[]{:S(2)}, u32[]{:S(2)}) collective-permute-start(bf16[48,1920]{1,0:T(8,128)(2,1)S(1)} %fusion.2), channel_id=1, source_target_pairs={{0,4},{1,5},{2,6},{3,7},{4,0},{5,1},{6,2},{7,3},{8,12},{9,13},{10,... | collective-permute-start | bytes 552968 | tf_op jit(solution)/shard_map/ppermute | solution.py:1165
  37.3 11.9 %collective-permute-done.4 = bf16[48,1920]{1,0:T(8,128)(2,1)S(1)} collective-permute-done((bf16[48,1920]{1,0:T(8,128)(2,1)S(1)}, bf16[48,1920]{1,0:T(8,128)(2,1)S(1)}, u32[]{:S(2)}, u32[]{:S(2)}) %collective-permute-start.4) | collective-permute-done | bytes 184352 | tf_op jit(solution)/shard_map/ppermute | solution.py:1165
  49.8 1.5 collective-permute-start.9
  51.4 2.7 collective-permute-start.18
  54.1 6.9 %collective-permute-start.17 = (bf16[192,768]{1,0:T(8,128)(2,1)S(1)}, bf16[192,768]{1,0:T(8,128)(2,1)}, u32[]{:S(2)}, u32[]{:S(2)}) collective-permute-start(bf16[192,768]{1,0:T(8,128)(2,1)S(1)} %constant_dynamic-slice_fusion), channel_id=1, source_target_pairs={{0,4},{1,5},{2,6},{3,7},{4,0},{5,1},{6,2},{7,3},{8,12},{9,13},{10,... | collective-permute-start | bytes 884744 | tf_op jit(solution)/shard_map/ppermute | solution.py:1165
  62.1 9.5 %qkv.1 = (bf16[896,2304]{1,0:T(8,128)(2,1)}, f32[16,768]{1,0:T(8,128)}) custom-call(s32[4]{0:T(128)} %pad_add_fusion.ids_ref, bf16[896,768]{1,0:T(8,128)(2,1)} %bitcast.86, bf16[4,48,2432]{2,1,0:T(8,128)(2,1)} %copy-done.2, bf16[4,48,2432]{2,1,0:T(8,128)(2,1)} %copy-done.5, bf16[4,48,2432]{2,1,0:T(8,128)(2,1)} %collective-permute-done.7.b2, ...), custom_call_target="tpu_custom_call" | custom-call | flops 1 | bytes 1 | tf_op jit(solution)/shard_map/qkv/pallas_call | solution.py:146
  72.2 10.1 %attention.1 = (bf16[896,768]{1,0:T(8,128)(2,1)}, f32[896,128]{1,0:T(8,128)}) custom-call(s32[7]{0:T(128)} %counts_ref.7, bf16[896,2304]{1,0:T(8,128)(2,1)} %get-tuple-element.86.qkv_ref.refs_0_.refs_1_.refs_2_.refs_3_.refs_4_.refs_5_), custom_call_target="tpu_custom_call" | custom-call | flops 1 | bytes 1 | tf_op jit(solution)/shard_map/attention/pallas_call | solution.py:146
  82.3 1.3 pad_maximum_fusion.b0
  84.6 5.0 %collective-permute-done.11.rest_3_ = bf16[4,48,1920]{2,1,0:T(8,128)(2,1)S(1)} collective-permute-done((bf16[4,48,1920]{2,1,0:T(8,128)(2,1)}, bf16[4,48,1920]{2,1,0:T(8,128)(2,1)S(1)}, u32[]{:S(2)}, u32[]{:S(2)}) %collective-permute-start.11) | collective-permute-done | bytes 737312 | tf_op jit(solution)/shard_map/ppermute | solution.py:1165
  92.0 19.0 %out_norm_up.1 = (bf16[896,3072]{1,0:T(8,128)(2,1)}, bf16[896,3072]{1,0:T(8,128)(2,1)}, f32[896,768]{1,0:T(8,128)}, f32[896,128]{1,0:T(8,128)}, bf16[896,768]{1,0:T(8,128)(2,1)}) custom-call(s32[4]{0:T(128)} %pad_add_fusion.ids_ref, bf16[896,768]{1,0:T(8,128)(2,1)} %get-tuple-element.87.ctx_ref, bf16[896,768]{1,0:T(8,128)(2,1)} %bitcast.87, ...), custom_call_target="tpu_custom_call" | custom-call | flops 1 | bytes 1 | tf_op jit(solution)/shard_map/out_norm_up/pallas_call | solution.py:146
  111.2 2.9 collective-permute-done.21.b3
  114.1 1.0 copy-done.10
  115.1 32.7 %down_and_back.1 = (f32[7,768]{1,0:T(8,128)}, f32[8,768]{1,0:T(8,128)}, bf16[1,2,4,384,384]{4,3,2,1,0:T(8,128)(2,1)}, bf16[1,2,4,384,384]{4,3,2,1,0:T(8,128)(2,1...) custom-call(s32[4]{0:T(128)} %pad_add_fusion.ids_ref, s32[7]{0:T(128)} %counts_ref.7, ...), custom_call_target="tpu_custom_call" | custom-call | flops 1 | bytes 1 | tf_op jit(solution)/shard_map/down_and_back/pallas_call | solution.py:146
  148.0 24.4 %up_and_back.1 = (bf16[2,2,4,48,1536]{4,3,2,1,0:T(8,128)(2,1)}, bf16[2,2,4,48,1536]{4,3,2,1,0:T(8,128)(2,1)}, bf16[896,768]{1,0:T(8,128)(2,1)}, f32[8,768]{1,0:T...) custom-call(s32[4]{0:T(128)} %pad_add_fusion.ids_ref, bf16[896,768]{1,0:T(8,128)(2,1)} %get-tuple-element.100.low_ref, ...), custom_call_target="tpu_custom_call" | custom-call | flops 1 | bytes 1 | tf_op jit(solution)/shard_map/up_and_back/pallas_call | solution.py:146
  172.9 2.2 add_convert_fusion.1
  175.1 1.3 slice_bitcast_fusion.1
  176.4 1.1 collective-permute-start.25
  178.2 1.2 slice_bitcast_fusion.3
  179.4 1.0 collective-permute-start.24
  180.4 12.8 %attention_back.1 = (bf16[896,1536]{1,0:T(8,128)(2,1)}, f32[8,512]{1,0:T(8,128)}) custom-call(s32[7]{0:T(128)} %counts_ref.7, bf16[896,2304]{1,0:T(8,128)(2,1)} %get-tuple-element.86.qkv_ref.refs_0_.refs_1_.refs_2_.refs_3_.refs_4_.refs_5_, bf16[896,2304]{1,0:T(8,128)(2,1)} %get-tuple-element.86.qkv_ref.refs_0_.refs_1_.refs_2_.refs_3_.refs_4_.refs_5_, ...), custom_call_target="tpu_custom_call" | custom-call | flops 1 | bytes 1 | tf_op jit(solution)/shard_map/attention_back/pallas_call | solution.py:146
  193.3 11.0 %attention_weight.1 = (bf16[2,2,4,48,1152]{4,3,2,1,0:T(8,128)(2,1)}, bf16[2,2,4,48,1152]{4,3,2,1,0:T(8,128)(2,1)}) custom-call(s32[4]{0:T(128)} %pad_add_fusion.ids_ref, bf16[896,1536]{1,0:T(8,128)(2,1)} %get-tuple-element.115.gqkv_ref.ga_hbm, bf16[896,768]{1,0:T(8,128)(2,1)} %get-tuple-element.116.glow_ref, bf16[896,768]{1,0:T(8,128)(2,1)} %bitcast.88, ...), custom_call_target="tpu_custom_call" | custom-call | flops 1 | bytes 1 | tf_op jit(solution)/shard_map/attention_weight/pallas_call | solution.py:146
  204.9 2.8 collective-permute-done.24
  207.7 1.6 add_convert_fusion.4
  209.4 0.9 slice_bitcast_fusion.15
  210.3 2.4 collective-permute-start.32
  212.7 3.9 %collective-permute-start.31 = (bf16[384,384]{1,0:T(8,128)(2,1)}, bf16[384,384]{1,0:T(8,128)(2,1)}, u32[]{:S(2)}, u32[]{:S(2)}) collective-permute-start(bf16[384,384]{1,0:T(8,128)(2,1)} %get-tuple-element.210), channel_id=1, source_target_pairs={{0,4},{1,5},{2,6},{3,7},{4,0},{5,1},{6,2},{7,3},{8,12},{9,13},{10,... | collective-permute-start | bytes 884744 | tf_op jit(solution)/shard_map/ppermute | solution.py:1165
  217.1 0.9 slice_bitcast_fusion.7
  218.0 1.4 collective-permute-start.29
  220.0 0.9 collective-permute-start.27
  220.9 8.7 %attention_back_rest.1 = (bf16[896,768]{1,0:T(8,128)(2,1)}, f32[8,256]{1,0:T(8,128)}) custom-call(s32[7]{0:T(128)} %counts_ref.7, bf16[896,2304]{1,0:T(8,128)(2,1)} %get-tuple-element.86.qkv_ref.refs_0_.refs_1_.refs_2_.refs_3_.refs_4_.refs_5_, bf16[896,2304]{1,0:T(8,128)(2,1)} %get-tuple-element.86.qkv_ref.refs_0_.refs_1_.refs_2_.refs_3_.refs_4_.refs_5_, ...), custom_call_target="tpu_custom_call" | custom-call | flops 1 | bytes 1 | tf_op jit(solution)/shard_map/attention_back_rest/pallas_call | solution.py:146
  229.6 6.3 %last_weight.1 = (bf16[2,2,4,48,512]{4,3,2,1,0:T(8,128)(2,1)}, bf16[2,2,4,48,512]{4,3,2,1,0:T(8,128)(2,1)}) custom-call(s32[4]{0:T(128)} %pad_add_fusion.ids_ref, bf16[896,768]{1,0:T(8,128)(2,1)} %get-tuple-element.135.gqkv_ref.gb_hbm, bf16[896,768]{1,0:T(8,128)(2,1)} %bitcast.89, f32[8,512]{1,0:T(8,128)} %get-tuple-element.124.va_ref, ...), custom_call_target="tpu_custom_call" | custom-call | flops 1 | bytes 1 | tf_op jit(solution)/shard_map/last_weight/pallas_call | solution.py:146
  235.9 4.9 %collective-permute-done.31 = bf16[384,384]{1,0:T(8,128)(2,1)} collective-permute-done((bf16[384,384]{1,0:T(8,128)(2,1)}, bf16[384,384]{1,0:T(8,128)(2,1)}, u32[]{:S(2)}, u32[]{:S(2)}) %collective-permute-start.31) | collective-permute-done | bytes 294944 | tf_op jit(solution)/shard_map/ppermute | solution.py:1165
  240.8 1.3 add_convert_fusion.11
  242.1 1.3 collective-permute-start.37
  243.6 1.4 add_convert_fusion.5
  245.2 2.4 collective-permute-start.35
  247.6 2.1 collective-permute-start.33
  250.7 10.3 %tokens_back.1 = f32[896,768]{1,0:T(8,128)} custom-call(s32[4]{0:T(128)} %pad_add_fusion.ids_ref, bf16[896,1536]{1,0:T(8,128)(2,1)} %get-tuple-element.115.gqkv_ref.ga_hbm, bf16[896,768]{1,0:T(8,128)(2,1)} %get-tuple-element.135.gqkv_ref.gb_hbm, f32[896,768]{1,0:T(8,128)} %get-tuple-element.136.gattn_ref, bf16[4,48,2432]{2,1,0:T(8,128)(2,1)} %copy-done.2, ...), custom_call_target="tpu_custom_call" | custom-call | flops 1 | bytes 1 | tf_op jit(solution)/shard_map/tokens_back/pallas_call | solution.py:76
  261.0 1.0 add_convert_fusion.14
  262.1 1.3 collective-permute-start.38
  263.4 1.0 add_convert_fusion.10
  264.6 8.0 %collective-permute-done.38 = bf16[2,4,48,512]{3,2,1,0:T(8,128)(2,1)S(1)} collective-permute-done((bf16[2,4,48,512]{3,2,1,0:T(8,128)(2,1)S(1)}, bf16[2,4,48,512]{3,2,1,0:T(8,128)(2,1)S(1)}, u32[]{:S(2)}, u32[]{:S(2)}) %collective-permute-start.38) | collective-permute-done | bytes 393248 | tf_op jit(solution)/shard_map/ppermute | solution.py:1165
  272.6 1.3 collective-permute-start.40
  274.0 1.0 collective-permute-start.39
  275.0 2.9 collective-permute-done.40
  277.9 1.8 collective-permute-done.39
  279.9 2.7 collective-permute-start.43
  282.6 1.7 collective-permute-start.41
  284.9 3.8 %collective-permute-done.43 = bf16[48,1664]{1,0:T(8,128)(2,1)S(1)} collective-permute-done((bf16[48,1664]{1,0:T(8,128)(2,1)S(1)}, bf16[48,1664]{1,0:T(8,128)(2,1)S(1)}, u32[]{:S(2)}, u32[]{:S(2)}) %collective-permute-start.43) | collective-permute-done | bytes 159776 | tf_op jit(solution)/shard_map/ppermute | solution.py:1165
  288.6 5.3 %collective-permute-done.42 = bf16[48,1664]{1,0:T(8,128)(2,1)S(1)} collective-permute-done((bf16[48,1664]{1,0:T(8,128)(2,1)S(1)}, bf16[48,1664]{1,0:T(8,128)(2,1)S(1)}, u32[]{:S(2)}, u32[]{:S(2)}) %collective-permute-start.42) | collective-permute-done | bytes 159776 | tf_op jit(solution)/shard_map/ppermute | solution.py:1165
  294.7 1.1 maximum_convert_fusion
  296.0 1.4 copy.56
  297.4 2.0 collective-permute-done.44
  301.7 0.9 slice_reduce_fusion
  303.6 0.9 copy-done.14
  (148 shorter events, 16.5 us)
Async XLA Ops:
  0.6 50.7 %copy-start = (bf16[384,768]{1,0:T(8,128)(2,1)S(1)}, bf16[384,768]{1,0:T(8,128)(2,1)}, u32[]{:S(2)}) copy-start(bf16[384,768]{1,0:T(8,128)(2,1)} %param.28) | copy-start | bytes 1769476
  0.7 25.6 %copy-start.12 = (bf16[96,3072]{1,0:T(8,128)(2,1)S(1)}, bf16[96,3072]{1,0:T(8,128)(2,1)}, u32[]{:S(2)}) copy-start(bf16[96,3072]{1,0:T(8,128)(2,1)} %param.26) | copy-start | bytes 1769476
  0.7 25.6 %copy-start.13 = (bf16[96,768]{1,0:T(8,128)(2,1)S(1)}, bf16[96,768]{1,0:T(8,128)(2,1)}, u32[]{:S(2)}) copy-start(bf16[96,768]{1,0:T(8,128)(2,1)} %param.22) | copy-start | bytes 442372
  3.5 16.6 %collective-permute-start.1 = (bf16[48,2432]{1,0:T(8,128)(2,1)S(1)}, bf16[48,2432]{1,0:T(8,128)(2,1)S(1)}, u32[]{:S(2)}, u32[]{:S(2)}) collective-permute-start(bf16[48,2432]{1,0:T(8,128)(2,1)S(1)} %fusion.1), channel_id=1, source_target_pairs={{0,4},{1,5},{2,6},{3,7},{4,0},{5,1},{6,2},{7,3},{8,12},{9,13},{10,... | collective-permute-start | bytes 700424 | tf_op jit(solution)/shard_map/ppermute | solution.py:1165
  7.6 12.5 %collective-permute-start = (bf16[48,2432]{1,0:T(8,128)(2,1)S(1)}, bf16[48,2432]{1,0:T(8,128)(2,1)S(1)}, u32[]{:S(2)}, u32[]{:S(2)}) collective-permute-start(bf16[48,2432]{1,0:T(8,128)(2,1)S(1)} %fusion.1), channel_id=1, source_target_pairs={{0,2},{1,3},{2,0},{3,1},{4,6},{5,7},{6,4},{7,5},{8,10},{9,11},{10,... | collective-permute-start | bytes 700424 | tf_op jit(solution)/shard_map/ppermute | solution.py:1165
  9.2 15.3 %collective-permute-start.2 = (bf16[48,2432]{1,0:T(8,128)(2,1)S(1)}, bf16[48,2432]{1,0:T(8,128)(2,1)S(1)}, u32[]{:S(2)}, u32[]{:S(2)}) collective-permute-start(bf16[48,2432]{1,0:T(8,128)(2,1)S(1)} %fusion.1), channel_id=1, source_target_pairs={{0,6},{1,7},{2,4},{3,5},{4,2},{5,3},{6,0},{7,1},{8,14},{9,15},{10,... | collective-permute-start | bytes 700424 | tf_op jit(solution)/shard_map/ppermute | solution.py:1165
  24.6 37.4 %copy-start.2 = (bf16[4,48,2432]{2,1,0:T(8,128)(2,1)}, bf16[4,48,2432]{2,1,0:T(8,128)(2,1)S(1)}, u32[]{:S(2)}) copy-start(bf16[4,48,2432]{2,1,0:T(8,128)(2,1)S(1)} %pad_maximum_fusion.1.b0) | copy-start | bytes 2801668
  24.7 24.7 %collective-permute-start.6 = (bf16[4,48,2432]{2,1,0:T(8,128)(2,1)S(1)}, bf16[4,48,2432]{2,1,0:T(8,128)(2,1)S(1)}, u32[]{:S(2)}, u32[]{:S(2)}) collective-permute-start(bf16[4,48,2432]{2,1,0:T(8,128)(2,1)S(1)} %pad_maximum_fusion.1.b0), channel_id=1, source_target_pairs={{0,1},{1,0},{2,3},{3,2},{4,5},{5,4},{6,7},{7,6},{8,9},{9,8},{10,11... | collective-permute-start | bytes 2801672 | tf_op jit(solution)/shard_map/ppermute | solution.py:1165
  26.3 11.0 %collective-permute-start.5 = (bf16[48,1920]{1,0:T(8,128)(2,1)S(1)}, bf16[48,1920]{1,0:T(8,128)(2,1)S(1)}, u32[]{:S(2)}, u32[]{:S(2)}) collective-permute-start(bf16[48,1920]{1,0:T(8,128)(2,1)S(1)} %fusion.2), channel_id=1, source_target_pairs={{0,6},{1,7},{2,4},{3,5},{4,2},{5,3},{6,0},{7,1},{8,14},{9,15},{10,... | collective-permute-start | bytes 552968 | tf_op jit(solution)/shard_map/ppermute | solution.py:1165
  28.8 20.4 %collective-permute-start.4 = (bf16[48,1920]{1,0:T(8,128)(2,1)S(1)}, bf16[48,1920]{1,0:T(8,128)(2,1)S(1)}, u32[]{:S(2)}, u32[]{:S(2)}) collective-permute-start(bf16[48,1920]{1,0:T(8,128)(2,1)S(1)} %fusion.2), channel_id=1, source_target_pairs={{0,4},{1,5},{2,6},{3,7},{4,0},{5,1},{6,2},{7,3},{8,12},{9,13},{10,... | collective-permute-start | bytes 552968 | tf_op jit(solution)/shard_map/ppermute | solution.py:1165
  36.8 12.4 %collective-permute-start.3 = (bf16[48,1920]{1,0:T(8,128)(2,1)S(1)}, bf16[48,1920]{1,0:T(8,128)(2,1)S(1)}, u32[]{:S(2)}, u32[]{:S(2)}) collective-permute-start(bf16[48,1920]{1,0:T(8,128)(2,1)S(1)} %fusion.2), channel_id=1, source_target_pairs={{0,2},{1,3},{2,0},{3,1},{4,6},{5,7},{6,4},{7,5},{8,10},{9,11},{10,... | collective-permute-start | bytes 552968 | tf_op jit(solution)/shard_map/ppermute | solution.py:1165
  37.3 16.7 %collective-permute-start.7 = (bf16[4,48,2432]{2,1,0:T(8,128)(2,1)S(1)}, bf16[4,48,2432]{2,1,0:T(8,128)(2,1)}, u32[]{:S(2)}, u32[]{:S(2)}) collective-permute-start(bf16[4,48,2432]{2,1,0:T(8,128)(2,1)S(1)} %pad_maximum_fusion.1.b0), channel_id=1, source_target_pairs={{0,8},{8,0},{16,24},{24,16},{1,9},{9,1},{17,25},{25,17},{2,10},{10... | collective-permute-start | bytes 2801672 | tf_op jit(solution)/shard_map/ppermute | solution.py:1165
  49.3 34.8 %copy-start.3 = (bf16[4,48,1920]{2,1,0:T(8,128)(2,1)}, bf16[4,48,1920]{2,1,0:T(8,128)(2,1)S(1)}, u32[]{:S(2)}) copy-start(bf16[4,48,1920]{2,1,0:T(8,128)(2,1)S(1)} %pad_maximum_fusion.2.rest_0_) | copy-start | bytes 2211844
  49.3 12.7 %copy-start.5 = (bf16[4,48,2432]{2,1,0:T(8,128)(2,1)}, bf16[4,48,2432]{2,1,0:T(8,128)(2,1)S(1)}, u32[]{:S(2)}) copy-start(bf16[4,48,2432]{2,1,0:T(8,128)(2,1)S(1)} %collective-permute-done.6.b1) | copy-start | bytes 2801668
  49.3 11.6 %collective-permute-start.8 = (bf16[4,48,2432]{2,1,0:T(8,128)(2,1)S(1)}, bf16[4,48,2432]{2,1,0:T(8,128)(2,1)}, u32[]{:S(2)}, u32[]{:S(2)}) collective-permute-start(bf16[4,48,2432]{2,1,0:T(8,128)(2,1)S(1)} %collective-permute-done.6.b1), channel_id=1, source_target_pairs={{0,8},{8,0},{16,24},{24,16},{1,9},{9,1},{17,25},{25,17},{2,10},{10... | collective-permute-start | bytes 2801672 | tf_op jit(solution)/shard_map/ppermute | solution.py:1165
  49.4 22.1 %collective-permute-start.10 = (bf16[4,48,1920]{2,1,0:T(8,128)(2,1)S(1)}, bf16[4,48,1920]{2,1,0:T(8,128)(2,1)}, u32[]{:S(2)}, u32[]{:S(2)}) collective-permute-start(bf16[4,48,1920]{2,1,0:T(8,128)(2,1)S(1)} %pad_maximum_fusion.2.rest_0_), channel_id=1, source_target_pairs={{0,1},{1,0},{2,3},{3,2},{4,5},{5,4},{6,7},{7,6},{8,9},{9,8},{10,11... | collective-permute-start | bytes 2211848 | tf_op jit(solution)/shard_map/ppermute | solution.py:1165
  49.8 22.3 %collective-permute-start.9 = (bf16[4,48,1920]{2,1,0:T(8,128)(2,1)S(1)}, bf16[4,48,1920]{2,1,0:T(8,128)(2,1)}, u32[]{:S(2)}, u32[]{:S(2)}) collective-permute-start(bf16[4,48,1920]{2,1,0:T(8,128)(2,1)S(1)} %pad_maximum_fusion.2.rest_0_), channel_id=1, source_target_pairs={{0,16},{8,24},{16,0},{24,8},{1,17},{9,25},{17,1},{25,9},{2,18},{10... | collective-permute-start | bytes 2211848 | tf_op jit(solution)/shard_map/ppermute | solution.py:1165
  51.4 30.9 %collective-permute-start.18 = (bf16[192,768]{1,0:T(8,128)(2,1)S(1)}, bf16[192,768]{1,0:T(8,128)(2,1)}, u32[]{:S(2)}, u32[]{:S(2)}) collective-permute-start(bf16[192,768]{1,0:T(8,128)(2,1)S(1)} %constant_dynamic-slice_fusion), channel_id=1, source_target_pairs={{0,6},{1,7},{2,4},{3,5},{4,2},{5,3},{6,0},{7,1},{8,14},{9,15},{10,... | collective-permute-start | bytes 884744 | tf_op jit(solution)/shard_map/ppermute | solution.py:1165
  54.1 28.2 %collective-permute-start.17 = (bf16[192,768]{1,0:T(8,128)(2,1)S(1)}, bf16[192,768]{1,0:T(8,128)(2,1)}, u32[]{:S(2)}, u32[]{:S(2)}) collective-permute-start(bf16[192,768]{1,0:T(8,128)(2,1)S(1)} %constant_dynamic-slice_fusion), channel_id=1, source_target_pairs={{0,4},{1,5},{2,6},{3,7},{4,0},{5,1},{6,2},{7,3},{8,12},{9,13},{10,... | collective-permute-start | bytes 884744 | tf_op jit(solution)/shard_map/ppermute | solution.py:1165
  60.9 21.3 %collective-permute-start.16 = (bf16[192,768]{1,0:T(8,128)(2,1)S(1)}, bf16[192,768]{1,0:T(8,128)(2,1)}, u32[]{:S(2)}, u32[]{:S(2)}) collective-permute-start(bf16[192,768]{1,0:T(8,128)(2,1)S(1)} %constant_dynamic-slice_fusion), channel_id=1, source_target_pairs={{0,2},{1,3},{2,0},{3,1},{4,6},{5,7},{6,4},{7,5},{8,10},{9,11},{10,... | collective-permute-start | bytes 884744 | tf_op jit(solution)/shard_map/ppermute | solution.py:1165
  71.5 18.1 %collective-permute-start.11 = (bf16[4,48,1920]{2,1,0:T(8,128)(2,1)}, bf16[4,48,1920]{2,1,0:T(8,128)(2,1)S(1)}, u32[]{:S(2)}, u32[]{:S(2)}) collective-permute-start(bf16[4,48,1920]{2,1,0:T(8,128)(2,1)} %collective-permute-done.10.rest_1_), channel_id=1, source_target_pairs={{0,16},{8,24},{16,0},{24,8},{1,17},{9,25},{17,1},{25,9},{2,18},{10... | collective-permute-start | bytes 2211848 | tf_op jit(solution)/shard_map/ppermute | solution.py:1165
  83.6 27.4 %copy-start.4 = (bf16[4,192,768]{2,1,0:T(8,128)(2,1)}, bf16[4,192,768]{2,1,0:T(8,128)(2,1)S(1)}, u32[]{:S(2)}) copy-start(bf16[4,192,768]{2,1,0:T(8,128)(2,1)S(1)} %pad_maximum_fusion.b0) | copy-start | bytes 3538948
  83.6 27.4 %collective-permute-start.19 = (bf16[4,192,768]{2,1,0:T(8,128)(2,1)S(1)}, bf16[4,192,768]{2,1,0:T(8,128)(2,1)}, u32[]{:S(2)}, u32[]{:S(2)}) collective-permute-start(bf16[4,192,768]{2,1,0:T(8,128)(2,1)S(1)} %pad_maximum_fusion.b0), channel_id=1, source_target_pairs={{0,1},{1,0},{2,3},{3,2},{4,5},{5,4},{6,7},{7,6},{8,9},{9,8},{10,11... | collective-permute-start | bytes 3538952 | tf_op jit(solution)/shard_map/ppermute | solution.py:1165
  84.1 7.0 %collective-permute-start.14 = (bf16[4,48,1920]{2,1,0:T(8,128)(2,1)}, bf16[4,48,1920]{2,1,0:T(8,128)(2,1)}, u32[]{:S(2)}, u32[]{:S(2)}) collective-permute-start(bf16[4,48,1920]{2,1,0:T(8,128)(2,1)} %collective-permute-done.9.rest_2_), channel_id=1, source_target_pairs={{0,8},{8,0},{16,24},{24,16},{1,9},{9,1},{17,25},{25,17},{2,10},{10... | collective-permute-start | bytes 2211848 | tf_op jit(solution)/shard_map/ppermute | solution.py:1165
  84.1 7.5 %collective-permute-start.12 = (bf16[4,48,1920]{2,1,0:T(8,128)(2,1)S(1)}, bf16[4,48,1920]{2,1,0:T(8,128)(2,1)}, u32[]{:S(2)}, u32[]{:S(2)}) collective-permute-start(bf16[4,48,1920]{2,1,0:T(8,128)(2,1)S(1)} %pad_maximum_fusion.2.rest_0_), channel_id=1, source_target_pairs={{0,8},{8,0},{16,24},{24,16},{1,9},{9,1},{17,25},{25,17},{2,10},{10... | collective-permute-start | bytes 2211848 | tf_op jit(solution)/shard_map/ppermute | solution.py:1165
  84.6 7.0 %collective-permute-start.13 = (bf16[4,48,1920]{2,1,0:T(8,128)(2,1)}, bf16[4,48,1920]{2,1,0:T(8,128)(2,1)}, u32[]{:S(2)}, u32[]{:S(2)}) collective-permute-start(bf16[4,48,1920]{2,1,0:T(8,128)(2,1)} %collective-permute-done.10.rest_1_), channel_id=1, source_target_pairs={{0,8},{8,0},{16,24},{24,16},{1,9},{9,1},{17,25},{25,17},{2,10},{10... | collective-permute-start | bytes 2211848 | tf_op jit(solution)/shard_map/ppermute | solution.py:1165
  89.6 2.4 copy-start.6
  89.6 2.3 collective-permute-start.15
  91.1 20.0 %collective-permute-start.20 = (bf16[4,192,768]{2,1,0:T(8,128)(2,1)S(1)}, bf16[4,192,768]{2,1,0:T(8,128)(2,1)}, u32[]{:S(2)}, u32[]{:S(2)}) collective-permute-start(bf16[4,192,768]{2,1,0:T(8,128)(2,1)S(1)} %pad_maximum_fusion.b0), channel_id=1, source_target_pairs={{0,8},{8,0},{16,24},{24,16},{1,9},{9,1},{17,25},{25,17},{2,10},{10... | collective-permute-start | bytes 3538952 | tf_op jit(solution)/shard_map/ppermute | solution.py:1165
  111.0 3.1 %collective-permute-start.21 = (bf16[4,192,768]{2,1,0:T(8,128)(2,1)}, bf16[4,192,768]{2,1,0:T(8,128)(2,1)S(1)}, u32[]{:S(2)}, u32[]{:S(2)}) collective-permute-start(bf16[4,192,768]{2,1,0:T(8,128)(2,1)} %collective-permute-done.19.b1), channel_id=1, source_target_pairs={{0,8},{8,0},{16,24},{24,16},{1,9},{9,1},{17,25},{25,17},{2,10},{10... | collective-permute-start | bytes 3538952 | tf_op jit(solution)/shard_map/ppermute | solution.py:1165
  147.8 25.1 %collective-permute-start.22 = (bf16[1,2,4,384,384]{4,3,2,1,0:T(8,128)(2,1)}, bf16[1,2,4,384,384]{4,3,2,1,0:T(8,128)(2,1)}, u32[]{:S(2)}, u32[]{:S(2)}) collective-permute-start(bf16[1,2,4,384,384]{4,3,2,1,0:T(8,128)(2,1)} %get-tuple-element.109), channel_id=1, source_target_pairs={{0,8},{8,0},{16,24},{24,16},{1,9},{9,1},{17,25},{25,17},{2,10},{10... | collective-permute-start | bytes 7077896 | tf_op jit(solution)/shard_map/ppermute | solution.py:1165
  148.0 24.9 %copy-start.7 = (bf16[1,2,4,384,384]{4,3,2,1,0:T(8,128)(2,1)S(1)}, bf16[1,2,4,384,384]{4,3,2,1,0:T(8,128)(2,1)}, u32[]{:S(2)}) copy-start(bf16[1,2,4,384,384]{4,3,2,1,0:T(8,128)(2,1)} %get-tuple-element.108) | copy-start | bytes 7077892
  172.4 5.1 %collective-permute-start.23 = (bf16[2,2,4,48,1536]{4,3,2,1,0:T(8,128)(2,1)}, bf16[2,2,4,48,1536]{4,3,2,1,0:T(8,128)(2,1)S(1)}, u32[]{:S(2)}, u32[]{:S(2)}) collective-permute-start(bf16[2,2,4,48,1536]{4,3,2,1,0:T(8,128)(2,1)} %get-tuple-element.112), channel_id=1, source_target_pairs={{0,8},{8,0},{16,24},{24,16},{1,9},{9,1},{17,25},{25,17},{2,10},{10... | collective-permute-start | bytes 7077896 | tf_op jit(solution)/shard_map/ppermute | solution.py:1165
  175.1 2.4 copy-start.8
  176.4 28.2 %collective-permute-start.25 = (bf16[4,384,384]{2,1,0:T(8,128)(2,1)}, bf16[4,384,384]{2,1,0:T(8,128)(2,1)S(1)}, u32[]{:S(2)}, u32[]{:S(2)}) collective-permute-start(bf16[4,384,384]{2,1,0:T(8,128)(2,1)} %get-tuple-element.203), channel_id=1, source_target_pairs={{0,1},{1,0},{2,3},{3,2},{4,5},{5,4},{6,7},{7,6},{8,9},{9,8},{10,11... | collective-permute-start | bytes 3538952 | tf_op jit(solution)/shard_map/ppermute | solution.py:1165
  179.4 28.3 %collective-permute-start.24 = (bf16[2,4,48,1536]{3,2,1,0:T(8,128)(2,1)}, bf16[2,4,48,1536]{3,2,1,0:T(8,128)(2,1)}, u32[]{:S(2)}, u32[]{:S(2)}) collective-permute-start(bf16[2,4,48,1536]{3,2,1,0:T(8,128)(2,1)} %get-tuple-element.205), channel_id=1, source_target_pairs={{0,16},{8,24},{16,0},{24,8},{1,17},{9,25},{17,1},{25,9},{2,18},{10... | collective-permute-start | bytes 3538952 | tf_op jit(solution)/shard_map/ppermute | solution.py:1165
  204.9 4.4 %copy-start.15 = (bf16[2,2,4,48,1152]{4,3,2,1,0:T(8,128)(2,1)S(1)}, bf16[2,2,4,48,1152]{4,3,2,1,0:T(8,128)(2,1)}, u32[]{:S(2)}) copy-start(bf16[2,2,4,48,1152]{4,3,2,1,0:T(8,128)(2,1)} %get-tuple-element.121) | copy-start | bytes 5308420
  209.3 10.1 %collective-permute-start.26 = (bf16[2,2,4,48,1152]{4,3,2,1,0:T(8,128)(2,1)S(1)}, bf16[2,2,4,48,1152]{4,3,2,1,0:T(8,128)(2,1)S(1)}, u32[]{:S(2)}, u32[]{:S(2)}) collective-permute-start(bf16[2,2,4,48,1152]{4,3,2,1,0:T(8,128)(2,1)S(1)} %copy-done.15), channel_id=1, source_target_pairs={{0,8},{8,0},{16,24},{24,16},{1,9},{9,1},{17,25},{25,17},{2,10},{10... | collective-permute-start | bytes 5308424 | tf_op jit(solution)/shard_map/ppermute | solution.py:1165
  210.3 9.1 %copy-start.9 = (bf16[2,2,4,48,1152]{4,3,2,1,0:T(8,128)(2,1)S(1)}, bf16[2,2,4,48,1152]{4,3,2,1,0:T(8,128)(2,1)}, u32[]{:S(2)}) copy-start(bf16[2,2,4,48,1152]{4,3,2,1,0:T(8,128)(2,1)} %get-tuple-element.117) | copy-start | bytes 5308420
  210.3 25.6 %collective-permute-start.32 = (bf16[384,384]{1,0:T(8,128)(2,1)}, bf16[384,384]{1,0:T(8,128)(2,1)}, u32[]{:S(2)}, u32[]{:S(2)}) collective-permute-start(bf16[384,384]{1,0:T(8,128)(2,1)} %get-tuple-element.209), channel_id=1, source_target_pairs={{0,6},{1,7},{2,4},{3,5},{4,2},{5,3},{6,0},{7,1},{8,14},{9,15},{10,... | collective-permute-start | bytes 884744 | tf_op jit(solution)/shard_map/ppermute | solution.py:1165
  212.7 28.1 %collective-permute-start.31 = (bf16[384,384]{1,0:T(8,128)(2,1)}, bf16[384,384]{1,0:T(8,128)(2,1)}, u32[]{:S(2)}, u32[]{:S(2)}) collective-permute-start(bf16[384,384]{1,0:T(8,128)(2,1)} %get-tuple-element.210), channel_id=1, source_target_pairs={{0,4},{1,5},{2,6},{3,7},{4,0},{5,1},{6,2},{7,3},{8,12},{9,13},{10,... | collective-permute-start | bytes 884744 | tf_op jit(solution)/shard_map/ppermute | solution.py:1165
  216.6 24.2 %collective-permute-start.30 = (bf16[384,384]{1,0:T(8,128)(2,1)S(1)}, bf16[384,384]{1,0:T(8,128)(2,1)}, u32[]{:S(2)}, u32[]{:S(2)}) collective-permute-start(bf16[384,384]{1,0:T(8,128)(2,1)S(1)} %get-tuple-element.211), channel_id=1, source_target_pairs={{0,2},{1,3},{2,0},{3,1},{4,6},{5,7},{6,4},{7,5},{8,10},{9,11},{10,... | collective-permute-start | bytes 884744 | tf_op jit(solution)/shard_map/ppermute | solution.py:1165
  218.0 25.4 %collective-permute-start.29 = (bf16[4,48,1536]{2,1,0:T(8,128)(2,1)}, bf16[4,48,1536]{2,1,0:T(8,128)(2,1)S(1)}, u32[]{:S(2)}, u32[]{:S(2)}) collective-permute-start(bf16[4,48,1536]{2,1,0:T(8,128)(2,1)} %get-tuple-element.213), channel_id=1, source_target_pairs={{0,1},{1,0},{2,3},{3,2},{4,5},{5,4},{6,7},{7,6},{8,9},{9,8},{10,11... | collective-permute-start | bytes 1769480 | tf_op jit(solution)/shard_map/ppermute | solution.py:1165
  220.0 23.6 %collective-permute-start.27 = (bf16[2,4,48,1152]{3,2,1,0:T(8,128)(2,1)S(1)}, bf16[2,4,48,1152]{3,2,1,0:T(8,128)(2,1)}, u32[]{:S(2)}, u32[]{:S(2)}) collective-permute-start(bf16[2,4,48,1152]{3,2,1,0:T(8,128)(2,1)S(1)} %get-tuple-element.207), channel_id=1, source_target_pairs={{0,16},{8,24},{16,0},{24,8},{1,17},{9,25},{17,1},{25,9},{2,18},{10... | collective-permute-start | bytes 2654216 | tf_op jit(solution)/shard_map/ppermute | solution.py:1165
  242.1 21.3 %collective-permute-start.37 = (bf16[384,384]{1,0:T(8,128)(2,1)S(1)}, bf16[384,384]{1,0:T(8,128)(2,1)}, u32[]{:S(2)}, u32[]{:S(2)}) collective-permute-start(bf16[384,384]{1,0:T(8,128)(2,1)S(1)} %add_convert_fusion.11), channel_id=1, source_target_pairs={{0,16},{8,24},{16,0},{24,8},{1,17},{9,25},{17,1},{25,9},{2,18},{10... | collective-permute-start | bytes 884744 | tf_op jit(solution)/shard_map/ppermute | solution.py:1165
  243.6 1.5 copy-start.16
  245.0 5.4 %copy-start.11 = (bf16[2,2,4,48,512]{4,3,2,1,0:T(8,128)(2,1)S(1)}, bf16[2,2,4,48,512]{4,3,2,1,0:T(8,128)(2,1)}, u32[]{:S(2)}) copy-start(bf16[2,2,4,48,512]{4,3,2,1,0:T(8,128)(2,1)} %get-tuple-element.129) | copy-start | bytes 2359300
  245.0 4.7 %collective-permute-start.28 = (bf16[2,2,4,48,512]{4,3,2,1,0:T(8,128)(2,1)S(1)}, bf16[2,2,4,48,512]{4,3,2,1,0:T(8,128)(2,1)S(1)}, u32[]{:S(2)}, u32[]{:S(2)}) collective-permute-start(bf16[2,2,4,48,512]{4,3,2,1,0:T(8,128)(2,1)S(1)} %copy-done.16), channel_id=1, source_target_pairs={{0,8},{8,0},{16,24},{24,16},{1,9},{9,1},{17,25},{25,17},{2,10},{10... | collective-permute-start | bytes 2359304 | tf_op jit(solution)/shard_map/ppermute | solution.py:1165
  245.2 15.8 %collective-permute-start.35 = (bf16[48,1536]{1,0:T(8,128)(2,1)S(1)}, bf16[48,1536]{1,0:T(8,128)(2,1)S(1)}, u32[]{:S(2)}, u32[]{:S(2)}) collective-permute-start(bf16[48,1536]{1,0:T(8,128)(2,1)S(1)} %get-tuple-element.227), channel_id=1, source_target_pairs={{0,6},{1,7},{2,4},{3,5},{4,2},{5,3},{6,0},{7,1},{8,14},{9,15},{10,... | collective-permute-start | bytes 442376 | tf_op jit(solution)/shard_map/ppermute | solution.py:1165
  247.6 13.4 %collective-permute-start.34 = (bf16[48,1536]{1,0:T(8,128)(2,1)S(1)}, bf16[48,1536]{1,0:T(8,128)(2,1)S(1)}, u32[]{:S(2)}, u32[]{:S(2)}) collective-permute-start(bf16[48,1536]{1,0:T(8,128)(2,1)S(1)} %get-tuple-element.228), channel_id=1, source_target_pairs={{0,4},{1,5},{2,6},{3,7},{4,0},{5,1},{6,2},{7,3},{8,12},{9,13},{10,... | collective-permute-start | bytes 442376 | tf_op jit(solution)/shard_map/ppermute | solution.py:1165
  247.6 13.5 %collective-permute-start.33 = (bf16[48,1536]{1,0:T(8,128)(2,1)S(1)}, bf16[48,1536]{1,0:T(8,128)(2,1)}, u32[]{:S(2)}, u32[]{:S(2)}) collective-permute-start(bf16[48,1536]{1,0:T(8,128)(2,1)S(1)} %get-tuple-element.229), channel_id=1, source_target_pairs={{0,2},{1,3},{2,0},{3,1},{4,6},{5,7},{6,4},{7,5},{8,10},{9,11},{10,... | collective-permute-start | bytes 442376 | tf_op jit(solution)/shard_map/ppermute | solution.py:1165
  249.7 14.7 %collective-permute-start.36 = (bf16[4,48,1152]{2,1,0:T(8,128)(2,1)S(1)}, bf16[4,48,1152]{2,1,0:T(8,128)(2,1)S(1)}, u32[]{:S(2)}, u32[]{:S(2)}) collective-permute-start(bf16[4,48,1152]{2,1,0:T(8,128)(2,1)S(1)} %get-tuple-element.215), channel_id=1, source_target_pairs={{0,1},{1,0},{2,3},{3,2},{4,5},{5,4},{6,7},{7,6},{8,9},{9,8},{10,11... | collective-permute-start | bytes 1327112 | tf_op jit(solution)/shard_map/ppermute | solution.py:1165
  262.1 10.5 %collective-permute-start.38 = (bf16[2,4,48,512]{3,2,1,0:T(8,128)(2,1)S(1)}, bf16[2,4,48,512]{3,2,1,0:T(8,128)(2,1)S(1)}, u32[]{:S(2)}, u32[]{:S(2)}) collective-permute-start(bf16[2,4,48,512]{3,2,1,0:T(8,128)(2,1)S(1)} %get-tuple-element.217), channel_id=1, source_target_pairs={{0,16},{8,24},{16,0},{24,8},{1,17},{9,25},{17,1},{25,9},{2,18},{10... | collective-permute-start | bytes 1179656 | tf_op jit(solution)/shard_map/ppermute | solution.py:1165
  272.6 5.2 %collective-permute-start.40 = (bf16[48,1536]{1,0:T(8,128)(2,1)S(1)}, bf16[48,1536]{1,0:T(8,128)(2,1)S(1)}, u32[]{:S(2)}, u32[]{:S(2)}) collective-permute-start(bf16[48,1536]{1,0:T(8,128)(2,1)S(1)} %add_convert_fusion.14), channel_id=1, source_target_pairs={{0,16},{8,24},{16,0},{24,8},{1,17},{9,25},{17,1},{25,9},{2,18},{10... | collective-permute-start | bytes 442376 | tf_op jit(solution)/shard_map/ppermute | solution.py:1165
  274.0 5.7 %collective-permute-start.39 = (bf16[4,48,512]{2,1,0:T(8,128)(2,1)S(1)}, bf16[4,48,512]{2,1,0:T(8,128)(2,1)S(1)}, u32[]{:S(2)}, u32[]{:S(2)}) collective-permute-start(bf16[4,48,512]{2,1,0:T(8,128)(2,1)S(1)} %get-tuple-element.233), channel_id=1, source_target_pairs={{0,1},{1,0},{2,3},{3,2},{4,5},{5,4},{6,7},{7,6},{8,9},{9,8},{10,11... | collective-permute-start | bytes 589832 | tf_op jit(solution)/shard_map/ppermute | solution.py:1165
  279.9 8.7 %collective-permute-start.43 = (bf16[48,1664]{1,0:T(8,128)(2,1)S(1)}, bf16[48,1664]{1,0:T(8,128)(2,1)S(1)}, u32[]{:S(2)}, u32[]{:S(2)}) collective-permute-start(bf16[48,1664]{1,0:T(8,128)(2,1)S(1)} %get-tuple-element.219), channel_id=1, source_target_pairs={{0,6},{1,7},{2,4},{3,5},{4,2},{5,3},{6,0},{7,1},{8,14},{9,15},{10,... | collective-permute-start | bytes 479240 | tf_op jit(solution)/shard_map/ppermute | solution.py:1165
  282.6 11.3 %collective-permute-start.42 = (bf16[48,1664]{1,0:T(8,128)(2,1)S(1)}, bf16[48,1664]{1,0:T(8,128)(2,1)S(1)}, u32[]{:S(2)}, u32[]{:S(2)}) collective-permute-start(bf16[48,1664]{1,0:T(8,128)(2,1)S(1)} %get-tuple-element.220), channel_id=1, source_target_pairs={{0,4},{1,5},{2,6},{3,7},{4,0},{5,1},{6,2},{7,3},{8,12},{9,13},{10,... | collective-permute-start | bytes 479240 | tf_op jit(solution)/shard_map/ppermute | solution.py:1165
  282.6 11.3 %collective-permute-start.41 = (bf16[48,1664]{1,0:T(8,128)(2,1)S(1)}, bf16[48,1664]{1,0:T(8,128)(2,1)S(1)}, u32[]{:S(2)}, u32[]{:S(2)}) collective-permute-start(bf16[48,1664]{1,0:T(8,128)(2,1)S(1)} %get-tuple-element.221), channel_id=1, source_target_pairs={{0,2},{1,3},{2,0},{3,1},{4,6},{5,7},{6,4},{7,5},{8,10},{9,11},{10,... | collective-permute-start | bytes 479240 | tf_op jit(solution)/shard_map/ppermute | solution.py:1165
  284.4 10.3 %collective-permute-start.47 = (bf16[48,3072]{1,0:T(8,128)(2,1)S(1)}, bf16[48,3072]{1,0:T(8,128)(2,1)S(1)}, u32[]{:S(2)}, u32[]{:S(2)}) collective-permute-start(bf16[48,3072]{1,0:T(8,128)(2,1)S(1)} %pad_maximum_fusion.3), channel_id=1, source_target_pairs={{0,8},{8,0},{16,24},{24,16},{1,9},{9,1},{17,25},{25,17},{2,10},{10... | collective-permute-start | bytes 884744 | tf_op jit(solution)/shard_map/ppermute | solution.py:1165
  284.4 11.5 %collective-permute-start.48 = (bf16[384,384]{1,0:T(8,128)(2,1)S(1)}, bf16[384,384]{1,0:T(8,128)(2,1)S(1)}, u32[]{:S(2)}, u32[]{:S(2)}) collective-permute-start(bf16[384,384]{1,0:T(8,128)(2,1)S(1)} %add_convert_fusion.10), channel_id=1, source_target_pairs={{0,8},{8,0},{16,24},{24,16},{1,9},{9,1},{17,25},{25,17},{2,10},{10... | collective-permute-start | bytes 884744 | tf_op jit(solution)/shard_map/ppermute | solution.py:1165
  294.0 5.3 %collective-permute-start.44 = (bf16[48,1664]{1,0:T(8,128)(2,1)S(1)}, bf16[48,1664]{1,0:T(8,128)(2,1)S(1)}, u32[]{:S(2)}, u32[]{:S(2)}) collective-permute-start(bf16[48,1664]{1,0:T(8,128)(2,1)S(1)} %add_convert_fusion.13), channel_id=1, source_target_pairs={{0,16},{8,24},{16,0},{24,8},{1,17},{9,25},{17,1},{25,9},{2,18},{10... | collective-permute-start | bytes 479240 | tf_op jit(solution)/shard_map/ppermute | solution.py:1165
  299.5 1.4 collective-permute-start.46
  299.6 3.1 %collective-permute-start.45 = (bf16[48,2304]{1,0:T(8,128)(2,1)S(1)}, bf16[48,2304]{1,0:T(8,128)(2,1)S(1)}, u32[]{:S(2)}, u32[]{:S(2)}) collective-permute-start(bf16[48,2304]{1,0:T(8,128)(2,1)S(1)} %pad_maximum_fusion.4), channel_id=1, source_target_pairs={{0,8},{8,0},{16,24},{24,16},{1,9},{9,1},{17,25},{25,17},{2,10},{10... | collective-permute-start | bytes 663560 | tf_op jit(solution)/shard_map/ppermute | solution.py:1165
  302.7 1.8 copy-start.1
  (2 other events, 1.9 us)

commit v4 on v3

--- a/solution.py
+++ b/solution.py
@@ -1298,8 +1298,8 @@
     gtokens = tokens_backward(gqkv_a, hold(gqkv_b, sums_b, sums2, sums3), gattn, ids, bufs1)
     sums2 = sum_z(sums2, gtokens)
     sums_b = sum_x(sums_b, sums2)
-    sums_a = sum_y(sums_a, sums2)
-    sums3 = add(hold(sums3, sums2), swap(sums3, "dp", 2))
+    sums_a = sum_y(sums_a, sums_b)
+    sums3 = add(hold(sums3, sums_a), swap(sums3, "dp", 2))
     sums_a, sums2, sums3, sums_b = lax.optimization_barrier((sums_a, sums2, sums3, sums_b))
     sums_b = sum_y(sums_b)
     g_in = in_order(sums2, swap(sums2, "dp", 2), x, 1)

time: 306 us -> 306 us (level)
  no operation moved by 1% of the time
where the time goes in v4:
time: 306 us; the launch traced here: 305 us
  Pallas kernels  145 us (47%)
  waiting for transfers between devices  68.1 us (22%)
  starting transfers between devices  61.1 us (20%)
  other arithmetic  16.3 us (5%)
  local copies, waits for them, and re-layouts  13.2 us (4%)
    pallas_call x9, Pallas kernels, grid_call(): pl.pallas_call(body, name=name, out_shape=tuple((o for o, _, _ in outs)),...  134 us
    ppermute x49, waiting for transfers between devices, swap(): return lax.ppermute(array, axis, pairs)  68.1 us
    ppermute x49, starting transfers between devices, swap(): return lax.ppermute(array, axis, pairs)  61.1 us
    convert_element_type x15, other arithmetic, add(): return total.astype(BF)  10.7 us
    pallas_call x1, Pallas kernels, call(): pl.pallas_call(body, name=name, out_shape=tuple(outs), in_specs=[spaces[s...  10.3 us
  transfers between devices with their start and end apart: 49, of which 16 were waited for; matrix products, arithmetic and copies ran while one was open for 7% of the time, Pallas kernels for 37%

profile of v4, /device:TPU:0, one launch (start us, length us, event | category | flops | bytes accessed | tf_op | source)
XLA Modules:
  0.0 304.7 jit_solution(5227516458414411228)
XLA Ops:
  0.7 0.9 reshape.53
  1.6 0.8 concatenate.37
  2.5 1.0 fusion.1
  3.5 4.1 %collective-permute-start.1 = (bf16[48,2432]{1,0:T(8,128)(2,1)S(1)}, bf16[48,2432]{1,0:T(8,128)(2,1)S(1)}, u32[]{:S(2)}, u32[]{:S(2)}) collective-permute-start(bf16[48,2432]{1,0:T(8,128)(2,1)S(1)} %fusion.1), channel_id=1, source_target_pairs={{0,4},{1,5},{2,6},{3,7},{4,0},{5,1},{6,2},{7,3},{8,12},{9,13},{10,... | collective-permute-start | bytes 700424 | tf_op jit(solution)/shard_map/ppermute | solution.py:1165
  7.6 1.6 collective-permute-start
  9.2 10.9 %collective-permute-done.1 = bf16[48,2432]{1,0:T(8,128)(2,1)S(1)} collective-permute-done((bf16[48,2432]{1,0:T(8,128)(2,1)S(1)}, bf16[48,2432]{1,0:T(8,128)(2,1)S(1)}, u32[]{:S(2)}, u32[]{:S(2)}) %collective-permute-start.1) | collective-permute-done | bytes 233504 | tf_op jit(solution)/shard_map/ppermute | solution.py:1165
  20.1 4.4 %collective-permute-done.2 = bf16[48,2432]{1,0:T(8,128)(2,1)S(1)} collective-permute-done((bf16[48,2432]{1,0:T(8,128)(2,1)S(1)}, bf16[48,2432]{1,0:T(8,128)(2,1)S(1)}, u32[]{:S(2)}, u32[]{:S(2)}) %collective-permute-start.2) | collective-permute-done | bytes 233504 | tf_op jit(solution)/shard_map/ppermute | solution.py:1165
  24.7 1.6 collective-permute-start.6
  26.3 2.5 collective-permute-start.5
  28.8 8.0 %collective-permute-start.4 = (bf16[48,1920]{1,0:T(8,128)(2,1)S(1)}, bf16[48,1920]{1,0:T(8,128)(2,1)S(1)}, u32[]{:S(2)}, u32[]{:S(2)}) collective-permute-start(bf16[48,1920]{1,0:T(8,128)(2,1)S(1)} %fusion.2), channel_id=1, source_target_pairs={{0,4},{1,5},{2,6},{3,7},{4,0},{5,1},{6,2},{7,3},{8,12},{9,13},{10,... | collective-permute-start | bytes 552968 | tf_op jit(solution)/shard_map/ppermute | solution.py:1165
  37.3 11.9 %collective-permute-done.4 = bf16[48,1920]{1,0:T(8,128)(2,1)S(1)} collective-permute-done((bf16[48,1920]{1,0:T(8,128)(2,1)S(1)}, bf16[48,1920]{1,0:T(8,128)(2,1)S(1)}, u32[]{:S(2)}, u32[]{:S(2)}) %collective-permute-start.4) | collective-permute-done | bytes 184352 | tf_op jit(solution)/shard_map/ppermute | solution.py:1165
  49.8 1.5 collective-permute-start.9
  51.4 2.7 collective-permute-start.18
  54.1 6.9 %collective-permute-start.17 = (bf16[192,768]{1,0:T(8,128)(2,1)S(1)}, bf16[192,768]{1,0:T(8,128)(2,1)}, u32[]{:S(2)}, u32[]{:S(2)}) collective-permute-start(bf16[192,768]{1,0:T(8,128)(2,1)S(1)} %constant_dynamic-slice_fusion), channel_id=1, source_target_pairs={{0,4},{1,5},{2,6},{3,7},{4,0},{5,1},{6,2},{7,3},{8,12},{9,13},{10,... | collective-permute-start | bytes 884744 | tf_op jit(solution)/shard_map/ppermute | solution.py:1165
  62.1 9.5 %qkv.1 = (bf16[896,2304]{1,0:T(8,128)(2,1)}, f32[16,768]{1,0:T(8,128)}) custom-call(s32[4]{0:T(128)} %pad_add_fusion.ids_ref, bf16[896,768]{1,0:T(8,128)(2,1)} %bitcast.86, bf16[4,48,2432]{2,1,0:T(8,128)(2,1)} %copy-done.2, bf16[4,48,2432]{2,1,0:T(8,128)(2,1)} %copy-done.5, bf16[4,48,2432]{2,1,0:T(8,128)(2,1)} %collective-permute-done.7.b2, ...), custom_call_target="tpu_custom_call" | custom-call | flops 1 | bytes 1 | tf_op jit(solution)/shard_map/qkv/pallas_call | solution.py:146
  72.2 10.1 %attention.1 = (bf16[896,768]{1,0:T(8,128)(2,1)}, f32[896,128]{1,0:T(8,128)}) custom-call(s32[7]{0:T(128)} %counts_ref.7, bf16[896,2304]{1,0:T(8,128)(2,1)} %get-tuple-element.86.qkv_ref.refs_0_.refs_1_.refs_2_.refs_3_.refs_4_.refs_5_), custom_call_target="tpu_custom_call" | custom-call | flops 1 | bytes 1 | tf_op jit(solution)/shard_map/attention/pallas_call | solution.py:146
  82.3 1.3 pad_maximum_fusion.b0
  84.6 5.0 %collective-permute-done.11.rest_3_ = bf16[4,48,1920]{2,1,0:T(8,128)(2,1)S(1)} collective-permute-done((bf16[4,48,1920]{2,1,0:T(8,128)(2,1)}, bf16[4,48,1920]{2,1,0:T(8,128)(2,1)S(1)}, u32[]{:S(2)}, u32[]{:S(2)}) %collective-permute-start.11) | collective-permute-done | bytes 737312 | tf_op jit(solution)/shard_map/ppermute | solution.py:1165
  92.0 19.0 %out_norm_up.1 = (bf16[896,3072]{1,0:T(8,128)(2,1)}, bf16[896,3072]{1,0:T(8,128)(2,1)}, f32[896,768]{1,0:T(8,128)}, f32[896,128]{1,0:T(8,128)}, bf16[896,768]{1,0:T(8,128)(2,1)}) custom-call(s32[4]{0:T(128)} %pad_add_fusion.ids_ref, bf16[896,768]{1,0:T(8,128)(2,1)} %get-tuple-element.87.ctx_ref, bf16[896,768]{1,0:T(8,128)(2,1)} %bitcast.87, ...), custom_call_target="tpu_custom_call" | custom-call | flops 1 | bytes 1 | tf_op jit(solution)/shard_map/out_norm_up/pallas_call | solution.py:146
  111.2 2.9 collective-permute-done.21.b3
  114.1 1.0 copy-done.10
  115.1 32.7 %down_and_back.1 = (f32[7,768]{1,0:T(8,128)}, f32[8,768]{1,0:T(8,128)}, bf16[1,2,4,384,384]{4,3,2,1,0:T(8,128)(2,1)}, bf16[1,2,4,384,384]{4,3,2,1,0:T(8,128)(2,1...) custom-call(s32[4]{0:T(128)} %pad_add_fusion.ids_ref, s32[7]{0:T(128)} %counts_ref.7, ...), custom_call_target="tpu_custom_call" | custom-call | flops 1 | bytes 1 | tf_op jit(solution)/shard_map/down_and_back/pallas_call | solution.py:146
  148.0 24.4 %up_and_back.1 = (bf16[2,2,4,48,1536]{4,3,2,1,0:T(8,128)(2,1)}, bf16[2,2,4,48,1536]{4,3,2,1,0:T(8,128)(2,1)}, bf16[896,768]{1,0:T(8,128)(2,1)}, f32[8,768]{1,0:T...) custom-call(s32[4]{0:T(128)} %pad_add_fusion.ids_ref, bf16[896,768]{1,0:T(8,128)(2,1)} %get-tuple-element.100.low_ref, ...), custom_call_target="tpu_custom_call" | custom-call | flops 1 | bytes 1 | tf_op jit(solution)/shard_map/up_and_back/pallas_call | solution.py:146
  172.9 2.2 add_convert_fusion.1
  175.1 1.3 slice_bitcast_fusion.1
  176.4 1.1 collective-permute-start.25
  178.2 1.2 slice_bitcast_fusion.3
  179.4 1.0 collective-permute-start.24
  180.4 12.8 %attention_back.1 = (bf16[896,1536]{1,0:T(8,128)(2,1)}, f32[8,512]{1,0:T(8,128)}) custom-call(s32[7]{0:T(128)} %counts_ref.7, bf16[896,2304]{1,0:T(8,128)(2,1)} %get-tuple-element.86.qkv_ref.refs_0_.refs_1_.refs_2_.refs_3_.refs_4_.refs_5_, bf16[896,2304]{1,0:T(8,128)(2,1)} %get-tuple-element.86.qkv_ref.refs_0_.refs_1_.refs_2_.refs_3_.refs_4_.refs_5_, ...), custom_call_target="tpu_custom_call" | custom-call | flops 1 | bytes 1 | tf_op jit(solution)/shard_map/attention_back/pallas_call | solution.py:146
  193.3 11.0 %attention_weight.1 = (bf16[2,2,4,48,1152]{4,3,2,1,0:T(8,128)(2,1)}, bf16[2,2,4,48,1152]{4,3,2,1,0:T(8,128)(2,1)}) custom-call(s32[4]{0:T(128)} %pad_add_fusion.ids_ref, bf16[896,1536]{1,0:T(8,128)(2,1)} %get-tuple-element.115.gqkv_ref.ga_hbm, bf16[896,768]{1,0:T(8,128)(2,1)} %get-tuple-element.116.glow_ref, bf16[896,768]{1,0:T(8,128)(2,1)} %bitcast.88, ...), custom_call_target="tpu_custom_call" | custom-call | flops 1 | bytes 1 | tf_op jit(solution)/shard_map/attention_weight/pallas_call | solution.py:146
  204.9 2.8 collective-permute-done.24
  207.7 1.6 add_convert_fusion.4
  209.4 0.9 slice_bitcast_fusion.15
  210.3 2.4 collective-permute-start.32
  212.7 3.9 %collective-permute-start.31 = (bf16[384,384]{1,0:T(8,128)(2,1)}, bf16[384,384]{1,0:T(8,128)(2,1)}, u32[]{:S(2)}, u32[]{:S(2)}) collective-permute-start(bf16[384,384]{1,0:T(8,128)(2,1)} %get-tuple-element.210), channel_id=1, source_target_pairs={{0,4},{1,5},{2,6},{3,7},{4,0},{5,1},{6,2},{7,3},{8,12},{9,13},{10,... | collective-permute-start | bytes 884744 | tf_op jit(solution)/shard_map/ppermute | solution.py:1165
  217.1 0.9 slice_bitcast_fusion.7
  218.0 1.4 collective-permute-start.29
  220.0 0.9 collective-permute-start.27
  220.9 8.7 %attention_back_rest.1 = (bf16[896,768]{1,0:T(8,128)(2,1)}, f32[8,256]{1,0:T(8,128)}) custom-call(s32[7]{0:T(128)} %counts_ref.7, bf16[896,2304]{1,0:T(8,128)(2,1)} %get-tuple-element.86.qkv_ref.refs_0_.refs_1_.refs_2_.refs_3_.refs_4_.refs_5_, bf16[896,2304]{1,0:T(8,128)(2,1)} %get-tuple-element.86.qkv_ref.refs_0_.refs_1_.refs_2_.refs_3_.refs_4_.refs_5_, ...), custom_call_target="tpu_custom_call" | custom-call | flops 1 | bytes 1 | tf_op jit(solution)/shard_map/attention_back_rest/pallas_call | solution.py:146
  229.6 6.3 %last_weight.1 = (bf16[2,2,4,48,512]{4,3,2,1,0:T(8,128)(2,1)}, bf16[2,2,4,48,512]{4,3,2,1,0:T(8,128)(2,1)}) custom-call(s32[4]{0:T(128)} %pad_add_fusion.ids_ref, bf16[896,768]{1,0:T(8,128)(2,1)} %get-tuple-element.135.gqkv_ref.gb_hbm, bf16[896,768]{1,0:T(8,128)(2,1)} %bitcast.89, f32[8,512]{1,0:T(8,128)} %get-tuple-element.124.va_ref, ...), custom_call_target="tpu_custom_call" | custom-call | flops 1 | bytes 1 | tf_op jit(solution)/shard_map/last_weight/pallas_call | solution.py:146
  235.9 4.9 %collective-permute-done.31 = bf16[384,384]{1,0:T(8,128)(2,1)} collective-permute-done((bf16[384,384]{1,0:T(8,128)(2,1)}, bf16[384,384]{1,0:T(8,128)(2,1)}, u32[]{:S(2)}, u32[]{:S(2)}) %collective-permute-start.31) | collective-permute-done | bytes 294944 | tf_op jit(solution)/shard_map/ppermute | solution.py:1165
  240.8 1.3 add_convert_fusion.11
  242.1 1.3 collective-permute-start.38
  243.6 1.4 add_convert_fusion.5
  245.2 2.4 collective-permute-start.35
  247.6 2.1 collective-permute-start.33
  250.7 10.3 %tokens_back.1 = f32[896,768]{1,0:T(8,128)} custom-call(s32[4]{0:T(128)} %pad_add_fusion.ids_ref, bf16[896,1536]{1,0:T(8,128)(2,1)} %get-tuple-element.115.gqkv_ref.ga_hbm, bf16[896,768]{1,0:T(8,128)(2,1)} %get-tuple-element.135.gqkv_ref.gb_hbm, f32[896,768]{1,0:T(8,128)} %get-tuple-element.136.gattn_ref, bf16[4,48,2432]{2,1,0:T(8,128)(2,1)} %copy-done.2, ...), custom_call_target="tpu_custom_call" | custom-call | flops 1 | bytes 1 | tf_op jit(solution)/shard_map/tokens_back/pallas_call | solution.py:76
  261.1 1.3 collective-permute-start.36
  262.4 1.0 add_convert_fusion.14
  263.4 8.1 %collective-permute-done.36 = bf16[2,4,48,512]{3,2,1,0:T(8,128)(2,1)S(1)} collective-permute-done((bf16[2,4,48,512]{3,2,1,0:T(8,128)(2,1)S(1)}, bf16[2,4,48,512]{3,2,1,0:T(8,128)(2,1)S(1)}, u32[]{:S(2)}, u32[]{:S(2)}) %collective-permute-start.36) | collective-permute-done | bytes 393248 | tf_op jit(solution)/shard_map/ppermute | solution.py:1165
  271.8 1.0 add_convert_fusion.10
  272.8 1.3 collective-permute-start.40
  274.2 1.0 collective-permute-start.39
  275.1 2.9 collective-permute-done.40
  278.1 1.8 collective-permute-done.39
  280.1 2.7 collective-permute-start.43
  282.8 1.7 collective-permute-start.41
  285.0 3.8 %collective-permute-done.43 = bf16[48,1664]{1,0:T(8,128)(2,1)S(1)} collective-permute-done((bf16[48,1664]{1,0:T(8,128)(2,1)S(1)}, bf16[48,1664]{1,0:T(8,128)(2,1)S(1)}, u32[]{:S(2)}, u32[]{:S(2)}) %collective-permute-start.43) | collective-permute-done | bytes 159776 | tf_op jit(solution)/shard_map/ppermute | solution.py:1165
  288.8 5.3 %collective-permute-done.42 = bf16[48,1664]{1,0:T(8,128)(2,1)S(1)} collective-permute-done((bf16[48,1664]{1,0:T(8,128)(2,1)S(1)}, bf16[48,1664]{1,0:T(8,128)(2,1)S(1)}, u32[]{:S(2)}, u32[]{:S(2)}) %collective-permute-start.42) | collective-permute-done | bytes 159776 | tf_op jit(solution)/shard_map/ppermute | solution.py:1165
  294.9 1.1 maximum_convert_fusion
  296.2 1.4 copy.56
  297.6 2.0 collective-permute-done.44
  301.9 0.9 slice_reduce_fusion
  303.8 0.9 copy-done.14
  (148 shorter events, 16.5 us)
Async XLA Ops:
  0.6 50.7 %copy-start = (bf16[384,768]{1,0:T(8,128)(2,1)S(1)}, bf16[384,768]{1,0:T(8,128)(2,1)}, u32[]{:S(2)}) copy-start(bf16[384,768]{1,0:T(8,128)(2,1)} %param.28) | copy-start | bytes 1769476
  0.7 25.6 %copy-start.12 = (bf16[96,3072]{1,0:T(8,128)(2,1)S(1)}, bf16[96,3072]{1,0:T(8,128)(2,1)}, u32[]{:S(2)}) copy-start(bf16[96,3072]{1,0:T(8,128)(2,1)} %param.26) | copy-start | bytes 1769476
  0.7 25.6 %copy-start.13 = (bf16[96,768]{1,0:T(8,128)(2,1)S(1)}, bf16[96,768]{1,0:T(8,128)(2,1)}, u32[]{:S(2)}) copy-start(bf16[96,768]{1,0:T(8,128)(2,1)} %param.22) | copy-start | bytes 442372
  3.5 16.6 %collective-permute-start.1 = (bf16[48,2432]{1,0:T(8,128)(2,1)S(1)}, bf16[48,2432]{1,0:T(8,128)(2,1)S(1)}, u32[]{:S(2)}, u32[]{:S(2)}) collective-permute-start(bf16[48,2432]{1,0:T(8,128)(2,1)S(1)} %fusion.1), channel_id=1, source_target_pairs={{0,4},{1,5},{2,6},{3,7},{4,0},{5,1},{6,2},{7,3},{8,12},{9,13},{10,... | collective-permute-start | bytes 700424 | tf_op jit(solution)/shard_map/ppermute | solution.py:1165
  7.6 12.5 %collective-permute-start = (bf16[48,2432]{1,0:T(8,128)(2,1)S(1)}, bf16[48,2432]{1,0:T(8,128)(2,1)S(1)}, u32[]{:S(2)}, u32[]{:S(2)}) collective-permute-start(bf16[48,2432]{1,0:T(8,128)(2,1)S(1)} %fusion.1), channel_id=1, source_target_pairs={{0,2},{1,3},{2,0},{3,1},{4,6},{5,7},{6,4},{7,5},{8,10},{9,11},{10,... | collective-permute-start | bytes 700424 | tf_op jit(solution)/shard_map/ppermute | solution.py:1165
  9.2 15.3 %collective-permute-start.2 = (bf16[48,2432]{1,0:T(8,128)(2,1)S(1)}, bf16[48,2432]{1,0:T(8,128)(2,1)S(1)}, u32[]{:S(2)}, u32[]{:S(2)}) collective-permute-start(bf16[48,2432]{1,0:T(8,128)(2,1)S(1)} %fusion.1), channel_id=1, source_target_pairs={{0,6},{1,7},{2,4},{3,5},{4,2},{5,3},{6,0},{7,1},{8,14},{9,15},{10,... | collective-permute-start | bytes 700424 | tf_op jit(solution)/shard_map/ppermute | solution.py:1165
  24.6 37.4 %copy-start.2 = (bf16[4,48,2432]{2,1,0:T(8,128)(2,1)}, bf16[4,48,2432]{2,1,0:T(8,128)(2,1)S(1)}, u32[]{:S(2)}) copy-start(bf16[4,48,2432]{2,1,0:T(8,128)(2,1)S(1)} %pad_maximum_fusion.1.b0) | copy-start | bytes 2801668
  24.7 24.7 %collective-permute-start.6 = (bf16[4,48,2432]{2,1,0:T(8,128)(2,1)S(1)}, bf16[4,48,2432]{2,1,0:T(8,128)(2,1)S(1)}, u32[]{:S(2)}, u32[]{:S(2)}) collective-permute-start(bf16[4,48,2432]{2,1,0:T(8,128)(2,1)S(1)} %pad_maximum_fusion.1.b0), channel_id=1, source_target_pairs={{0,1},{1,0},{2,3},{3,2},{4,5},{5,4},{6,7},{7,6},{8,9},{9,8},{10,11... | collective-permute-start | bytes 2801672 | tf_op jit(solution)/shard_map/ppermute | solution.py:1165
  26.3 11.0 %collective-permute-start.5 = (bf16[48,1920]{1,0:T(8,128)(2,1)S(1)}, bf16[48,1920]{1,0:T(8,128)(2,1)S(1)}, u32[]{:S(2)}, u32[]{:S(2)}) collective-permute-start(bf16[48,1920]{1,0:T(8,128)(2,1)S(1)} %fusion.2), channel_id=1, source_target_pairs={{0,6},{1,7},{2,4},{3,5},{4,2},{5,3},{6,0},{7,1},{8,14},{9,15},{10,... | collective-permute-start | bytes 552968 | tf_op jit(solution)/shard_map/ppermute | solution.py:1165
  28.8 20.4 %collective-permute-start.4 = (bf16[48,1920]{1,0:T(8,128)(2,1)S(1)}, bf16[48,1920]{1,0:T(8,128)(2,1)S(1)}, u32[]{:S(2)}, u32[]{:S(2)}) collective-permute-start(bf16[48,1920]{1,0:T(8,128)(2,1)S(1)} %fusion.2), channel_id=1, source_target_pairs={{0,4},{1,5},{2,6},{3,7},{4,0},{5,1},{6,2},{7,3},{8,12},{9,13},{10,... | collective-permute-start | bytes 552968 | tf_op jit(solution)/shard_map/ppermute | solution.py:1165
  36.8 12.4 %collective-permute-start.3 = (bf16[48,1920]{1,0:T(8,128)(2,1)S(1)}, bf16[48,1920]{1,0:T(8,128)(2,1)S(1)}, u32[]{:S(2)}, u32[]{:S(2)}) collective-permute-start(bf16[48,1920]{1,0:T(8,128)(2,1)S(1)} %fusion.2), channel_id=1, source_target_pairs={{0,2},{1,3},{2,0},{3,1},{4,6},{5,7},{6,4},{7,5},{8,10},{9,11},{10,... | collective-permute-start | bytes 552968 | tf_op jit(solution)/shard_map/ppermute | solution.py:1165
  37.3 16.7 %collective-permute-start.7 = (bf16[4,48,2432]{2,1,0:T(8,128)(2,1)S(1)}, bf16[4,48,2432]{2,1,0:T(8,128)(2,1)}, u32[]{:S(2)}, u32[]{:S(2)}) collective-permute-start(bf16[4,48,2432]{2,1,0:T(8,128)(2,1)S(1)} %pad_maximum_fusion.1.b0), channel_id=1, source_target_pairs={{0,8},{8,0},{16,24},{24,16},{1,9},{9,1},{17,25},{25,17},{2,10},{10... | collective-permute-start | bytes 2801672 | tf_op jit(solution)/shard_map/ppermute | solution.py:1165
  49.3 34.8 %copy-start.3 = (bf16[4,48,1920]{2,1,0:T(8,128)(2,1)}, bf16[4,48,1920]{2,1,0:T(8,128)(2,1)S(1)}, u32[]{:S(2)}) copy-start(bf16[4,48,1920]{2,1,0:T(8,128)(2,1)S(1)} %pad_maximum_fusion.2.rest_0_) | copy-start | bytes 2211844
  49.3 12.7 %copy-start.5 = (bf16[4,48,2432]{2,1,0:T(8,128)(2,1)}, bf16[4,48,2432]{2,1,0:T(8,128)(2,1)S(1)}, u32[]{:S(2)}) copy-start(bf16[4,48,2432]{2,1,0:T(8,128)(2,1)S(1)} %collective-permute-done.6.b1) | copy-start | bytes 2801668
  49.3 11.6 %collective-permute-start.8 = (bf16[4,48,2432]{2,1,0:T(8,128)(2,1)S(1)}, bf16[4,48,2432]{2,1,0:T(8,128)(2,1)}, u32[]{:S(2)}, u32[]{:S(2)}) collective-permute-start(bf16[4,48,2432]{2,1,0:T(8,128)(2,1)S(1)} %collective-permute-done.6.b1), channel_id=1, source_target_pairs={{0,8},{8,0},{16,24},{24,16},{1,9},{9,1},{17,25},{25,17},{2,10},{10... | collective-permute-start | bytes 2801672 | tf_op jit(solution)/shard_map/ppermute | solution.py:1165
  49.4 22.1 %collective-permute-start.10 = (bf16[4,48,1920]{2,1,0:T(8,128)(2,1)S(1)}, bf16[4,48,1920]{2,1,0:T(8,128)(2,1)}, u32[]{:S(2)}, u32[]{:S(2)}) collective-permute-start(bf16[4,48,1920]{2,1,0:T(8,128)(2,1)S(1)} %pad_maximum_fusion.2.rest_0_), channel_id=1, source_target_pairs={{0,1},{1,0},{2,3},{3,2},{4,5},{5,4},{6,7},{7,6},{8,9},{9,8},{10,11... | collective-permute-start | bytes 2211848 | tf_op jit(solution)/shard_map/ppermute | solution.py:1165
  49.8 22.3 %collective-permute-start.9 = (bf16[4,48,1920]{2,1,0:T(8,128)(2,1)S(1)}, bf16[4,48,1920]{2,1,0:T(8,128)(2,1)}, u32[]{:S(2)}, u32[]{:S(2)}) collective-permute-start(bf16[4,48,1920]{2,1,0:T(8,128)(2,1)S(1)} %pad_maximum_fusion.2.rest_0_), channel_id=1, source_target_pairs={{0,16},{8,24},{16,0},{24,8},{1,17},{9,25},{17,1},{25,9},{2,18},{10... | collective-permute-start | bytes 2211848 | tf_op jit(solution)/shard_map/ppermute | solution.py:1165
  51.4 30.9 %collective-permute-start.18 = (bf16[192,768]{1,0:T(8,128)(2,1)S(1)}, bf16[192,768]{1,0:T(8,128)(2,1)}, u32[]{:S(2)}, u32[]{:S(2)}) collective-permute-start(bf16[192,768]{1,0:T(8,128)(2,1)S(1)} %constant_dynamic-slice_fusion), channel_id=1, source_target_pairs={{0,6},{1,7},{2,4},{3,5},{4,2},{5,3},{6,0},{7,1},{8,14},{9,15},{10,... | collective-permute-start | bytes 884744 | tf_op jit(solution)/shard_map/ppermute | solution.py:1165
  54.1 28.2 %collective-permute-start.17 = (bf16[192,768]{1,0:T(8,128)(2,1)S(1)}, bf16[192,768]{1,0:T(8,128)(2,1)}, u32[]{:S(2)}, u32[]{:S(2)}) collective-permute-start(bf16[192,768]{1,0:T(8,128)(2,1)S(1)} %constant_dynamic-slice_fusion), channel_id=1, source_target_pairs={{0,4},{1,5},{2,6},{3,7},{4,0},{5,1},{6,2},{7,3},{8,12},{9,13},{10,... | collective-permute-start | bytes 884744 | tf_op jit(solution)/shard_map/ppermute | solution.py:1165
  60.9 21.3 %collective-permute-start.16 = (bf16[192,768]{1,0:T(8,128)(2,1)S(1)}, bf16[192,768]{1,0:T(8,128)(2,1)}, u32[]{:S(2)}, u32[]{:S(2)}) collective-permute-start(bf16[192,768]{1,0:T(8,128)(2,1)S(1)} %constant_dynamic-slice_fusion), channel_id=1, source_target_pairs={{0,2},{1,3},{2,0},{3,1},{4,6},{5,7},{6,4},{7,5},{8,10},{9,11},{10,... | collective-permute-start | bytes 884744 | tf_op jit(solution)/shard_map/ppermute | solution.py:1165
  71.5 18.1 %collective-permute-start.11 = (bf16[4,48,1920]{2,1,0:T(8,128)(2,1)}, bf16[4,48,1920]{2,1,0:T(8,128)(2,1)S(1)}, u32[]{:S(2)}, u32[]{:S(2)}) collective-permute-start(bf16[4,48,1920]{2,1,0:T(8,128)(2,1)} %collective-permute-done.10.rest_1_), channel_id=1, source_target_pairs={{0,16},{8,24},{16,0},{24,8},{1,17},{9,25},{17,1},{25,9},{2,18},{10... | collective-permute-start | bytes 2211848 | tf_op jit(solution)/shard_map/ppermute | solution.py:1165
  83.6 27.4 %copy-start.4 = (bf16[4,192,768]{2,1,0:T(8,128)(2,1)}, bf16[4,192,768]{2,1,0:T(8,128)(2,1)S(1)}, u32[]{:S(2)}) copy-start(bf16[4,192,768]{2,1,0:T(8,128)(2,1)S(1)} %pad_maximum_fusion.b0) | copy-start | bytes 3538948
  83.6 27.4 %collective-permute-start.19 = (bf16[4,192,768]{2,1,0:T(8,128)(2,1)S(1)}, bf16[4,192,768]{2,1,0:T(8,128)(2,1)}, u32[]{:S(2)}, u32[]{:S(2)}) collective-permute-start(bf16[4,192,768]{2,1,0:T(8,128)(2,1)S(1)} %pad_maximum_fusion.b0), channel_id=1, source_target_pairs={{0,1},{1,0},{2,3},{3,2},{4,5},{5,4},{6,7},{7,6},{8,9},{9,8},{10,11... | collective-permute-start | bytes 3538952 | tf_op jit(solution)/shard_map/ppermute | solution.py:1165
  84.1 7.0 %collective-permute-start.14 = (bf16[4,48,1920]{2,1,0:T(8,128)(2,1)}, bf16[4,48,1920]{2,1,0:T(8,128)(2,1)}, u32[]{:S(2)}, u32[]{:S(2)}) collective-permute-start(bf16[4,48,1920]{2,1,0:T(8,128)(2,1)} %collective-permute-done.9.rest_2_), channel_id=1, source_target_pairs={{0,8},{8,0},{16,24},{24,16},{1,9},{9,1},{17,25},{25,17},{2,10},{10... | collective-permute-start | bytes 2211848 | tf_op jit(solution)/shard_map/ppermute | solution.py:1165
  84.1 7.5 %collective-permute-start.12 = (bf16[4,48,1920]{2,1,0:T(8,128)(2,1)S(1)}, bf16[4,48,1920]{2,1,0:T(8,128)(2,1)}, u32[]{:S(2)}, u32[]{:S(2)}) collective-permute-start(bf16[4,48,1920]{2,1,0:T(8,128)(2,1)S(1)} %pad_maximum_fusion.2.rest_0_), channel_id=1, source_target_pairs={{0,8},{8,0},{16,24},{24,16},{1,9},{9,1},{17,25},{25,17},{2,10},{10... | collective-permute-start | bytes 2211848 | tf_op jit(solution)/shard_map/ppermute | solution.py:1165
  84.6 7.0 %collective-permute-start.13 = (bf16[4,48,1920]{2,1,0:T(8,128)(2,1)}, bf16[4,48,1920]{2,1,0:T(8,128)(2,1)}, u32[]{:S(2)}, u32[]{:S(2)}) collective-permute-start(bf16[4,48,1920]{2,1,0:T(8,128)(2,1)} %collective-permute-done.10.rest_1_), channel_id=1, source_target_pairs={{0,8},{8,0},{16,24},{24,16},{1,9},{9,1},{17,25},{25,17},{2,10},{10... | collective-permute-start | bytes 2211848 | tf_op jit(solution)/shard_map/ppermute | solution.py:1165
  89.6 2.4 copy-start.6
  89.6 2.3 collective-permute-start.15
  91.1 20.0 %collective-permute-start.20 = (bf16[4,192,768]{2,1,0:T(8,128)(2,1)S(1)}, bf16[4,192,768]{2,1,0:T(8,128)(2,1)}, u32[]{:S(2)}, u32[]{:S(2)}) collective-permute-start(bf16[4,192,768]{2,1,0:T(8,128)(2,1)S(1)} %pad_maximum_fusion.b0), channel_id=1, source_target_pairs={{0,8},{8,0},{16,24},{24,16},{1,9},{9,1},{17,25},{25,17},{2,10},{10... | collective-permute-start | bytes 3538952 | tf_op jit(solution)/shard_map/ppermute | solution.py:1165
  111.0 3.1 %collective-permute-start.21 = (bf16[4,192,768]{2,1,0:T(8,128)(2,1)}, bf16[4,192,768]{2,1,0:T(8,128)(2,1)S(1)}, u32[]{:S(2)}, u32[]{:S(2)}) collective-permute-start(bf16[4,192,768]{2,1,0:T(8,128)(2,1)} %collective-permute-done.19.b1), channel_id=1, source_target_pairs={{0,8},{8,0},{16,24},{24,16},{1,9},{9,1},{17,25},{25,17},{2,10},{10... | collective-permute-start | bytes 3538952 | tf_op jit(solution)/shard_map/ppermute | solution.py:1165
  147.8 25.1 %collective-permute-start.22 = (bf16[1,2,4,384,384]{4,3,2,1,0:T(8,128)(2,1)}, bf16[1,2,4,384,384]{4,3,2,1,0:T(8,128)(2,1)}, u32[]{:S(2)}, u32[]{:S(2)}) collective-permute-start(bf16[1,2,4,384,384]{4,3,2,1,0:T(8,128)(2,1)} %get-tuple-element.109), channel_id=1, source_target_pairs={{0,8},{8,0},{16,24},{24,16},{1,9},{9,1},{17,25},{25,17},{2,10},{10... | collective-permute-start | bytes 7077896 | tf_op jit(solution)/shard_map/ppermute | solution.py:1165
  148.0 24.9 %copy-start.7 = (bf16[1,2,4,384,384]{4,3,2,1,0:T(8,128)(2,1)S(1)}, bf16[1,2,4,384,384]{4,3,2,1,0:T(8,128)(2,1)}, u32[]{:S(2)}) copy-start(bf16[1,2,4,384,384]{4,3,2,1,0:T(8,128)(2,1)} %get-tuple-element.108) | copy-start | bytes 7077892
  172.4 5.1 %collective-permute-start.23 = (bf16[2,2,4,48,1536]{4,3,2,1,0:T(8,128)(2,1)}, bf16[2,2,4,48,1536]{4,3,2,1,0:T(8,128)(2,1)S(1)}, u32[]{:S(2)}, u32[]{:S(2)}) collective-permute-start(bf16[2,2,4,48,1536]{4,3,2,1,0:T(8,128)(2,1)} %get-tuple-element.112), channel_id=1, source_target_pairs={{0,8},{8,0},{16,24},{24,16},{1,9},{9,1},{17,25},{25,17},{2,10},{10... | collective-permute-start | bytes 7077896 | tf_op jit(solution)/shard_map/ppermute | solution.py:1165
  175.1 2.4 copy-start.8
  176.4 28.2 %collective-permute-start.25 = (bf16[4,384,384]{2,1,0:T(8,128)(2,1)}, bf16[4,384,384]{2,1,0:T(8,128)(2,1)S(1)}, u32[]{:S(2)}, u32[]{:S(2)}) collective-permute-start(bf16[4,384,384]{2,1,0:T(8,128)(2,1)} %get-tuple-element.203), channel_id=1, source_target_pairs={{0,1},{1,0},{2,3},{3,2},{4,5},{5,4},{6,7},{7,6},{8,9},{9,8},{10,11... | collective-permute-start | bytes 3538952 | tf_op jit(solution)/shard_map/ppermute | solution.py:1165
  179.4 28.3 %collective-permute-start.24 = (bf16[2,4,48,1536]{3,2,1,0:T(8,128)(2,1)}, bf16[2,4,48,1536]{3,2,1,0:T(8,128)(2,1)}, u32[]{:S(2)}, u32[]{:S(2)}) collective-permute-start(bf16[2,4,48,1536]{3,2,1,0:T(8,128)(2,1)} %get-tuple-element.205), channel_id=1, source_target_pairs={{0,16},{8,24},{16,0},{24,8},{1,17},{9,25},{17,1},{25,9},{2,18},{10... | collective-permute-start | bytes 3538952 | tf_op jit(solution)/shard_map/ppermute | solution.py:1165
  204.9 4.4 %copy-start.15 = (bf16[2,2,4,48,1152]{4,3,2,1,0:T(8,128)(2,1)S(1)}, bf16[2,2,4,48,1152]{4,3,2,1,0:T(8,128)(2,1)}, u32[]{:S(2)}) copy-start(bf16[2,2,4,48,1152]{4,3,2,1,0:T(8,128)(2,1)} %get-tuple-element.121) | copy-start | bytes 5308420
  209.3 10.1 %collective-permute-start.26 = (bf16[2,2,4,48,1152]{4,3,2,1,0:T(8,128)(2,1)S(1)}, bf16[2,2,4,48,1152]{4,3,2,1,0:T(8,128)(2,1)S(1)}, u32[]{:S(2)}, u32[]{:S(2)}) collective-permute-start(bf16[2,2,4,48,1152]{4,3,2,1,0:T(8,128)(2,1)S(1)} %copy-done.15), channel_id=1, source_target_pairs={{0,8},{8,0},{16,24},{24,16},{1,9},{9,1},{17,25},{25,17},{2,10},{10... | collective-permute-start | bytes 5308424 | tf_op jit(solution)/shard_map/ppermute | solution.py:1165
  210.3 9.1 %copy-start.9 = (bf16[2,2,4,48,1152]{4,3,2,1,0:T(8,128)(2,1)S(1)}, bf16[2,2,4,48,1152]{4,3,2,1,0:T(8,128)(2,1)}, u32[]{:S(2)}) copy-start(bf16[2,2,4,48,1152]{4,3,2,1,0:T(8,128)(2,1)} %get-tuple-element.117) | copy-start | bytes 5308420
  210.3 25.6 %collective-permute-start.32 = (bf16[384,384]{1,0:T(8,128)(2,1)}, bf16[384,384]{1,0:T(8,128)(2,1)}, u32[]{:S(2)}, u32[]{:S(2)}) collective-permute-start(bf16[384,384]{1,0:T(8,128)(2,1)} %get-tuple-element.209), channel_id=1, source_target_pairs={{0,6},{1,7},{2,4},{3,5},{4,2},{5,3},{6,0},{7,1},{8,14},{9,15},{10,... | collective-permute-start | bytes 884744 | tf_op jit(solution)/shard_map/ppermute | solution.py:1165
  212.7 28.1 %collective-permute-start.31 = (bf16[384,384]{1,0:T(8,128)(2,1)}, bf16[384,384]{1,0:T(8,128)(2,1)}, u32[]{:S(2)}, u32[]{:S(2)}) collective-permute-start(bf16[384,384]{1,0:T(8,128)(2,1)} %get-tuple-element.210), channel_id=1, source_target_pairs={{0,4},{1,5},{2,6},{3,7},{4,0},{5,1},{6,2},{7,3},{8,12},{9,13},{10,... | collective-permute-start | bytes 884744 | tf_op jit(solution)/shard_map/ppermute | solution.py:1165
  216.6 24.2 %collective-permute-start.30 = (bf16[384,384]{1,0:T(8,128)(2,1)S(1)}, bf16[384,384]{1,0:T(8,128)(2,1)}, u32[]{:S(2)}, u32[]{:S(2)}) collective-permute-start(bf16[384,384]{1,0:T(8,128)(2,1)S(1)} %get-tuple-element.211), channel_id=1, source_target_pairs={{0,2},{1,3},{2,0},{3,1},{4,6},{5,7},{6,4},{7,5},{8,10},{9,11},{10,... | collective-permute-start | bytes 884744 | tf_op jit(solution)/shard_map/ppermute | solution.py:1165
  218.0 25.4 %collective-permute-start.29 = (bf16[4,48,1536]{2,1,0:T(8,128)(2,1)}, bf16[4,48,1536]{2,1,0:T(8,128)(2,1)S(1)}, u32[]{:S(2)}, u32[]{:S(2)}) collective-permute-start(bf16[4,48,1536]{2,1,0:T(8,128)(2,1)} %get-tuple-element.213), channel_id=1, source_target_pairs={{0,1},{1,0},{2,3},{3,2},{4,5},{5,4},{6,7},{7,6},{8,9},{9,8},{10,11... | collective-permute-start | bytes 1769480 | tf_op jit(solution)/shard_map/ppermute | solution.py:1165
  220.0 23.6 %collective-permute-start.27 = (bf16[2,4,48,1152]{3,2,1,0:T(8,128)(2,1)S(1)}, bf16[2,4,48,1152]{3,2,1,0:T(8,128)(2,1)}, u32[]{:S(2)}, u32[]{:S(2)}) collective-permute-start(bf16[2,4,48,1152]{3,2,1,0:T(8,128)(2,1)S(1)} %get-tuple-element.207), channel_id=1, source_target_pairs={{0,16},{8,24},{16,0},{24,8},{1,17},{9,25},{17,1},{25,9},{2,18},{10... | collective-permute-start | bytes 2654216 | tf_op jit(solution)/shard_map/ppermute | solution.py:1165
  242.1 29.7 %collective-permute-start.38 = (bf16[384,384]{1,0:T(8,128)(2,1)S(1)}, bf16[384,384]{1,0:T(8,128)(2,1)}, u32[]{:S(2)}, u32[]{:S(2)}) collective-permute-start(bf16[384,384]{1,0:T(8,128)(2,1)S(1)} %add_convert_fusion.11), channel_id=1, source_target_pairs={{0,16},{8,24},{16,0},{24,8},{1,17},{9,25},{17,1},{25,9},{2,18},{10... | collective-permute-start | bytes 884744 | tf_op jit(solution)/shard_map/ppermute | solution.py:1165
  243.6 1.5 copy-start.16
  245.0 5.4 %copy-start.11 = (bf16[2,2,4,48,512]{4,3,2,1,0:T(8,128)(2,1)S(1)}, bf16[2,2,4,48,512]{4,3,2,1,0:T(8,128)(2,1)}, u32[]{:S(2)}) copy-start(bf16[2,2,4,48,512]{4,3,2,1,0:T(8,128)(2,1)} %get-tuple-element.129) | copy-start | bytes 2359300
  245.0 4.7 %collective-permute-start.28 = (bf16[2,2,4,48,512]{4,3,2,1,0:T(8,128)(2,1)S(1)}, bf16[2,2,4,48,512]{4,3,2,1,0:T(8,128)(2,1)S(1)}, u32[]{:S(2)}, u32[]{:S(2)}) collective-permute-start(bf16[2,2,4,48,512]{4,3,2,1,0:T(8,128)(2,1)S(1)} %copy-done.16), channel_id=1, source_target_pairs={{0,8},{8,0},{16,24},{24,16},{1,9},{9,1},{17,25},{25,17},{2,10},{10... | collective-permute-start | bytes 2359304 | tf_op jit(solution)/shard_map/ppermute | solution.py:1165
  245.2 15.9 %collective-permute-start.35 = (bf16[48,1536]{1,0:T(8,128)(2,1)S(1)}, bf16[48,1536]{1,0:T(8,128)(2,1)S(1)}, u32[]{:S(2)}, u32[]{:S(2)}) collective-permute-start(bf16[48,1536]{1,0:T(8,128)(2,1)S(1)} %get-tuple-element.227), channel_id=1, source_target_pairs={{0,6},{1,7},{2,4},{3,5},{4,2},{5,3},{6,0},{7,1},{8,14},{9,15},{10,... | collective-permute-start | bytes 442376 | tf_op jit(solution)/shard_map/ppermute | solution.py:1165
  247.6 14.8 %collective-permute-start.34 = (bf16[48,1536]{1,0:T(8,128)(2,1)S(1)}, bf16[48,1536]{1,0:T(8,128)(2,1)S(1)}, u32[]{:S(2)}, u32[]{:S(2)}) collective-permute-start(bf16[48,1536]{1,0:T(8,128)(2,1)S(1)} %get-tuple-element.228), channel_id=1, source_target_pairs={{0,4},{1,5},{2,6},{3,7},{4,0},{5,1},{6,2},{7,3},{8,12},{9,13},{10,... | collective-permute-start | bytes 442376 | tf_op jit(solution)/shard_map/ppermute | solution.py:1165
  247.6 14.8 %collective-permute-start.33 = (bf16[48,1536]{1,0:T(8,128)(2,1)S(1)}, bf16[48,1536]{1,0:T(8,128)(2,1)}, u32[]{:S(2)}, u32[]{:S(2)}) collective-permute-start(bf16[48,1536]{1,0:T(8,128)(2,1)S(1)} %get-tuple-element.229), channel_id=1, source_target_pairs={{0,2},{1,3},{2,0},{3,1},{4,6},{5,7},{6,4},{7,5},{8,10},{9,11},{10,... | collective-permute-start | bytes 442376 | tf_op jit(solution)/shard_map/ppermute | solution.py:1165
  249.7 21.9 %collective-permute-start.37 = (bf16[4,48,1152]{2,1,0:T(8,128)(2,1)S(1)}, bf16[4,48,1152]{2,1,0:T(8,128)(2,1)S(1)}, u32[]{:S(2)}, u32[]{:S(2)}) collective-permute-start(bf16[4,48,1152]{2,1,0:T(8,128)(2,1)S(1)} %get-tuple-element.215), channel_id=1, source_target_pairs={{0,1},{1,0},{2,3},{3,2},{4,5},{5,4},{6,7},{7,6},{8,9},{9,8},{10,11... | collective-permute-start | bytes 1327112 | tf_op jit(solution)/shard_map/ppermute | solution.py:1165
  261.1 10.5 %collective-permute-start.36 = (bf16[2,4,48,512]{3,2,1,0:T(8,128)(2,1)S(1)}, bf16[2,4,48,512]{3,2,1,0:T(8,128)(2,1)S(1)}, u32[]{:S(2)}, u32[]{:S(2)}) collective-permute-start(bf16[2,4,48,512]{3,2,1,0:T(8,128)(2,1)S(1)} %get-tuple-element.217), channel_id=1, source_target_pairs={{0,16},{8,24},{16,0},{24,8},{1,17},{9,25},{17,1},{25,9},{2,18},{10... | collective-permute-start | bytes 1179656 | tf_op jit(solution)/shard_map/ppermute | solution.py:1165
  272.8 5.2 %collective-permute-start.40 = (bf16[48,1536]{1,0:T(8,128)(2,1)S(1)}, bf16[48,1536]{1,0:T(8,128)(2,1)S(1)}, u32[]{:S(2)}, u32[]{:S(2)}) collective-permute-start(bf16[48,1536]{1,0:T(8,128)(2,1)S(1)} %add_convert_fusion.14), channel_id=1, source_target_pairs={{0,16},{8,24},{16,0},{24,8},{1,17},{9,25},{17,1},{25,9},{2,18},{10... | collective-permute-start | bytes 442376 | tf_op jit(solution)/shard_map/ppermute | solution.py:1165
  274.2 5.7 %collective-permute-start.39 = (bf16[4,48,512]{2,1,0:T(8,128)(2,1)S(1)}, bf16[4,48,512]{2,1,0:T(8,128)(2,1)S(1)}, u32[]{:S(2)}, u32[]{:S(2)}) collective-permute-start(bf16[4,48,512]{2,1,0:T(8,128)(2,1)S(1)} %get-tuple-element.233), channel_id=1, source_target_pairs={{0,1},{1,0},{2,3},{3,2},{4,5},{5,4},{6,7},{7,6},{8,9},{9,8},{10,11... | collective-permute-start | bytes 589832 | tf_op jit(solution)/shard_map/ppermute | solution.py:1165
  280.1 8.7 %collective-permute-start.43 = (bf16[48,1664]{1,0:T(8,128)(2,1)S(1)}, bf16[48,1664]{1,0:T(8,128)(2,1)S(1)}, u32[]{:S(2)}, u32[]{:S(2)}) collective-permute-start(bf16[48,1664]{1,0:T(8,128)(2,1)S(1)} %get-tuple-element.219), channel_id=1, source_target_pairs={{0,6},{1,7},{2,4},{3,5},{4,2},{5,3},{6,0},{7,1},{8,14},{9,15},{10,... | collective-permute-start | bytes 479240 | tf_op jit(solution)/shard_map/ppermute | solution.py:1165
  282.8 11.3 %collective-permute-start.42 = (bf16[48,1664]{1,0:T(8,128)(2,1)S(1)}, bf16[48,1664]{1,0:T(8,128)(2,1)S(1)}, u32[]{:S(2)}, u32[]{:S(2)}) collective-permute-start(bf16[48,1664]{1,0:T(8,128)(2,1)S(1)} %get-tuple-element.220), channel_id=1, source_target_pairs={{0,4},{1,5},{2,6},{3,7},{4,0},{5,1},{6,2},{7,3},{8,12},{9,13},{10,... | collective-permute-start | bytes 479240 | tf_op jit(solution)/shard_map/ppermute | solution.py:1165
  282.8 11.3 %collective-permute-start.41 = (bf16[48,1664]{1,0:T(8,128)(2,1)S(1)}, bf16[48,1664]{1,0:T(8,128)(2,1)S(1)}, u32[]{:S(2)}, u32[]{:S(2)}) collective-permute-start(bf16[48,1664]{1,0:T(8,128)(2,1)S(1)} %get-tuple-element.221), channel_id=1, source_target_pairs={{0,2},{1,3},{2,0},{3,1},{4,6},{5,7},{6,4},{7,5},{8,10},{9,11},{10,... | collective-permute-start | bytes 479240 | tf_op jit(solution)/shard_map/ppermute | solution.py:1165
  284.5 10.3 %collective-permute-start.47 = (bf16[48,3072]{1,0:T(8,128)(2,1)S(1)}, bf16[48,3072]{1,0:T(8,128)(2,1)S(1)}, u32[]{:S(2)}, u32[]{:S(2)}) collective-permute-start(bf16[48,3072]{1,0:T(8,128)(2,1)S(1)} %pad_maximum_fusion.3), channel_id=1, source_target_pairs={{0,8},{8,0},{16,24},{24,16},{1,9},{9,1},{17,25},{25,17},{2,10},{10... | collective-permute-start | bytes 884744 | tf_op jit(solution)/shard_map/ppermute | solution.py:1165
  284.5 11.5 %collective-permute-start.48 = (bf16[384,384]{1,0:T(8,128)(2,1)S(1)}, bf16[384,384]{1,0:T(8,128)(2,1)S(1)}, u32[]{:S(2)}, u32[]{:S(2)}) collective-permute-start(bf16[384,384]{1,0:T(8,128)(2,1)S(1)} %add_convert_fusion.10), channel_id=1, source_target_pairs={{0,8},{8,0},{16,24},{24,16},{1,9},{9,1},{17,25},{25,17},{2,10},{10... | collective-permute-start | bytes 884744 | tf_op jit(solution)/shard_map/ppermute | solution.py:1165
  294.2 5.3 %collective-permute-start.44 = (bf16[48,1664]{1,0:T(8,128)(2,1)S(1)}, bf16[48,1664]{1,0:T(8,128)(2,1)S(1)}, u32[]{:S(2)}, u32[]{:S(2)}) collective-permute-start(bf16[48,1664]{1,0:T(8,128)(2,1)S(1)} %add_convert_fusion.13), channel_id=1, source_target_pairs={{0,16},{8,24},{16,0},{24,8},{1,17},{9,25},{17,1},{25,9},{2,18},{10... | collective-permute-start | bytes 479240 | tf_op jit(solution)/shard_map/ppermute | solution.py:1165
  299.7 1.4 collective-permute-start.46
  299.8 3.1 %collective-permute-start.45 = (bf16[48,2304]{1,0:T(8,128)(2,1)S(1)}, bf16[48,2304]{1,0:T(8,128)(2,1)S(1)}, u32[]{:S(2)}, u32[]{:S(2)}) collective-permute-start(bf16[48,2304]{1,0:T(8,128)(2,1)S(1)} %pad_maximum_fusion.4), channel_id=1, source_target_pairs={{0,8},{8,0},{16,24},{24,16},{1,9},{9,1},{17,25},{25,17},{2,10},{10... | collective-permute-start | bytes 663560 | tf_op jit(solution)/shard_map/ppermute | solution.py:1165
  302.9 1.8 copy-start.1
  (2 other events, 1.9 us)
